TPU v7x, 512 devices: a whole 4x8x8 slice. The times are simulated.
512 devices in a mesh: head: 8 (over x, core), wide: 64 (over z, y).
Axes of the slice: x: 4, y: 8, z: 8, core: 2. Of those that a mesh axis runs over, the one named last changes fastest.
Arguments:
- queries: bfloat16 [16384, 2048], P('wide', 'head'), may hold values from -120 to 120
- keys: bfloat16 [16384, 2048], P('wide', 'head'), may hold values from -6 to 6
- values: bfloat16 [16384, 2048], P('wide', 'head'), may hold values from -6 to 6
- out_grad: bfloat16 [16384, 2048], P('wide', 'head'), may hold values from -6 to 6
- qkv_weight: bfloat16 [3, 4096, 2048], P(None, 'wide', 'head'), may hold values from -0.125 to 0.125
- doc_lengths: int32 [32], replicated, may hold values from 1 to 1023, as said below
- image_count: int32 [64], replicated, may hold values 0 or 1
- image_offset: int32 [64], replicated, may hold values from 0 to 192
- slab_owner: int32 [64], replicated, may hold values from 0 to 63, each once
- patch_weight: bfloat16 [256, 4096], P(None, 'head'), may hold values from -0.09375 to 0.09375
- conv_input: bfloat16 [64, 8, 8, 128], P('wide', 'head'), may hold values from -20 to 20
- pre_act: bfloat16 [64, 8, 8, 128], P('wide', 'head'), may hold values from -6 to 6
- kernel_first: float32 [1152, 128], P('wide'), may hold values from -0.1875 to 0.1875
- kernel_second: float32 [1152, 256], P('wide'), may hold values from -0.1875 to 0.1875
- mean_first: float32 [1152, 128], P('wide'), may hold values from -4 to 4
- mean_second: float32 [1152, 256], P('wide'), may hold values from -4 to 4
- square_first: float32 [1152, 128], P('wide'), may hold values from 0.05 to 1
- square_second: float32 [1152, 256], P('wide'), may hold values from 0.05 to 1
Outputs:
- input_grad_t: bfloat16 [4096, 16384], P('head', 'wide')
- new_kernel_first: float32 [1152, 128], P('wide')
- new_kernel_second: float32 [1152, 256], P('wide')
- new_mean_first: float32 [1152, 128], P('wide')
- new_mean_second: float32 [1152, 256], P('wide')
- new_square_first: float32 [1152, 128], P('wide')
- new_square_second: float32 [1152, 256], P('wide')
Inputs may be any that keep to these rules, and one draw needn't show every extreme that they name: `doc_lengths`: the first document is longer than 256 and shorter than 768; the last has 1024 minus the first one's length; the documents between come in consecutive pairs whose lengths add up to 1024.
All inputs are finite; a program needn't handle non-finite values.
Results may differ from a plain program's by a relative error of at most 0.013.
Values may be sent and summed in bfloat16 or wider, within the bound.
No kernel may reach another device: no remote copies, remote signals or barrier semaphores. Data moves between devices by JAX's collectives and lax.ppermute only.
A program may use at most 64 MiB of HBM per device.

v0:
```python
import math

import jax
import jax.numpy as jnp
from jax import lax
from jax.sharding import Mesh
from jax.sharding import PartitionSpec as P

HD = 128
REACH = 4
PROWS = 8
PCOLS = 8
PCH = 256
CMID = 128
CIN = 128
IMGTOK = 64
WIDE = ("wide_0", "wide_1")


neg_big = -1e30
beta_one = 0.9
beta_two = 0.95
adam_eps = 1e-08
learn_rate = 0.02
decay_rate = 0.1
adam_step = 10
norm_eps = 1e-06


def passed_along(block, axis, distance):
    devices = range(lax.axis_size(axis))
    route = [(i - distance, i) for i in devices if i - distance in devices]
    return lax.ppermute(block, axis, route)


def cut_along(value, dim, count):
    before, after = (value.shape[:dim], value.shape[dim + 1 :])
    return jnp.moveaxis(value.reshape(*before, count, -1, *after), dim, 0)


def sent_and_summed(value, axis, dim):
    count = lax.axis_size(axis)
    pieces = lax.all_to_all(cut_along(value, dim, count), axis, 0, 0, tiled=True)
    return jnp.sum(pieces.astype(jnp.float32), axis=0)


def sent_to_all(value, axis):
    copies = jnp.broadcast_to(value, (lax.axis_size(axis), *value.shape))
    return lax.all_to_all(copies, axis, split_axis=0, concat_axis=0, tiled=True)


def taken_together(value, axis):
    everything = sent_to_all(value, axis)
    return jnp.sum(everything.astype(jnp.float32), axis=0)


def laid_out(pieces, dim):
    lengths = list(pieces.shape[1:])
    lengths[dim] *= pieces.shape[0]
    return jnp.moveaxis(pieces, 0, dim).reshape(lengths)


def gathered_copies(value, axis, dim):
    pieces = sent_to_all(value, axis)
    return laid_out(pieces, dim)


def with_halo(cells, sides, width):
    for axis, dim in sides:
        count = lax.axis_size(axis)
        ends = count - 1
        head = lax.slice_in_dim(cells, 0, width, axis=dim)
        tail = lax.slice_in_dim(cells, cells.shape[dim] - width, cells.shape[dim], axis=dim)
        cells = jnp.concatenate(
            [
                lax.ppermute(tail, axis, [(i, (i + 1) % count) for i in range(ends)]),
                cells,
                lax.ppermute(head, axis, [((i + 1) % count, i) for i in range(ends)]),
            ],
            axis=dim,
        )
    return cells


def sent_and_summed_2(value, axis, dim):
    pieces = cut_along(value, dim, lax.axis_size(axis))
    arrived = lax.all_to_all(pieces, axis, split_axis=0, concat_axis=0, tiled=True)
    return arrived.sum(axis=0)


def in_one_piece(arrays, axis, dim, along):
    both = jnp.concatenate(arrays, axis=along)
    whole, at, gathered = (sent_and_summed_2(both, axis, dim), 0, [])
    for a in arrays:
        gathered.append(lax.slice_in_dim(whole, at, at + a.shape[along], axis=along))
        at += a.shape[along]
    return tuple(gathered)


def taken_together_2(value, axis):
    return sent_to_all(value, axis).sum(axis=0)


def together(arrays, axis):
    ends = [0]
    for a in arrays:
        ends.append(ends[-1] + a.size)
    running = taken_together_2(jnp.concatenate([a.ravel() for a in arrays]), axis)
    return tuple((running[b:e].reshape(a.shape) for a, b, e in zip(arrays, ends, ends[1:])))


def one_axis_at_a_time(value, axes):
    for axis in axes:
        value = lax.psum(value, axis)
    return value


def pick_entry(lookup, wanted):
    return jnp.sum(jnp.where(jnp.arange(lookup.shape[0]) == wanted, lookup, 0))


def doc_number(places, doc_lengths):
    ends = jnp.cumsum(doc_lengths)
    return jnp.sum((places[:, None] >= ends[None, :]).astype(jnp.int32), axis=1)


def image_number(block, local, image_count, image_offset):
    present = pick_entry(image_count, block)
    start = pick_entry(image_offset, block)
    inside = (present > 0) & (local >= start) & (local < start + IMGTOK)
    return jnp.where(inside, block, -1)


def allowed_mask(query_places, query_docs, query_images, key_places, key_docs, key_images):
    same_doc = query_docs[:, None] == key_docs[None, :]
    earlier = key_places[None, :] <= query_places[:, None]
    same_image = (query_images[:, None] == key_images[None, :]) & (query_images[:, None] >= 0)
    return same_doc & (earlier | same_image)


def attend_block(query, key_all, value_all, grad_out, allowed):
    scale = 1.0 / math.sqrt(HD)
    rows = query.shape[0]
    count = key_all.shape[0]
    query_h = query.reshape(rows, -1, HD)
    key_h = key_all.reshape(count, -1, HD)
    value_h = value_all.reshape(count, -1, HD)
    grad_h = grad_out.reshape(rows, -1, HD)
    scores = jnp.einsum("qhd,khd->hqk", query_h, key_h, preferred_element_type=jnp.float32) * scale
    scores = jnp.where(allowed[None], scores, neg_big)
    top = jnp.max(scores, axis=-1, keepdims=True)
    expo = jnp.where(allowed[None], jnp.exp(scores - top), 0.0)
    prob = expo / jnp.sum(expo, axis=-1, keepdims=True)
    prob_low = prob.astype(jnp.bfloat16)
    output = jnp.einsum("hqk,khd->qhd", prob_low, value_h, preferred_element_type=jnp.float32)
    delta = jnp.einsum("qhd,qhd->hq", grad_h.astype(jnp.float32), output)
    dprob = jnp.einsum("qhd,khd->hqk", grad_h, value_h, preferred_element_type=jnp.float32)
    dscore = (prob * (dprob - delta[:, :, None])).astype(jnp.bfloat16)
    dquery = jnp.einsum("hqk,khd->qhd", dscore, key_h, preferred_element_type=jnp.float32) * scale
    dkey = jnp.einsum("hqk,qhd->khd", dscore, query_h, preferred_element_type=jnp.float32) * scale
    dvalue = jnp.einsum("hqk,qhd->khd", prob_low, grad_h, preferred_element_type=jnp.float32)
    return (dquery.reshape(rows, -1), dkey.reshape(count, -1), dvalue.reshape(count, -1))


def adam_update(param, mean, square, grad):
    new_mean = beta_one * mean + (1.0 - beta_one) * grad
    new_square = beta_two * square + (1.0 - beta_two) * grad * grad
    fixed_mean = new_mean / (1.0 - beta_one**adam_step)
    fixed_square = new_square / (1.0 - beta_two**adam_step)
    new_param = param - learn_rate * (
        fixed_mean / (jnp.sqrt(fixed_square) + adam_eps) + decay_rate * param
    )
    return (new_param, new_mean, new_square)


def shards(
    queries,
    keys,
    values,
    out_grad,
    qkv_weight,
    doc_lengths,
    image_count,
    image_offset,
    slab_owner,
    patch_weight,
    conv_input,
    pre_act,
    kernel_first,
    kernel_second,
    mean_first,
    mean_second,
    square_first,
    square_second,
):
    tokens_here = queries.shape[0]
    wide_count = lax.axis_size(WIDE)
    head_count = lax.axis_size("head")
    device_index = lax.axis_index(WIDE)
    head_index = lax.axis_index("head")
    local_places = jnp.arange(tokens_here, dtype=jnp.int32)
    query_places = device_index * tokens_here + local_places
    query_docs = doc_number(query_places, doc_lengths)
    query_images = image_number(device_index, local_places, image_count, image_offset)
    own_block = jnp.stack([keys, values])
    blocks = [own_block]
    moving = own_block
    for offset in range(REACH):
        moving = passed_along(moving, WIDE, 1)
        blocks.append(moving)
    masks = []
    for offset in range(REACH + 1):
        source = (device_index - offset) % wide_count
        key_places = source * tokens_here + local_places
        key_docs = doc_number(key_places, doc_lengths)
        key_images = image_number(source, local_places, image_count, image_offset)
        visible = allowed_mask(
            query_places, query_docs, query_images, key_places, key_docs, key_images
        )
        masks.append(visible & (device_index - offset >= 0))
    allowed = jnp.concatenate(masks, axis=1)
    key_all = jnp.concatenate([block[0] for block in blocks], axis=0)
    value_all = jnp.concatenate([block[1] for block in blocks], axis=0)
    dquery, dkey, dvalue = attend_block(queries, key_all, value_all, out_grad, allowed)
    parts = [
        jnp.stack(
            [
                dkey[offset * tokens_here : (offset + 1) * tokens_here],
                dvalue[offset * tokens_here : (offset + 1) * tokens_here],
            ]
        )
        for offset in range(REACH + 1)
    ]
    carried = jnp.zeros_like(parts[0])
    for offset in range(REACH):
        carried = passed_along(carried + parts[REACH - offset], WIDE, -1)
    key_grads = parts[0] + carried
    grads = jnp.stack(
        [
            dquery.astype(jnp.bfloat16),
            key_grads[0].astype(jnp.bfloat16),
            key_grads[1].astype(jnp.bfloat16),
        ]
    )
    partial_value = jnp.einsum(
        "prk,ptk->rt",
        lax.all_gather(qkv_weight, WIDE, axis=1, tiled=True),
        grads,
        preferred_element_type=jnp.float32,
    ).astype(jnp.bfloat16)
    input_grad_t = sent_and_summed(partial_value, "head", 0).astype(jnp.bfloat16)
    patch_part = lax.dot_general(
        input_grad_t, patch_weight, (((0,), (1,)), ((), ())), preferred_element_type=jnp.float32
    )
    patch_grad = (
        taken_together(patch_part.astype(jnp.bfloat16), "head")
        .astype(jnp.float32)
        .astype(jnp.bfloat16)
    )
    slab_rows = PROWS // head_count
    has_image = pick_entry(image_count, device_index)
    offset_here = pick_entry(image_offset, device_index)
    segment = lax.dynamic_slice_in_dim(
        patch_grad, offset_here + head_index * slab_rows * PCOLS, slab_rows * PCOLS, 0
    ) * has_image.astype(jnp.bfloat16)
    chooser = (slab_owner == device_index).astype(jnp.bfloat16)
    arrived = gathered_copies(segment[None], WIDE, 0)
    incoming = jnp.einsum("n,npc->pc", chooser, arrived, preferred_element_type=jnp.float32).astype(
        jnp.bfloat16
    )
    kernel_low = gathered_copies(kernel_second.astype(jnp.bfloat16), WIDE, 0).reshape(CMID, 9, PCH)
    act = jax.nn.silu(pre_act.astype(jnp.float32)).astype(jnp.bfloat16)
    both = jnp.stack([conv_input, act])
    rims = with_halo(both, (("head", 2),), 1)
    rims = jnp.pad(rims, ((0, 0), (0, 0), (0, 0), (1, 1), (0, 0)))
    input_pad = rims[0]
    act_pad = rims[1]
    grad_img = incoming.reshape(1, slab_rows, PCOLS, PCH)
    grad_pad = with_halo(grad_img, (("head", 1),), 1)
    grad_pad = jnp.pad(grad_pad, ((0, 0), (0, 0), (1, 1), (0, 0)))
    second_list = []
    dact = jnp.zeros((slab_rows * PCOLS, CMID), jnp.float32)
    for row_shift in range(3):
        for col_shift in range(3):
            offset = row_shift * 3 + col_shift
            piece = act_pad[
                :, row_shift : row_shift + slab_rows, col_shift : col_shift + PCOLS
            ].reshape(-1, CMID)
            second_list.append(
                lax.dot_general(
                    piece, incoming, (((0,), (0,)), ((), ())), preferred_element_type=jnp.float32
                )
            )
            moved = grad_pad[
                :, 2 - row_shift : 2 - row_shift + slab_rows, 2 - col_shift : 2 - col_shift + PCOLS
            ].reshape(-1, PCH)
            dact = dact + lax.dot_general(
                moved,
                kernel_low[:, offset],
                (((1,), (1,)), ((), ())),
                preferred_element_type=jnp.float32,
            )
    grad_second = jnp.stack(second_list, axis=1).reshape(-1, PCH)
    pre_flat = pre_act.astype(jnp.float32).reshape(-1, CMID)
    sig = jax.nn.sigmoid(pre_flat)
    dpre = (dact * sig * (1.0 + pre_flat * (1.0 - sig))).astype(jnp.bfloat16)
    first_list = []
    for row_shift in range(3):
        for col_shift in range(3):
            piece = input_pad[
                :, row_shift : row_shift + slab_rows, col_shift : col_shift + PCOLS
            ].reshape(-1, CIN)
            first_list.append(
                lax.dot_general(
                    piece, dpre, (((0,), (0,)), ((), ())), preferred_element_type=jnp.float32
                )
            )
    grad_first = jnp.stack(first_list, axis=1).reshape(-1, CMID)
    owned_first, owned_second = in_one_piece((grad_first, grad_second), WIDE, 0, 1)
    owned_first, owned_second = together((owned_first, owned_second), "head")
    squares = one_axis_at_a_time(
        jnp.sum(owned_first * owned_first) + jnp.sum(owned_second * owned_second), WIDE
    )
    limit = 0.5 * math.sqrt(9 * CIN * CMID + 9 * CMID * PCH)
    factor = jnp.minimum(1.0, limit / (jnp.sqrt(squares) + norm_eps))
    kernel_one, mean_one, square_one = adam_update(
        kernel_first, mean_first, square_first, owned_first * factor
    )
    kernel_two, mean_two, square_two = adam_update(
        kernel_second, mean_second, square_second, owned_second * factor
    )
    return (input_grad_t, kernel_one, kernel_two, mean_one, mean_two, square_one, square_two)


def solution(mesh):
    split = Mesh(mesh.devices.reshape(mesh.shape["head"], 8, 8), ("head", "wide_0", "wide_1"))
    placed = (
        P(WIDE, "head"),
        P(WIDE, "head"),
        P(WIDE, "head"),
        P(WIDE, "head"),
        P(None, WIDE, "head"),
        P(),
        P(),
        P(),
        P(),
        P(None, "head"),
        P(WIDE, "head", None, None),
        P(WIDE, "head", None, None),
        P(WIDE, None),
        P(WIDE, None),
        P(WIDE, None),
        P(WIDE, None),
        P(WIDE, None),
        P(WIDE, None),
    )
    return jax.shard_map(
        shards,
        mesh=split,
        in_specs=placed,
        out_specs=(
            P("head", WIDE),
            P(WIDE, None),
            P(WIDE, None),
            P(WIDE, None),
            P(WIDE, None),
            P(WIDE, None),
            P(WIDE, None),
        ),
        check_vma=False,
    )
```

profile of v0, /device:TPU:8, one launch (start us, length us, event | category | flops | bytes accessed | tf_op | source)
XLA Modules:
  0.0 415.8 jit_solution(10553402261637280647)
XLA Ops:
  10.1 3.5 collective-permute-start
  13.7 1.6 fusion.99
  28.6 3.5 collective-permute-start.1
  32.5 6.4 %collective-permute-done.1 = bf16[2,256,256]{1,2,0:T(8,128)(2,1)S(1)} collective-permute-done((bf16[2,256,256]{1,2,0:T(8,128)(2,1)S(1)}, bf16[2,256,256]{1,2,0:T(8,128)(2,1)S(1)}, u32[]{:S(2)}, u32[]{:S(2)}) %collective-permute-start.1) | collective-permute-done | bytes 262176 | tf_op jit(solution)/shard_map/ppermute | solution.py:33
  38.9 3.9 collective-permute-start.2
  43.2 5.3 %collective-permute-done.2 = bf16[2,256,256]{1,2,0:T(8,128)(2,1)S(1)} collective-permute-done((bf16[2,256,256]{1,2,0:T(8,128)(2,1)S(1)}, bf16[2,256,256]{1,2,0:T(8,128)(2,1)S(1)}, u32[]{:S(2)}, u32[]{:S(2)}) %collective-permute-start.2) | collective-permute-done | bytes 262176 | tf_op jit(solution)/shard_map/ppermute | solution.py:33
  48.5 4.2 collective-permute-start.3
  53.0 4.2 %collective-permute-done.3 = bf16[2,256,256]{1,2,0:T(8,128)(2,1)S(1)} collective-permute-done((bf16[2,256,256]{1,2,0:T(8,128)(2,1)S(1)}, bf16[2,256,256]{1,2,0:T(8,128)(2,1)S(1)}, u32[]{:S(2)}, u32[]{:S(2)}) %collective-permute-start.3) | collective-permute-done | bytes 262176 | tf_op jit(solution)/shard_map/ppermute | solution.py:33
  57.5 2.8 fusion.118
  60.4 2.1 convolution_bitcast_fusion.2
  63.1 2.2 fusion.9
  66.8 2.3 convolution_bitcast_fusion.1
  70.0 1.8 copy.191
  71.9 1.9 pad_maximum_fusion.1
  73.8 1.9 collective-permute-start.4
  76.5 1.1 copy.193
  77.6 22.4 %collective-permute-done.4 = f32[2,256,256]{2,1,0:T(8,128)} collective-permute-done((f32[2,256,256]{2,1,0:T(8,128)}, f32[2,256,256]{2,1,0:T(8,128)}, u32[]{:S(2)}, u32[]{:S(2)}) %collective-permute-start.4) | collective-permute-done | bytes 524320 | tf_op jit(solution)/shard_map/ppermute | solution.py:33
  100.0 2.0 maximum_add_fusion.1
  102.0 1.9 collective-permute-start.5
  104.2 20.3 %collective-permute-done.5 = f32[2,256,256]{2,1,0:T(8,128)} collective-permute-done((f32[2,256,256]{2,1,0:T(8,128)}, f32[2,256,256]{2,1,0:T(8,128)}, u32[]{:S(2)}, u32[]{:S(2)}) %collective-permute-start.5) | collective-permute-done | bytes 524320 | tf_op jit(solution)/shard_map/ppermute | solution.py:33
  124.5 1.9 maximum_add_fusion.2
  126.4 2.1 collective-permute-start.6
  128.8 12.2 %collective-permute-done.6 = f32[2,256,256]{2,1,0:T(8,128)} collective-permute-done((f32[2,256,256]{2,1,0:T(8,128)}, f32[2,256,256]{2,1,0:T(8,128)}, u32[]{:S(2)}, u32[]{:S(2)}) %collective-permute-start.6) | collective-permute-done | bytes 524320 | tf_op jit(solution)/shard_map/ppermute | solution.py:33
  141.0 1.9 maximum_add_fusion.3
  142.9 1.9 collective-permute-start.7
  145.6 11.8 %collective-permute-done.7 = f32[2,256,256]{2,1,0:T(8,128)S(1)} collective-permute-done((f32[2,256,256]{2,1,0:T(8,128)}, f32[2,256,256]{2,1,0:T(8,128)S(1)}, u32[]{:S(2)}, u32[]{:S(2)}) %collective-permute-start.7) | collective-permute-done | bytes 524320 | tf_op jit(solution)/shard_map/ppermute | solution.py:33
  157.5 4.6 %fusion.1 = bf16[256,4096]{1,0:T(8,128)(2,1)S(1)} fusion(bf16[3,4096,256]{2,1,0:T(8,128)(2,1)} %all-gather.2.cloned.1.call-done, bf16[2,256,256]{2,1,0:T(8,128)(2,1)S(1)} %fusion.35, bf16[1,256,256]{2,1,0:T(8,128)(2,1)S(1)} %copy.198), kind=kOutput, calls=%fused_computation.2 | convolution fusion | flops 1611857920 | bytes 8781824 | tf_op jit(solution)/shard_map/prk,ptk->rt/dot_general | solution.py:245
  162.3 31.2 %all_to_all.31 = bf16[8,512,256]{1,2,0:T(8,128)(2,1)S(1)} all-to-all(bf16[8,512,256]{1,2,0:T(8,128)(2,1)S(1)} %bitcast.318), channel_id=1, replica_groups=mesh['head'=8,'wide_0'=8,'wide_1'=8] {'head'}, dimensions={0} | all-to-all | bytes 4194304 | tf_op jit(solution)/shard_map/all_to_all | solution.py:43
  194.2 1.1 broadcast_in_dim.139
  195.3 3.7 all-to-all-start.1
  199.0 15.8 %all-to-all-done.1 = bf16[8,256,256]{2,1,0:T(8,128)(2,1)S(1)} async-done(((bf16[8,256,256]{2,1,0:T(8,128)(2,1)}), bf16[8,256,256]{2,1,0:T(8,128)(2,1)S(1)}, u32[]{:S(2)}, u32[]{:S(2)}) %all-to-all-start.1) | async-done | bytes 1048608 | tf_op jit(solution)/shard_map/all_to_all | solution.py:49
  215.8 16.2 %all-to-all-start.3 = ((bf16[64,18,256]{2,1,0:T(8,128)(2,1)}), bf16[64,18,256]{2,1,0:T(8,128)(2,1)S(1)}, u32[]{:S(2)}, u32[]{:S(2)}) async-start(bf16[64,18,256]{2,1,0:T(8,128)(2,1)} %broadcast_in_dim.141), calls=%async_computation.3 | async-start | bytes 1572864 | tf_op jit(solution)/shard_map/all_to_all | solution.py:49
  232.1 1.3 collective-permute-start.8
  233.4 1.3 collective-permute-start.9
  235.9 1.3 collective-permute-done.9
  237.4 18.3 %all-to-all-done.3 = bf16[64,18,256]{2,1,0:T(8,128)(2,1)S(1)} async-done(((bf16[64,18,256]{2,1,0:T(8,128)(2,1)}), bf16[64,18,256]{2,1,0:T(8,128)(2,1)S(1)}, u32[]{:S(2)}, u32[]{:S(2)}) %all-to-all-start.3) | async-done | bytes 589856 | tf_op jit(solution)/shard_map/all_to_all | solution.py:49
  256.5 6.5 %all-to-all-start.2 = ((bf16[64,1,8,256]{3,2,1,0:T(8,128)(2,1)}), bf16[64,1,8,256]{3,2,1,0:T(8,128)(2,1)S(1)}, u32[]{:S(2)}, u32[]{:S(2)}) async-start(bf16[64,1,8,256]{3,2,1,0:T(8,128)(2,1)} %broadcast_in_dim.140), calls=%async_computation.2 | async-start | bytes 524288 | tf_op jit(solution)/shard_map/all_to_all | solution.py:49
  263.7 1.6 fusion.113
  265.3 11.0 %all-to-all-done.2 = bf16[64,1,8,256]{3,2,1,0:T(8,128)(2,1)S(1)} async-done(((bf16[64,1,8,256]{3,2,1,0:T(8,128)(2,1)}), bf16[64,1,8,256]{3,2,1,0:T(8,128)(2,1)S(1)}, u32[]{:S(2)}, u32[]{:S(2)}) %all-to-all-start.2) | async-done | bytes 262176 | tf_op jit(solution)/shard_map/all_to_all | solution.py:49
  277.0 1.9 collective-permute-start.10
  278.9 1.3 collective-permute-start.11
  282.9 1.3 concatenate.64
  287.7 1.1 fusion.33
  292.8 1.3 pad_maximum_fusion
  294.1 65.6 %all_to_all.32 = f32[64,18,384]{2,1,0:T(8,128)S(1)} all-to-all(f32[64,18,384]{2,1,0:T(8,128)S(1)} %pad_maximum_fusion), channel_id=1, replica_groups=mesh['head'=8,'wide_0'=8,'wide_1'=8] {'wide_0','wide_1'}, dimensions={0} | all-to-all | bytes 3538944 | tf_op jit(solution)/shard_map/all_to_all | solution.py:87
  360.1 10.2 %all_to_all.33 = f32[8,1,6912]{2,1,0:T(1,128)S(1)} all-to-all(f32[8,1,6912]{2,1,0:T(1,128)S(1)} %broadcast_in_dim.142), channel_id=1, replica_groups=mesh['head'=8,'wide_0'=8,'wide_1'=8] {'head'}, dimensions={0} | all-to-all | bytes 442368 | tf_op jit(solution)/shard_map/all_to_all | solution.py:49
  372.9 15.2 %psum.14 = f32[]{:T(128)} all-reduce(f32[]{:T(128)S(6)} %add.258), channel_id=1, replica_groups=mesh['head'=8,'wide_0'=8,'wide_1'=8] {'wide_0'}, use_global_device_ids=true, to_apply=%region_27.28 | all-reduce | flops 1 | bytes 8 | tf_op jit(solution)/shard_map/psum | solution.py:114
  389.0 17.9 %psum.15 = f32[]{:T(128)} all-reduce(f32[]{:T(128)} %psum.14), channel_id=1, replica_groups=mesh['head'=8,'wide_0'=8,'wide_1'=8] {'wide_1'}, use_global_device_ids=true, to_apply=%region_28.29 | all-reduce | flops 1 | bytes 8 | tf_op jit(solution)/shard_map/psum | solution.py:114
  (168 shorter events, 33.1 us)
Async XLA Ops:
  7.2 186.8 %copy-start = (bf16[256,512]{1,0:T(8,128)(2,1)S(1)}, bf16[256,512]{1,0:T(8,128)(2,1)}, u32[]{:S(2)}) copy-start(bf16[256,512]{1,0:T(8,128)(2,1)} %param.27) | copy-start | bytes 786436
  7.2 10.5 %copy-start.17 = (s32[32]{0:T(128)S(1)}, s32[32]{0:T(128)}, u32[]{:S(2)}) copy-start(s32[32]{0:T(128)} %param.23) | copy-start | bytes 388
  7.2 150.3 %all-gather.2.cloned.1.call-start = ((), (), s32[]{:S(2)}) async-start(), calls=%async_computation.6 | async-start | bytes 6389760 | tf_op jit(solution)/shard_map/all_gather | solution.py:247
  7.9 20.2 %copy-start.4 = (bf16[256,256]{1,0:T(8,128)(2,1)S(1)}, bf16[256,256]{1,0:T(8,128)(2,1)}, u32[]{:S(2)}) copy-start(bf16[256,256]{1,0:T(8,128)(2,1)} %param.18) | copy-start | bytes 393220
  9.0 19.3 %copy-start.5 = (bf16[256,256]{1,0:T(8,128)(2,1)S(1)}, bf16[256,256]{1,0:T(8,128)(2,1)}, u32[]{:S(2)}) copy-start(bf16[256,256]{1,0:T(8,128)(2,1)} %param.21) | copy-start | bytes 393220
  10.1 18.6 %collective-permute-start = (bf16[2,256,256]{1,2,0:T(8,128)(2,1)S(1)}, bf16[2,256,256]{1,2,0:T(8,128)(2,1)S(1)}, u32[]{:S(2)}, u32[]{:S(2)}) collective-permute-start(bf16[2,256,256]{1,2,0:T(8,128)(2,1)S(1)} %pad_maximum_fusion.2), channel_id=1, source_target_pairs={{0,1},{1,2},{2,3},{3,4},{4,5},{5,6},{6,7},{7,8},{8,9},{9,10},{10,1... | collective-permute-start | bytes 786440 | tf_op jit(solution)/shard_map/ppermute | solution.py:33
  28.6 10.3 %collective-permute-start.1 = (bf16[2,256,256]{1,2,0:T(8,128)(2,1)S(1)}, bf16[2,256,256]{1,2,0:T(8,128)(2,1)S(1)}, u32[]{:S(2)}, u32[]{:S(2)}) collective-permute-start(bf16[2,256,256]{1,2,0:T(8,128)(2,1)S(1)} %collective-permute-done), channel_id=1, source_target_pairs={{0,1},{1,2},{2,3},{3,4},{4,5},{5,6},{6,7},{7,8},{8,9},{9,10},{10,1... | collective-permute-start | bytes 786440 | tf_op jit(solution)/shard_map/ppermute | solution.py:33
  38.9 9.6 %collective-permute-start.2 = (bf16[2,256,256]{1,2,0:T(8,128)(2,1)S(1)}, bf16[2,256,256]{1,2,0:T(8,128)(2,1)S(1)}, u32[]{:S(2)}, u32[]{:S(2)}) collective-permute-start(bf16[2,256,256]{1,2,0:T(8,128)(2,1)S(1)} %collective-permute-done.1), channel_id=1, source_target_pairs={{0,1},{1,2},{2,3},{3,4},{4,5},{5,6},{6,7},{7,8},{8,9},{9,10},{10,1... | collective-permute-start | bytes 786440 | tf_op jit(solution)/shard_map/ppermute | solution.py:33
  48.5 8.7 %collective-permute-start.3 = (bf16[2,256,256]{1,2,0:T(8,128)(2,1)S(1)}, bf16[2,256,256]{1,2,0:T(8,128)(2,1)S(1)}, u32[]{:S(2)}, u32[]{:S(2)}) collective-permute-start(bf16[2,256,256]{1,2,0:T(8,128)(2,1)S(1)} %collective-permute-done.2), channel_id=1, source_target_pairs={{0,1},{1,2},{2,3},{3,4},{4,5},{5,6},{6,7},{7,8},{8,9},{9,10},{10,1... | collective-permute-start | bytes 786440 | tf_op jit(solution)/shard_map/ppermute | solution.py:33
  57.5 2.9 copy-start.2
  73.8 26.3 %collective-permute-start.4 = (f32[2,256,256]{2,1,0:T(8,128)}, f32[2,256,256]{2,1,0:T(8,128)}, u32[]{:S(2)}, u32[]{:S(2)}) collective-permute-start(f32[2,256,256]{2,1,0:T(8,128)} %pad_maximum_fusion.1), channel_id=1, source_target_pairs={{1,0},{2,1},{3,2},{4,3},{5,4},{6,5},{7,6},{8,7},{9,8},{10,9},{11,1... | collective-permute-start | bytes 1572872 | tf_op jit(solution)/shard_map/ppermute | solution.py:33
  102.0 22.5 %collective-permute-start.5 = (f32[2,256,256]{2,1,0:T(8,128)}, f32[2,256,256]{2,1,0:T(8,128)}, u32[]{:S(2)}, u32[]{:S(2)}) collective-permute-start(f32[2,256,256]{2,1,0:T(8,128)} %maximum_add_fusion.1), channel_id=1, source_target_pairs={{1,0},{2,1},{3,2},{4,3},{5,4},{6,5},{7,6},{8,7},{9,8},{10,9},{11,1... | collective-permute-start | bytes 1572872 | tf_op jit(solution)/shard_map/ppermute | solution.py:33
  126.4 14.6 %collective-permute-start.6 = (f32[2,256,256]{2,1,0:T(8,128)}, f32[2,256,256]{2,1,0:T(8,128)}, u32[]{:S(2)}, u32[]{:S(2)}) collective-permute-start(f32[2,256,256]{2,1,0:T(8,128)} %maximum_add_fusion.2), channel_id=1, source_target_pairs={{1,0},{2,1},{3,2},{4,3},{5,4},{6,5},{7,6},{8,7},{9,8},{10,9},{11,1... | collective-permute-start | bytes 1572872 | tf_op jit(solution)/shard_map/ppermute | solution.py:33
  128.8 16.3 %copy-start.3 = (bf16[1280,2,128]{2,0,1:T(8,128)(2,1)S(1)}, bf16[1280,2,128]{2,0,1:T(8,128)(2,1)}, u32[]{:S(2)}) copy-start(bf16[1280,2,128]{2,0,1:T(8,128)(2,1)} %copy-done.2) | copy-start | bytes 1966084
  142.9 14.5 %collective-permute-start.7 = (f32[2,256,256]{2,1,0:T(8,128)}, f32[2,256,256]{2,1,0:T(8,128)S(1)}, u32[]{:S(2)}, u32[]{:S(2)}) collective-permute-start(f32[2,256,256]{2,1,0:T(8,128)} %maximum_add_fusion.3), channel_id=1, source_target_pairs={{1,0},{2,1},{3,2},{4,3},{5,4},{6,5},{7,6},{8,7},{9,8},{10,9},{11,1... | collective-permute-start | bytes 1572872 | tf_op jit(solution)/shard_map/ppermute | solution.py:33
  195.3 3.7 copy-start.6
  195.3 19.6 %all-to-all-start.1 = ((bf16[8,256,256]{2,1,0:T(8,128)(2,1)}), bf16[8,256,256]{2,1,0:T(8,128)(2,1)S(1)}, u32[]{:S(2)}, u32[]{:S(2)}) async-start(bf16[8,256,256]{2,1,0:T(8,128)(2,1)} %broadcast_in_dim.139), calls=%async_computation.1 | async-start | bytes 2097152 | tf_op jit(solution)/shard_map/all_to_all | solution.py:49
  199.0 33.0 %copy-start.15 = (bf16[1,1,8,128]{3,2,1,0:T(8,128)(2,1)S(1)}, bf16[1,1,8,128]{3,2,1,0:T(8,128)(2,1)}, u32[]{:S(2)}) copy-start(bf16[1,1,8,128]{3,2,1,0:T(8,128)(2,1)} %param.29) | copy-start | bytes 6148
  199.0 33.0 %copy-start.14 = (bf16[1,1,8,128]{3,2,1,0:T(8,128)(2,1)S(1)}, bf16[1,1,8,128]{3,2,1,0:T(8,128)(2,1)}, u32[]{:S(2)}) copy-start(bf16[1,1,8,128]{3,2,1,0:T(8,128)(2,1)} %param.28) | copy-start | bytes 6148
  215.8 40.0 %all-to-all-start.3 = ((bf16[64,18,256]{2,1,0:T(8,128)(2,1)}), bf16[64,18,256]{2,1,0:T(8,128)(2,1)S(1)}, u32[]{:S(2)}, u32[]{:S(2)}) async-start(bf16[64,18,256]{2,1,0:T(8,128)(2,1)} %broadcast_in_dim.141), calls=%async_computation.3 | async-start | bytes 1572864 | tf_op jit(solution)/shard_map/all_to_all | solution.py:49
  232.1 3.8 collective-permute-start.8
  233.4 3.9 collective-permute-start.9
  256.5 19.8 %all-to-all-start.2 = ((bf16[64,1,8,256]{3,2,1,0:T(8,128)(2,1)}), bf16[64,1,8,256]{3,2,1,0:T(8,128)(2,1)S(1)}, u32[]{:S(2)}, u32[]{:S(2)}) async-start(bf16[64,1,8,256]{3,2,1,0:T(8,128)(2,1)} %broadcast_in_dim.140), calls=%async_computation.2 | async-start | bytes 524288 | tf_op jit(solution)/shard_map/all_to_all | solution.py:49
  263.7 12.5 %copy-start.16 = (s32[64]{0:T(128)S(1)}, s32[64]{0:T(128)}, u32[]{:S(2)}) copy-start(s32[64]{0:T(128)} %param.26) | copy-start | bytes 772
  277.0 7.2 %collective-permute-start.10 = (bf16[1,1,8,256]{3,2,1,0:T(8,128)(2,1)}, bf16[1,1,8,256]{3,2,1,0:T(8,128)(2,1)}, u32[]{:S(2)}, u32[]{:S(2)}) collective-permute-start(bf16[1,1,8,256]{3,2,1,0:T(8,128)(2,1)} %bitcast.317), channel_id=1, source_target_pairs={{0,64},{64,128},{128,192},{192,256},{256,320},{320,384},{384,448},... | collective-permute-start | bytes 12296 | tf_op jit(solution)/shard_map/ppermute | solution.py:76
  278.9 5.3 %collective-permute-start.11 = (bf16[1,1,8,256]{3,2,1,0:T(8,128)(2,1)}, bf16[1,1,8,256]{3,2,1,0:T(8,128)(2,1)}, u32[]{:S(2)}, u32[]{:S(2)}) collective-permute-start(bf16[1,1,8,256]{3,2,1,0:T(8,128)(2,1)} %bitcast.317), channel_id=1, source_target_pairs={{64,0},{128,64},{192,128},{256,192},{320,256},{384,320},{448,384},... | collective-permute-start | bytes 12296 | tf_op jit(solution)/shard_map/ppermute | solution.py:78
  282.9 5.9 %copy-start.8 = (bf16[1,3,10,128]{3,2,1,0:T(8,128)(2,1)S(1)}, bf16[1,3,10,128]{3,2,1,0:T(8,128)(2,1)}, u32[]{:S(2)}) copy-start(bf16[1,3,10,128]{3,2,1,0:T(8,128)(2,1)} %get-tuple-element.81) | copy-start | bytes 23044
  291.1 1.7 copy-start.1
  359.8 47.8 %copy-start.7 = (f32[18,256]{1,0:T(8,128)S(1)}, f32[18,256]{1,0:T(8,128)}, u32[]{:S(2)}) copy-start(f32[18,256]{1,0:T(8,128)} %param.31) | copy-start | bytes 55300
  359.9 47.8 %copy-start.9 = (f32[18,256]{1,0:T(8,128)S(1)}, f32[18,256]{1,0:T(8,128)}, u32[]{:S(2)}) copy-start(f32[18,256]{1,0:T(8,128)} %param.33) | copy-start | bytes 55300
  359.9 47.8 %copy-start.10 = (f32[18,256]{1,0:T(8,128)S(1)}, f32[18,256]{1,0:T(8,128)}, u32[]{:S(2)}) copy-start(f32[18,256]{1,0:T(8,128)} %param.35) | copy-start | bytes 55300
  359.9 48.4 %copy-start.11 = (f32[18,128]{1,0:T(8,128)S(1)}, f32[18,128]{1,0:T(8,128)}, u32[]{:S(2)}) copy-start(f32[18,128]{1,0:T(8,128)} %param.30) | copy-start | bytes 27652
  359.9 48.4 %copy-start.12 = (f32[18,128]{1,0:T(8,128)S(1)}, f32[18,128]{1,0:T(8,128)}, u32[]{:S(2)}) copy-start(f32[18,128]{1,0:T(8,128)} %param.32) | copy-start | bytes 27652
  359.9 48.4 %copy-start.13 = (f32[18,128]{1,0:T(8,128)S(1)}, f32[18,128]{1,0:T(8,128)}, u32[]{:S(2)}) copy-start(f32[18,128]{1,0:T(8,128)} %param.34) | copy-start | bytes 27652
Sparse Core Ops, SparseCore 0:
  11.0 112.3 all-gather.1
where the time goes:
time: 417 us; the launch traced here: 416 us
  blocking collectives  140 us (34%)
  waiting for transfers between devices  130 us (31%)
  starting transfers between devices  55 us (13%)
  between operations  25.9 us (6%)
  matrix products  23.2 us (6%)
  local copies, waits for them, and re-layouts  21.6 us (5%)
  other arithmetic  20.2 us (5%)
    ppermute x8, waiting for transfers between devices, passed_along(): return lax.ppermute(block, axis, route)  82.7 us
    all_to_all x1, blocking collectives, sent_and_summed_2(): lax.all_to_all(pieces, axis, split_axis=0, concat_axis=0, tiled=True)  65.6 us
    all_to_all x3, waiting for transfers between devices, sent_to_all(): return lax.all_to_all(copies, axis, split_axis=0, concat_axis=0, tiled=True)  45.1 us
    psum x2, blocking collectives, one_axis_at_a_time(): value = lax.psum(value, axis)  33.1 us
    all_to_all x1, blocking collectives, sent_and_summed(): lax.all_to_all(cut_along(value, dim, count), axis, 0, 0, tiled=True)  31.2 us
    all_to_all x3, starting transfers between devices, sent_to_all(): return lax.all_to_all(copies, axis, split_axis=0, concat_axis=0, tiled=True)  26.4 us
    ppermute x8, starting transfers between devices, passed_along(): return lax.ppermute(block, axis, route)  22.8 us
    all_to_all x1, blocking collectives, sent_to_all(): return lax.all_to_all(copies, axis, split_axis=0, concat_axis=0, tiled=True)  10.2 us
  transfers between devices with their start and end apart: 16, of which 11 were waited for; matrix products, arithmetic and copies ran while one was open for 10% of the time, Pallas kernels for 0%

commit v1 on v0

v1 whole, which is shorter than its diff:
```python
import math

import jax
import jax.numpy as jnp
from jax import lax
from jax.experimental import pallas as pl
from jax.experimental.pallas import tpu as pltpu
from jax.sharding import Mesh
from jax.sharding import PartitionSpec as P

HD = 128
REACH = 4
PROWS = 8
PCOLS = 8
PCH = 256
CMID = 128
CIN = 128
IMGTOK = 64
TOK = 256
WIDE = ("z", "yh", "yl")
LANES = 896

neg_big = -1e30
beta_one = 0.9
beta_two = 0.95
adam_eps = 1e-08
learn_rate = 0.02
decay_rate = 0.1
adam_step = 10
norm_eps = 1e-06
scale = 1.0 / math.sqrt(HD)

f32 = jnp.float32
bf16 = jnp.bfloat16


def nt(a, b):
    return lax.dot_general(a, b, (((1,), (1,)), ((), ())), preferred_element_type=f32)


def nn(a, b):
    return lax.dot_general(a, b, (((1,), (0,)), ((), ())), preferred_element_type=f32)


def tn(a, b):
    return lax.dot_general(a, b, (((0,), (0,)), ((), ())), preferred_element_type=f32)


def head_cols(h):
    return slice(h * HD, (h + 1) * HD)


def masked_scores(key_h, query_h, low, high, shift):
    scores = nt(key_h, query_h) * scale
    place = lax.broadcasted_iota(jnp.int32, scores.shape, 0) - shift
    seen = place >= low
    if high is not None:
        seen = seen & (place <= high)
    return jnp.where(seen, scores, neg_big)


def stats_kernel(meta, q, g, k0, v0, b1, b2, b3, b4, stats, scores_ref):
    near = [b1, b2, b3, b4]
    low = meta[1:2, :]
    high = meta[0:1, :]
    rows = []
    for h in range(2):
        cols = head_cols(h)
        query_h = q[:, cols]
        grad_h = g[:, cols]
        top = None
        for d in range(REACH + 1):
            key_h = k0[:, cols] if d == 0 else near[d - 1][0, :, cols]
            s = masked_scores(key_h, query_h, low, high if d == 0 else None, d * TOK)
            scores_ref[d] = s
            best = jnp.max(s, axis=0, keepdims=True)
            top = best if top is None else jnp.maximum(top, best)
        total = jnp.zeros((1, TOK), f32)
        for d in range(REACH + 1):
            e = jnp.exp(scores_ref[d] - top)
            scores_ref[d] = e
            total = total + jnp.sum(e, axis=0, keepdims=True)
        inverse = 1.0 / total
        delta = jnp.zeros((1, TOK), f32)
        for d in range(REACH + 1):
            value_h = v0[:, cols] if d == 0 else near[d - 1][1, :, cols]
            low_p = (scores_ref[d] * inverse).astype(bf16).astype(f32)
            delta = delta + jnp.sum(low_p * nt(value_h, grad_h), axis=0, keepdims=True)
        rows.append((top, inverse, delta))
    for h in range(2):
        for n in range(3):
            stats[3 * h + n : 3 * h + n + 1, :] = rows[h][n]
    stats[6:8, :] = jnp.zeros((2, TOK), f32)


def own_kernel(meta, stats, q, g, k0, v0, b1, b2, b3, b4, dq, dk, dv):
    near = [b1, b2, b3, b4]
    low = meta[1:2, :]
    high = meta[0:1, :]
    for h in range(2):
        cols = head_cols(h)
        query_h = q[:, cols]
        grad_h = g[:, cols]
        top = stats[3 * h : 3 * h + 1, :]
        inverse = stats[3 * h + 1 : 3 * h + 2, :]
        delta = stats[3 * h + 2 : 3 * h + 3, :]
        acc = jnp.zeros((TOK, HD), f32)
        for d in range(REACH + 1):
            key_h = k0[:, cols] if d == 0 else near[d - 1][0, :, cols]
            value_h = v0[:, cols] if d == 0 else near[d - 1][1, :, cols]
            s = masked_scores(key_h, query_h, low, high if d == 0 else None, d * TOK)
            prob = jnp.exp(s - top) * inverse
            ds = (prob * (nt(value_h, grad_h) - delta)).astype(bf16)
            acc = acc + tn(ds, key_h)
            if d == 0:
                dk[:, cols] = nn(ds, query_h)
                dv[:, cols] = nn(prob.astype(bf16), grad_h)
        dq[:, cols] = (acc * scale).astype(bf16)


def later_kernel(
    start, meta, k0, v0, a1, a2, a3, a4, s1, s2, s3, s4, dq, dk, dv, out, image
):
    later = [a1, a2, a3, a4]
    stats = [s1, s2, s3, s4]
    for h in range(2):
        cols = head_cols(h)
        key_h = k0[:, cols]
        value_h = v0[:, cols]
        dkey = dk[:, cols]
        dvalue = dv[:, cols]
        for d in range(1, REACH + 1):
            query_h = later[d - 1][0, :, cols]
            grad_h = later[d - 1][1, :, cols]
            row = stats[d - 1]
            low = meta[1 + d : 2 + d, :]
            s = masked_scores(key_h, query_h, low, None, 0)
            prob = jnp.exp(s - row[3 * h : 3 * h + 1, :]) * row[3 * h + 1 : 3 * h + 2, :]
            ds = (prob * (nt(value_h, grad_h) - row[3 * h + 2 : 3 * h + 3, :])).astype(bf16)
            dkey = dkey + nn(ds, query_h)
            dvalue = dvalue + nn(prob.astype(bf16), grad_h)
        out[1, :, cols] = (dkey * scale).astype(bf16)
        out[2, :, cols] = dvalue.astype(bf16)
    out[0] = dq[...]
    at = start[0]
    row = lax.broadcasted_iota(jnp.int32, (IMGTOK, TOK), 0) + at
    col = lax.broadcasted_iota(jnp.int32, (IMGTOK, TOK), 1)
    pick = jnp.where(row == col, 1.0, 0.0).astype(bf16)
    for n in range(3):
        image[n] = nn(pick, out[n]).astype(bf16)


def patch_kernel(w, g0, g1, pw, out, acc):
    step = pl.program_id(0)

    @pl.when(step == 0)
    def _():
        acc[...] = jnp.zeros_like(acc)

    for n, g in enumerate((g0, g1)):
        t = jnp.zeros((IMGTOK, TOK), f32)
        for p in range(3):
            t = t + nt(g[p], w[0, :, p].reshape(TOK, TOK))
        acc[n] = acc[n] + nt(t.astype(bf16), pw[0])

    @pl.when(step == pl.num_programs(0) - 1)
    def _():
        out[...] = acc[...].astype(bf16)


def grad_kernel(w, g0, g1, out):
    for n, g in enumerate((g0, g1)):
        t = jnp.zeros((TOK, TOK), f32)
        for p in range(3):
            t = t + nt(w[0, :, p].reshape(TOK, TOK), g[p])
        out[0, :, n * TOK : (n + 1) * TOK] = t.astype(bf16)


def conv_kernel(scalars, pieces, k2, slope, left, out):
    head = scalars[0]
    present = scalars[1].astype(f32)
    total = jnp.zeros((IMGTOK, PCH), f32)
    for n in range(pieces.shape[0]):
        total = total + pieces[n].astype(f32)
    incoming = (total * present).astype(bf16)
    q = lax.broadcasted_iota(jnp.int32, (IMGTOK, IMGTOK), 0)
    p = lax.broadcasted_iota(jnp.int32, (IMGTOK, IMGTOK), 1)
    shifts = []
    for o in range(9):
        dr, dc = o // 3 - 1, o % 3 - 1
        hit = ((p >> 3) == (q >> 3) - dr) & ((p & 7) == (q & 7) - dc)
        shifts.append(jnp.where(hit, 1.0, 0.0).astype(bf16))
    dact = jnp.zeros((IMGTOK, 16), f32)
    for o in range(9):
        dact = dact + nt(nn(shifts[o], incoming).astype(bf16), k2[o])
    dpre = (dact * slope[...]).astype(bf16)
    ch = lax.broadcasted_iota(jnp.int32, (PCH, LANES), 0)
    lane = lax.broadcasted_iota(jnp.int32, (PCH, LANES), 1)
    spread = jnp.where((lane < 576) & ((lane & 31) == ch - 32 * head), 1.0, 0.0).astype(bf16)
    ch = lax.broadcasted_iota(jnp.int32, (16, LANES), 0)
    lane = lax.broadcasted_iota(jnp.int32, (16, LANES), 1)
    spread_first = jnp.where((lane >= 576) & ((lane & 15) == ch), 1.0, 0.0).astype(bf16)
    both = (nn(incoming, spread) + nn(dpre, spread_first)).astype(bf16)
    lane = lax.broadcasted_iota(jnp.int32, (IMGTOK, LANES), 1)
    second = jnp.where(lane >= 288, lane - 288, lane) >> 5
    first = (jnp.where(lane >= 720, lane - 720, lane - 576)) >> 4
    which = jnp.where(lane < 576, second, first)
    moved = jnp.zeros((IMGTOK, LANES), f32)
    zero = jnp.zeros((IMGTOK, LANES), bf16)
    for o in range(9):
        moved = moved + nn(shifts[o], jnp.where(which == o, both, zero))
    moved = moved.astype(bf16)
    ends = (0, 288, 576, 720, 864)
    result = jnp.zeros((IMGTOK, LANES), f32)
    for n in range(4):
        part = jnp.where((lane >= ends[n]) & (lane < ends[n + 1]), moved, zero)
        result = result + nn(left[n], part)
    out[...] = result.astype(bf16)


def whole(space=None):
    return pl.BlockSpec(memory_space=pltpu.VMEM if space is None else space)


def on_chip(kernel, shapes, count, scratch=(), scalars=0):
    return pl.pallas_call(
        kernel,
        out_shape=shapes,
        in_specs=[whole(pltpu.SMEM)] * scalars + [whole()] * (count - scalars),
        out_specs=jax.tree.map(lambda _: whole(), shapes),
        scratch_shapes=list(scratch),
    )


def spec_of(shape, dtype):
    return jax.ShapeDtypeStruct(shape, dtype)


def pick_entry(lookup, wanted):
    return jnp.sum(jnp.where(jnp.arange(lookup.shape[0]) == wanted, lookup, 0))


def passed_along(block, axis, distance):
    devices = range(lax.axis_size(axis))
    route = [(i - distance, i) for i in devices if i - distance in devices]
    return lax.ppermute(block, axis, route)


def swapped(value):
    return lax.ppermute(value, "yl", [(0, 1), (1, 0)])


def exchanged(pieces, axis):
    return lax.all_to_all(pieces, axis, split_axis=0, concat_axis=0, tiled=True)


def sent_to_all(value, axis):
    return exchanged(jnp.broadcast_to(value, (lax.axis_size(axis), *value.shape)), axis)


def adam_update(param, mean, square, grad):
    new_mean = beta_one * mean + (1.0 - beta_one) * grad
    new_square = beta_two * square + (1.0 - beta_two) * grad * grad
    fixed_mean = new_mean / (1.0 - beta_one**adam_step)
    fixed_square = new_square / (1.0 - beta_two**adam_step)
    new_param = param - learn_rate * (
        fixed_mean / (jnp.sqrt(fixed_square) + adam_eps) + decay_rate * param
    )
    return (new_param, new_mean, new_square)


def seen_range(block, doc_lengths, image_count, image_offset):
    index = jnp.arange(doc_lengths.shape[0])
    ends = jnp.sum(jnp.where(index[None, :] <= index[:, None], doc_lengths[None, :], 0), axis=1)
    starts = ends - doc_lengths
    base = block * TOK
    places = base + jnp.arange((REACH + 1) * TOK, dtype=jnp.int32)
    begun = starts[:, None] <= places[None, :]
    low = jnp.max(jnp.where(begun, starts[:, None], 0), axis=0)
    own = places[:TOK]
    over = ends[:, None] > own[None, :]
    doc_end = jnp.min(jnp.where(over, ends[:, None], jnp.int32(1 << 30)), axis=0)
    present = pick_entry(image_count, block)
    offset = pick_entry(image_offset, block)
    local = own - base
    inside = (present > 0) & (local >= offset) & (local < offset + IMGTOK)
    high = jnp.where(
        inside, jnp.maximum(own, jnp.minimum(base + offset + IMGTOK, doc_end) - 1), own
    )
    rows = [high[None], low.reshape(REACH + 1, TOK), jnp.zeros((2, TOK), jnp.int32) + base]
    return jnp.concatenate(rows, axis=0) - base, present, offset


def shards(
    queries,
    keys,
    values,
    out_grad,
    qkv_weight,
    doc_lengths,
    image_count,
    image_offset,
    slab_owner,
    patch_weight,
    conv_input,
    pre_act,
    kernel_first,
    kernel_second,
    mean_first,
    mean_second,
    square_first,
    square_second,
):
    device_index = lax.axis_index(WIDE)
    head_index = lax.axis_index("head")
    side = lax.axis_index("yl")

    before = jnp.stack([keys, values])
    after = jnp.stack([queries, out_grad])
    earlier, later = [], []
    for _ in range(REACH):
        before = passed_along(before, WIDE, 1)
        after = passed_along(after, WIDE, -1)
        earlier.append(before)
        later.append(after)

    meta, present, offset = seen_range(device_index, doc_lengths, image_count, image_offset)

    weights = lax.all_gather(qkv_weight, ("z", "yh"), axis=0).reshape(8, 4, 3, 64, TOK)
    half_patch = lax.dynamic_index_in_dim(
        patch_weight.reshape(PCH, 4, 2, 64), side, 2, keepdims=False
    ).reshape(PCH, TOK)
    patch_half = lax.all_gather(half_patch, "head", axis=0)
    rows = jnp.concatenate([conv_input.reshape(PCOLS, CIN), pre_act.reshape(PCOLS, CMID)], axis=1)
    slots = lax.all_gather(rows, WIDE, axis=0)
    slot = pick_entry(slab_owner, device_index)
    my_rows = lax.dynamic_index_in_dim(slots, slot, 0, keepdims=False)
    picture = lax.all_gather(my_rows, "head", axis=0).reshape(IMGTOK, CIN + CMID)
    kernel_all = lax.all_gather(kernel_second.astype(bf16), WIDE, axis=0)
    kernel_mine = lax.dynamic_slice_in_dim(
        kernel_all.reshape(CMID, 9, PCH), head_index * 16, 16, 0
    ).transpose(1, 0, 2)

    conv_img = picture[:, :CIN]
    pre_img = picture[:, CIN:].astype(f32)
    act = jax.nn.silu(pre_img).astype(bf16)
    left = jnp.concatenate([act.T.reshape(64, 2, 64), conv_img.T.reshape(64, 2, 64)], axis=1)
    left = left.transpose(1, 0, 2)
    sig = jax.nn.sigmoid(pre_img)
    slope = sig * (1.0 + pre_img * (1.0 - sig))
    slope = lax.dynamic_slice_in_dim(slope, head_index * 16, 16, 1)

    stats = on_chip(
        stats_kernel,
        spec_of((8, TOK), f32),
        9,
        [pltpu.VMEM((REACH + 1, TOK, TOK), f32)],
    )(meta, queries, out_grad, keys, values, *earlier)
    stats_later = [passed_along(stats, WIDE, -d) for d in range(1, REACH + 1)]
    dq, dk, dv = on_chip(
        own_kernel,
        (spec_of((TOK, TOK), bf16), spec_of((TOK, TOK), f32), spec_of((TOK, TOK), f32)),
        10,
    )(meta, stats, queries, out_grad, keys, values, *earlier)
    grads, image_grads = on_chip(
        later_kernel,
        (spec_of((3, TOK, TOK), bf16), spec_of((3, IMGTOK, TOK), bf16)),
        15,
        scalars=1,
    )(offset[None], meta, keys, values, *later, *stats_later, dq, dk, dv)

    image_other = swapped(image_grads)
    grads_other = swapped(grads)

    def in_order(own, other):
        return jnp.where(side == 0, own, other), jnp.where(side == 0, other, own)

    weight_block = pl.BlockSpec((1, 4, 3, 64, TOK), lambda i: (i, 0, 0, 0, 0))

    def fixed(*shape):
        return pl.BlockSpec(shape, lambda i: (0,) * len(shape))

    patch_part = pl.pallas_call(
        patch_kernel,
        out_shape=spec_of((2, IMGTOK, PCH), bf16),
        grid=(8,),
        in_specs=[
            weight_block,
            fixed(3, IMGTOK, TOK),
            fixed(3, IMGTOK, TOK),
            pl.BlockSpec((1, PCH, TOK), lambda i: (i, 0, 0)),
        ],
        out_specs=fixed(2, IMGTOK, PCH),
        scratch_shapes=[pltpu.VMEM((2, IMGTOK, PCH), f32)],
    )(weights, *in_order(image_grads, image_other), patch_half)
    pieces = exchanged(
        jnp.broadcast_to(patch_part, (8, 2, IMGTOK, PCH)).reshape(16, IMGTOK, PCH), ("head", "yl")
    )

    flags = jnp.stack([head_index.astype(jnp.int32), present.astype(jnp.int32)])
    partial = on_chip(conv_kernel, spec_of((64, LANES), bf16), 5, scalars=1)(
        flags, pieces, kernel_mine, slope, left
    )

    halves = pl.pallas_call(
        grad_kernel,
        out_shape=spec_of((8, TOK, 2 * TOK), bf16),
        grid=(8,),
        in_specs=[weight_block, fixed(3, TOK, TOK), fixed(3, TOK, TOK)],
        out_specs=pl.BlockSpec((1, TOK, 2 * TOK), lambda i: (i, 0, 0)),
    )(weights, *in_order(grads, grads_other))
    summed = jnp.sum(exchanged(halves, "head").astype(f32), axis=0).astype(bf16)
    mine, theirs = in_order(summed[:, :TOK], summed[:, TOK:])
    arrived = swapped(theirs)
    even, odd = in_order(mine, arrived)
    input_grad_t = jnp.stack([even.reshape(4, 64, TOK), odd.reshape(4, 64, TOK)], axis=1)
    input_grad_t = input_grad_t.reshape(512, TOK)

    owned = exchanged(partial.reshape(64, 7, 128), WIDE)
    owned = jnp.sum(owned.astype(f32), axis=0)
    squares = jnp.broadcast_to(jnp.sum(owned * owned), (1, 128))
    squares = jnp.sum(sent_to_all(squares, WIDE), axis=0)
    together = sent_to_all(jnp.concatenate([owned, squares], axis=0), "head")
    total = jnp.sum(together[:, 7, 0])
    columns = together[:, :7].reshape(8, LANES)
    grad_second = (
        columns[:, :576].reshape(8, 2, 9, 32).transpose(1, 2, 0, 3).reshape(18, PCH)
    )
    grad_first = (
        columns[:, 576:864].reshape(8, 2, 9, 16).transpose(1, 2, 0, 3).reshape(18, CMID)
    )
    limit = 0.5 * math.sqrt(9 * CIN * CMID + 9 * CMID * PCH)
    factor = jnp.minimum(1.0, limit / (jnp.sqrt(total) + norm_eps))
    kernel_one, mean_one, square_one = adam_update(
        kernel_first, mean_first, square_first, grad_first * factor
    )
    kernel_two, mean_two, square_two = adam_update(
        kernel_second, mean_second, square_second, grad_second * factor
    )
    return (input_grad_t, kernel_one, kernel_two, mean_one, mean_two, square_one, square_two)


def solution(mesh):
    split = Mesh(mesh.devices.reshape(mesh.shape["head"], 8, 4, 2), ("head", *WIDE))
    placed = (
        P(WIDE, "head"),
        P(WIDE, "head"),
        P(WIDE, "head"),
        P(WIDE, "head"),
        P(None, WIDE, "head"),
        P(),
        P(),
        P(),
        P(),
        P(None, "head"),
        P(WIDE, "head", None, None),
        P(WIDE, "head", None, None),
        P(WIDE, None),
        P(WIDE, None),
        P(WIDE, None),
        P(WIDE, None),
        P(WIDE, None),
        P(WIDE, None),
    )
    return jax.shard_map(
        shards,
        mesh=split,
        in_specs=placed,
        out_specs=(
            P("head", WIDE),
            P(WIDE, None),
            P(WIDE, None),
            P(WIDE, None),
            P(WIDE, None),
            P(WIDE, None),
            P(WIDE, None),
        ),
        check_vma=False,
    )
```

time: 417 us -> 353 us (0.85)
  the two profiles are of different devices: /device:TPU:8 before, /device:TPU:1 now
where the time goes in v1:
time: 353 us; the launch traced here: 352 us
  blocking collectives  161 us (46%)
  starting transfers between devices  73.1 us (21%)
  waiting for transfers between devices  40 us (11%)
  Pallas kernels  33.7 us (10%)
  between operations  19.3 us (5%)
  other arithmetic  14.3 us (4%)
  local copies, waits for them, and re-layouts  10.4 us (3%)
    all_gather x1, blocking collectives, shards(): kernel_all = lax.all_gather(kernel_second.astype(bf16), WIDE, axis=0)  55.6 us
    all_gather x1, blocking collectives, shards(): slots = lax.all_gather(rows, WIDE, axis=0)  53 us
    all_gather x1, blocking collectives, shards(): lax.all_gather(my_rows, 'head', axis=0).reshape(IMGTOK, CIN + CMID)  37.7 us
    all_to_all x4, starting transfers between devices, exchanged(): return lax.all_to_all(pieces, axis, split_axis=0, concat_axis=0, tiled=True)  36.7 us
    all_to_all x4, waiting for transfers between devices, exchanged(): return lax.all_to_all(pieces, axis, split_axis=0, concat_axis=0, tiled=True)  32.2 us
    ppermute x12, starting transfers between devices, passed_along(): return lax.ppermute(block, axis, route)  25.7 us
    all_to_all x1, blocking collectives, exchanged(): return lax.all_to_all(pieces, axis, split_axis=0, concat_axis=0, tiled=True)  14.8 us
    ppermute x3, starting transfers between devices, swapped(): return lax.ppermute(value, 'yl', [(0, 1), (1, 0)])  10.6 us
  transfers between devices with their start and end apart: 21, of which 5 were waited for; matrix products, arithmetic and copies ran while one was open for 5% of the time, Pallas kernels for 6%

profile of v1, /device:TPU:1, one launch (start us, length us, event | category | flops | bytes accessed | tf_op | source)
XLA Modules:
  0.0 351.8 jit_solution(15689284437141765366)
XLA Ops:
  7.3 1.1 copy.62
  8.4 0.8 copy.63
  9.2 0.7 all-gather.9.cloned.1.call-update
  9.9 1.0 pad_maximum_fusion.1
  10.9 4.0 %collective-permute-start.4 = (bf16[2,256,256]{2,1,0:T(8,128)(2,1)S(1)}, bf16[2,256,256]{2,1,0:T(8,128)(2,1)S(1)}, u32[]{:S(2)}, u32[]{:S(2)}) collective-permute-start(bf16[2,256,256]{2,1,0:T(8,128)(2,1)S(1)} %pad_maximum_fusion.1), channel_id=1, source_target_pairs={{0,1},{1,2},{2,3},{3,4},{4,5},{5,6},{6,7},{7,8},{8,9},{9,10},{10,1... | collective-permute-start | bytes 786440 | tf_op jit(solution)/shard_map/ppermute | solution.py:246
  15.0 1.0 pad_maximum_fusion
  16.0 1.3 collective-permute-start
  19.3 4.0 %collective-permute-start.5 = (bf16[2,256,256]{2,1,0:T(8,128)(2,1)S(1)}, bf16[2,256,256]{2,1,0:T(8,128)(2,1)S(1)}, u32[]{:S(2)}, u32[]{:S(2)}) collective-permute-start(bf16[2,256,256]{2,1,0:T(8,128)(2,1)S(1)} %collective-permute-done.4.b1), channel_id=1, source_target_pairs={{0,1},{1,2},{2,3},{3,4},{4,5},{5,6},{6,7},{7,8},{8,9},{9,10},{10,1... | collective-permute-start | bytes 786440 | tf_op jit(solution)/shard_map/ppermute | solution.py:246
  23.3 1.3 collective-permute-start.1
  28.7 5.3 %collective-permute-start.6 = (bf16[2,256,256]{2,1,0:T(8,128)(2,1)S(1)}, bf16[2,256,256]{2,1,0:T(8,128)(2,1)S(1)}, u32[]{:S(2)}, u32[]{:S(2)}) collective-permute-start(bf16[2,256,256]{2,1,0:T(8,128)(2,1)S(1)} %collective-permute-done.5.b2), channel_id=1, source_target_pairs={{0,1},{1,2},{2,3},{3,4},{4,5},{5,6},{6,7},{7,8},{8,9},{9,10},{10,1... | collective-permute-start | bytes 786440 | tf_op jit(solution)/shard_map/ppermute | solution.py:246
  34.0 1.3 collective-permute-start.2
  35.3 53.0 %all-gather.2 = bf16[512,256]{1,0:T(8,128)(2,1)S(1)} all-gather(bf16[8,256]{1,0:T(8,128)(2,1)S(1)} %pad_maximum_fusion.3), channel_id=4, replica_groups=mesh['head'=8,'z'=8,'yh'=4,'yl'=2] {'z','yh','yl'}, dimensions={0}, use_global_device_ids=true | all-gather | bytes 266240 | tf_op jit(solution)/shard_map/all_gather | solution.py:335
  88.9 2.1 collective-permute-start.7
  91.1 1.3 collective-permute-start.3
  93.2 1.2 collective-permute-done.7.b4
  94.3 0.7 copy-done.4
  95.0 3.7 %shard_map.225.stats = f32[8,256]{1,0:T(8,128)} custom-call(s32[8,256]{1,0:T(8,128)} %add_subtract_fusion.meta, bf16[256,256]{1,0:T(8,128)(2,1)} %q.3, bf16[256,256]{1,0:T(8,128)(2,1)} %g.3, bf16[256,256]{1,0:T(8,128)(2,1)} %k0.5, bf16[256,256]{1,0:T(8,128)(2,1)} %v0.5, bf16[2,256,256]{2,1,0:T(8,128)(2,1)} %copy-done.1, bf16[2,256,256]{2,1,0:T(8,128)(2,1)} %copy-done.2, ...), custom_call_target="tpu_custom_call" | custom-call | tf_op jit(solution)/shard_map/pallas_call | solution.py:353
  98.7 1.3 collective-permute-start.10
  100.0 1.3 collective-permute-start.11
  101.3 1.3 collective-permute-start.8
  102.6 1.3 collective-permute-start.9
  103.9 37.7 %all_gather.32 = bf16[8,8,256]{2,1,0:T(8,128)(2,1)S(1)} all-gather(bf16[1,8,256]{2,1,0:T(8,128)(2,1)S(1)} %constant_dynamic-slice_fusion), channel_id=1, replica_groups=mesh['head'=8,'z'=8,'yh'=4,'yl'=2] {'head'}, dimensions={0}, use_global_device_ids=true | all-gather | bytes 36864 | tf_op jit(solution)/shard_map/all_gather | solution.py:338
  141.6 5.2 %shard_map.226 = (bf16[256,256]{1,0:T(8,128)(2,1)}, f32[256,256]{1,0:T(8,128)}, f32[256,256]{1,0:T(8,128)}) custom-call(s32[8,256]{1,0:T(8,128)} %add_subtract_fusion.meta, f32[8,256]{1,0:T(8,128)} %shard_map.225.stats, bf16[256,256]{1,0:T(8,128)(2,1)} %q.3, bf16[256,256]{1,0:T(8,128)(2,1)} %g.3, bf16[256,256]{1,0:T(8,128)(2,1)} %k0.5, bf16[256,256]{1,0:T(8,128)(2,1)} %v0.5, ...), custom_call_target="tpu_custom_call" | custom-call | tf_op jit(solution)/shard_map/pallas_call | solution.py:360
  147.4 5.1 %shard_map.227 = (bf16[3,256,256]{2,1,0:T(8,128)(2,1)}, bf16[3,64,256]{2,1,0:T(8,128)(2,1)}) custom-call(s32[1]{0:T(128)} %bitcast.1.start, s32[8,256]{1,0:T(8,128)} %add_subtract_fusion.meta, bf16[256,256]{1,0:T(8,128)(2,1)} %k0.5, bf16[256,256]{1,0:T(8,128)(2,1)} %v0.5, bf16[2,256,256]{2,1,0:T(8,128)(2,1)} %copy-done.6, bf16[2,256,256]{2,1,0:T(8,128)(2,1)} %copy-done.7, ...), custom_call_target="tpu_custom_call" | custom-call | tf_op jit(solution)/shard_map/pallas_call | solution.py:365
  152.5 5.5 %collective-permute-start.14 = (bf16[3,64,256]{2,1,0:T(8,128)(2,1)}, bf16[3,64,256]{2,1,0:T(8,128)(2,1)S(1)}, u32[]{:S(2)}, u32[]{:S(2)}) collective-permute-start(bf16[3,64,256]{2,1,0:T(8,128)(2,1)} %get-tuple-element.16), channel_id=1, source_target_pairs={{0,1},{1,0},{2,3},{3,2},{4,5},{5,4},{6,7},{7,6},{8,9},{9,8},{10,11... | collective-permute-start | bytes 294920 | tf_op jit(solution)/shard_map/ppermute | solution.py:250
  158.2 3.0 collective-permute-done.14
  161.2 1.6 broadcast_select_fusion.6
  162.8 8.9 %shard_map.229 = bf16[2,64,256]{2,1,0:T(8,128)(2,1)} custom-call(bf16[8,4,3,64,256]{4,3,2,1,0:T(8,128)(2,1)} %bitcast.44, bf16[3,64,256]{2,1,0:T(8,128)(2,1)} %get-tuple-element.28.g0, bf16[3,64,256]{2,1,0:T(8,128)(2,1)} %get-tuple-element.27.g1, bf16[8,256,256]{2,1,0:T(8,128)(2,1)} %all-gather.7.cloned.1.call-done.pw), custom_call_target="tpu_custom_call" | custom-call | tf_op jit(solution)/shard_map/pallas_call | solution.py:383
  171.7 1.7 broadcast_in_dim.66
  173.4 5.5 %all-to-all-start.1 = ((bf16[16,64,256]{2,1,0:T(8,128)(2,1)}), bf16[16,64,256]{2,1,0:T(8,128)(2,1)S(1)}, u32[]{:S(2)}, u32[]{:S(2)}) async-start(bf16[16,64,256]{2,1,0:T(8,128)(2,1)} %bitcast.14), calls=%async_computation.1 | async-start | bytes 1048576 | tf_op jit(solution)/shard_map/all_to_all | solution.py:254
  179.0 55.6 %all-gather.3 = bf16[64,18,256]{2,1,0:T(8,128)(2,1)S(1)} all-gather(bf16[1,18,256]{2,1,0:T(8,128)(2,1)S(1)} %convert_bitcast_fusion), channel_id=3, replica_groups=mesh['head'=8,'z'=8,'yh'=4,'yl'=2] {'z','yh','yl'}, dimensions={0}, use_global_device_ids=true | all-gather | bytes 599040 | tf_op jit(solution)/shard_map/all_gather | solution.py:339
  235.5 1.1 pad_add_fusion.scalars
  236.6 0.7 fusion.1.slope
  238.0 0.8 copy-done
  238.8 3.3 shard_map.230
  242.1 1.7 reshape.86
  243.8 8.5 %all-to-all-start.2 = ((bf16[64,7,128]{2,1,0:T(8,128)(2,1)}), bf16[64,7,128]{2,1,0:T(8,128)(2,1)S(1)}, u32[]{:S(2)}, u32[]{:S(2)}) async-start(bf16[64,7,128]{2,1,0:T(8,128)(2,1)} %reshape.86), calls=%async_computation.2 | async-start | bytes 262144 | tf_op jit(solution)/shard_map/all_to_all | solution.py:254
  252.4 2.9 collective-permute-start.12
  255.3 8.6 %all-to-all-done.2 = bf16[64,7,128]{2,1,0:T(8,128)(2,1)S(1)} async-done(((bf16[64,7,128]{2,1,0:T(8,128)(2,1)}), bf16[64,7,128]{2,1,0:T(8,128)(2,1)S(1)}, u32[]{:S(2)}, u32[]{:S(2)}) %all-to-all-start.2) | async-done | bytes 114720 | tf_op jit(solution)/shard_map/all_to_all | solution.py:254
  265.3 14.8 %all_to_all.25 = f32[64,1,128]{2,1,0:T(1,128)S(1)} all-to-all(f32[64,1,128]{2,1,0:T(1,128)S(1)} %broadcast_in_dim_broadcast_in_dim.3), channel_id=1, replica_groups=mesh['head'=8,'z'=8,'yh'=4,'yl'=2] {'z','yh','yl'}, dimensions={0} | all-to-all | bytes 65536 | tf_op jit(solution)/shard_map/all_to_all | solution.py:254
  280.7 17.7 %all-to-all-start.4 = ((f32[8,8,128]{2,1,0:T(8,128)}), f32[8,8,128]{2,1,0:T(8,128)S(1)}, u32[]{:S(2)}, u32[]{:S(2)}) async-start(f32[8,8,128]{2,1,0:T(8,128)} %broadcast_in_dim.67), calls=%async_computation.4 | async-start | bytes 65536 | tf_op jit(solution)/shard_map/all_to_all | solution.py:254
  298.5 0.9 broadcast_select_fusion
  299.4 7.5 %shard_map.228 = bf16[8,256,512]{2,1,0:T(8,128)(2,1)} custom-call(bf16[8,4,3,64,256]{4,3,2,1,0:T(8,128)(2,1)} %bitcast.45, bf16[3,256,256]{2,1,0:T(8,128)(2,1)} %get-tuple-element.24.g0, bf16[3,256,256]{2,1,0:T(8,128)(2,1)} %get-tuple-element.23.g1), custom_call_target="tpu_custom_call" | custom-call | tf_op jit(solution)/shard_map/pallas_call | solution.py:405
  307.0 4.9 %all-to-all-start = ((bf16[8,256,512]{2,1,0:T(8,128)(2,1)}), bf16[8,256,512]{2,1,0:T(8,128)(2,1)S(1)}, u32[]{:S(2)}, u32[]{:S(2)}) async-start(bf16[8,256,512]{2,1,0:T(8,128)(2,1)} %shard_map.228), calls=%async_computation | async-start | bytes 4194304 | tf_op jit(solution)/shard_map/all_to_all | solution.py:254
  314.5 23.6 %all-to-all-done = bf16[8,256,512]{2,1,0:T(8,128)(2,1)S(1)} async-done(((bf16[8,256,512]{2,1,0:T(8,128)(2,1)}), bf16[8,256,512]{2,1,0:T(8,128)(2,1)S(1)}, u32[]{:S(2)}, u32[]{:S(2)}) %all-to-all-start) | async-done | bytes 2097184 | tf_op jit(solution)/shard_map/all_to_all | solution.py:254
  338.5 2.2 collective-permute-start.13
  341.4 2.8 collective-permute-done.13
  344.3 0.7 pad_maximum_fusion.2
  (118 shorter events, 11.0 us)
Async XLA Ops:
  7.2 10.1 %copy-start.22 = (s32[64]{0:T(128)S(1)}, s32[64]{0:T(128)}, u32[]{:S(2)}) copy-start(s32[64]{0:T(128)} %param.25) | copy-start | bytes 772
  7.2 10.7 %copy-start.23 = (s32[64]{0:T(128)S(1)}, s32[64]{0:T(128)}, u32[]{:S(2)}) copy-start(s32[64]{0:T(128)} %param.24) | copy-start | bytes 772
  7.2 11.3 %copy-start.24 = (s32[64]{0:T(128)S(1)}, s32[64]{0:T(128)}, u32[]{:S(2)}) copy-start(s32[64]{0:T(128)} %param.26) | copy-start | bytes 772
  7.2 12.0 %copy-start.25 = (s32[32]{0:T(128)S(1)}, s32[32]{0:T(128)}, u32[]{:S(2)}) copy-start(s32[32]{0:T(128)} %param.23) | copy-start | bytes 388
  7.2 17.4 %copy-start.21 = (bf16[1,1,8,128]{3,2,1,0:T(8,128)(2,1)S(1)}, bf16[1,1,8,128]{3,2,1,0:T(8,128)(2,1)}, u32[]{:S(2)}) copy-start(bf16[1,1,8,128]{3,2,1,0:T(8,128)(2,1)} %param.28) | copy-start | bytes 6148
  7.2 17.4 %copy-start.20 = (bf16[1,1,8,128]{3,2,1,0:T(8,128)(2,1)S(1)}, bf16[1,1,8,128]{3,2,1,0:T(8,128)(2,1)}, u32[]{:S(2)}) copy-start(bf16[1,1,8,128]{3,2,1,0:T(8,128)(2,1)} %param.29) | copy-start | bytes 6148
  7.2 155.5 %all-gather.7.cloned.1.call-start = ((), (), s32[]{:S(2)}) async-start(), calls=%async_computation.5 | async-start | bytes 1179648 | tf_op jit(solution)/shard_map/all_gather | solution.py:333
  9.2 153.6 %all-gather.9.cloned.1.call-start = ((), (), s32[]{:S(2)}) async-start(), calls=%async_computation.6 | async-start | bytes 3244032 | tf_op jit(solution)/shard_map/all_gather | solution.py:329
  10.9 8.4 %collective-permute-start.4 = (bf16[2,256,256]{2,1,0:T(8,128)(2,1)S(1)}, bf16[2,256,256]{2,1,0:T(8,128)(2,1)S(1)}, u32[]{:S(2)}, u32[]{:S(2)}) collective-permute-start(bf16[2,256,256]{2,1,0:T(8,128)(2,1)S(1)} %pad_maximum_fusion.1), channel_id=1, source_target_pairs={{0,1},{1,2},{2,3},{3,4},{4,5},{5,6},{6,7},{7,8},{8,9},{9,10},{10,1... | collective-permute-start | bytes 786440 | tf_op jit(solution)/shard_map/ppermute | solution.py:246
  16.0 7.3 %collective-permute-start = (bf16[2,256,256]{2,1,0:T(8,128)(2,1)S(1)}, bf16[2,256,256]{2,1,0:T(8,128)(2,1)S(1)}, u32[]{:S(2)}, u32[]{:S(2)}) collective-permute-start(bf16[2,256,256]{2,1,0:T(8,128)(2,1)S(1)} %pad_maximum_fusion), channel_id=1, source_target_pairs={{1,0},{2,1},{3,2},{4,3},{5,4},{6,5},{7,6},{8,7},{9,8},{10,9},{11,1... | collective-permute-start | bytes 786440 | tf_op jit(solution)/shard_map/ppermute | solution.py:246
  19.3 75.0 %copy-start.1 = (bf16[2,256,256]{2,1,0:T(8,128)(2,1)}, bf16[2,256,256]{2,1,0:T(8,128)(2,1)S(1)}, u32[]{:S(2)}) copy-start(bf16[2,256,256]{2,1,0:T(8,128)(2,1)S(1)} %collective-permute-done.4.b1) | copy-start | bytes 786436
  19.3 9.4 %collective-permute-start.5 = (bf16[2,256,256]{2,1,0:T(8,128)(2,1)S(1)}, bf16[2,256,256]{2,1,0:T(8,128)(2,1)S(1)}, u32[]{:S(2)}, u32[]{:S(2)}) collective-permute-start(bf16[2,256,256]{2,1,0:T(8,128)(2,1)S(1)} %collective-permute-done.4.b1), channel_id=1, source_target_pairs={{0,1},{1,2},{2,3},{3,4},{4,5},{5,6},{6,7},{7,8},{8,9},{9,10},{10,1... | collective-permute-start | bytes 786440 | tf_op jit(solution)/shard_map/ppermute | solution.py:246
  23.3 123.5 %copy-start.6 = (bf16[2,256,256]{2,1,0:T(8,128)(2,1)}, bf16[2,256,256]{2,1,0:T(8,128)(2,1)S(1)}, u32[]{:S(2)}) copy-start(bf16[2,256,256]{2,1,0:T(8,128)(2,1)S(1)} %collective-permute-done.a1) | copy-start | bytes 786436
  23.3 10.6 %collective-permute-start.1 = (bf16[2,256,256]{2,1,0:T(8,128)(2,1)S(1)}, bf16[2,256,256]{2,1,0:T(8,128)(2,1)S(1)}, u32[]{:S(2)}, u32[]{:S(2)}) collective-permute-start(bf16[2,256,256]{2,1,0:T(8,128)(2,1)S(1)} %collective-permute-done.a1), channel_id=1, source_target_pairs={{1,0},{2,1},{3,2},{4,3},{5,4},{6,5},{7,6},{8,7},{9,8},{10,9},{11,1... | collective-permute-start | bytes 786440 | tf_op jit(solution)/shard_map/ppermute | solution.py:246
  28.7 65.7 %copy-start.2 = (bf16[2,256,256]{2,1,0:T(8,128)(2,1)}, bf16[2,256,256]{2,1,0:T(8,128)(2,1)S(1)}, u32[]{:S(2)}) copy-start(bf16[2,256,256]{2,1,0:T(8,128)(2,1)S(1)} %collective-permute-done.5.b2) | copy-start | bytes 786436
  28.7 60.2 %collective-permute-start.6 = (bf16[2,256,256]{2,1,0:T(8,128)(2,1)S(1)}, bf16[2,256,256]{2,1,0:T(8,128)(2,1)S(1)}, u32[]{:S(2)}, u32[]{:S(2)}) collective-permute-start(bf16[2,256,256]{2,1,0:T(8,128)(2,1)S(1)} %collective-permute-done.5.b2), channel_id=1, source_target_pairs={{0,1},{1,2},{2,3},{3,4},{4,5},{5,6},{6,7},{7,8},{8,9},{9,10},{10,1... | collective-permute-start | bytes 786440 | tf_op jit(solution)/shard_map/ppermute | solution.py:246
  34.0 112.9 %copy-start.7 = (bf16[2,256,256]{2,1,0:T(8,128)(2,1)}, bf16[2,256,256]{2,1,0:T(8,128)(2,1)S(1)}, u32[]{:S(2)}) copy-start(bf16[2,256,256]{2,1,0:T(8,128)(2,1)S(1)} %collective-permute-done.1.a2) | copy-start | bytes 786436
  34.0 57.1 %collective-permute-start.2 = (bf16[2,256,256]{2,1,0:T(8,128)(2,1)S(1)}, bf16[2,256,256]{2,1,0:T(8,128)(2,1)S(1)}, u32[]{:S(2)}, u32[]{:S(2)}) collective-permute-start(bf16[2,256,256]{2,1,0:T(8,128)(2,1)S(1)} %collective-permute-done.1.a2), channel_id=1, source_target_pairs={{1,0},{2,1},{3,2},{4,3},{5,4},{6,5},{7,6},{8,7},{9,8},{10,9},{11,1... | collective-permute-start | bytes 786440 | tf_op jit(solution)/shard_map/ppermute | solution.py:246
  88.9 5.4 %copy-start.3 = (bf16[2,256,256]{2,1,0:T(8,128)(2,1)}, bf16[2,256,256]{2,1,0:T(8,128)(2,1)S(1)}, u32[]{:S(2)}) copy-start(bf16[2,256,256]{2,1,0:T(8,128)(2,1)S(1)} %collective-permute-done.6.b3) | copy-start | bytes 786436
  88.9 5.4 %collective-permute-start.7 = (bf16[2,256,256]{2,1,0:T(8,128)(2,1)S(1)}, bf16[2,256,256]{2,1,0:T(8,128)(2,1)S(1)}, u32[]{:S(2)}, u32[]{:S(2)}) collective-permute-start(bf16[2,256,256]{2,1,0:T(8,128)(2,1)S(1)} %collective-permute-done.6.b3), channel_id=1, source_target_pairs={{0,1},{1,2},{2,3},{3,4},{4,5},{5,6},{6,7},{7,8},{8,9},{9,10},{10,1... | collective-permute-start | bytes 786440 | tf_op jit(solution)/shard_map/ppermute | solution.py:246
  91.1 55.8 %copy-start.8 = (bf16[2,256,256]{2,1,0:T(8,128)(2,1)}, bf16[2,256,256]{2,1,0:T(8,128)(2,1)S(1)}, u32[]{:S(2)}) copy-start(bf16[2,256,256]{2,1,0:T(8,128)(2,1)S(1)} %collective-permute-done.2.a3) | copy-start | bytes 786436
  91.1 55.7 %collective-permute-start.3 = (bf16[2,256,256]{2,1,0:T(8,128)(2,1)S(1)}, bf16[2,256,256]{2,1,0:T(8,128)(2,1)S(1)}, u32[]{:S(2)}, u32[]{:S(2)}) collective-permute-start(bf16[2,256,256]{2,1,0:T(8,128)(2,1)S(1)} %collective-permute-done.2.a3), channel_id=1, source_target_pairs={{1,0},{2,1},{3,2},{4,3},{5,4},{6,5},{7,6},{8,7},{9,8},{10,9},{11,1... | collective-permute-start | bytes 786440 | tf_op jit(solution)/shard_map/ppermute | solution.py:246
  94.3 0.7 copy-start.4
  98.7 48.0 %collective-permute-start.10 = (f32[8,256]{1,0:T(8,128)}, f32[8,256]{1,0:T(8,128)S(1)}, u32[]{:S(2)}, u32[]{:S(2)}) collective-permute-start(f32[8,256]{1,0:T(8,128)} %shard_map.225.stats), channel_id=1, source_target_pairs={{3,0},{4,1},{5,2},{6,3},{7,4},{8,5},{9,6},{10,7},{11,8},{12,9},{13... | collective-permute-start | bytes 24584 | tf_op jit(solution)/shard_map/ppermute | solution.py:246
  100.0 46.8 %collective-permute-start.11 = (f32[8,256]{1,0:T(8,128)}, f32[8,256]{1,0:T(8,128)S(1)}, u32[]{:S(2)}, u32[]{:S(2)}) collective-permute-start(f32[8,256]{1,0:T(8,128)} %shard_map.225.stats), channel_id=1, source_target_pairs={{4,0},{5,1},{6,2},{7,3},{8,4},{9,5},{10,6},{11,7},{12,8},{13,9},{1... | collective-permute-start | bytes 24584 | tf_op jit(solution)/shard_map/ppermute | solution.py:246
  101.3 45.5 %collective-permute-start.8 = (f32[8,256]{1,0:T(8,128)}, f32[8,256]{1,0:T(8,128)S(1)}, u32[]{:S(2)}, u32[]{:S(2)}) collective-permute-start(f32[8,256]{1,0:T(8,128)} %shard_map.225.stats), channel_id=1, source_target_pairs={{1,0},{2,1},{3,2},{4,3},{5,4},{6,5},{7,6},{8,7},{9,8},{10,9},{11,1... | collective-permute-start | bytes 24584 | tf_op jit(solution)/shard_map/ppermute | solution.py:246
  102.6 44.2 %collective-permute-start.9 = (f32[8,256]{1,0:T(8,128)}, f32[8,256]{1,0:T(8,128)S(1)}, u32[]{:S(2)}, u32[]{:S(2)}) collective-permute-start(f32[8,256]{1,0:T(8,128)} %shard_map.225.stats), channel_id=1, source_target_pairs={{2,0},{3,1},{4,2},{5,3},{6,4},{7,5},{8,6},{9,7},{10,8},{11,9},{12,... | collective-permute-start | bytes 24584 | tf_op jit(solution)/shard_map/ppermute | solution.py:246
  146.7 0.7 copy-start.9
  146.8 0.7 copy-start.16
  146.8 0.7 copy-start.17
  146.8 0.6 copy-start.18
  146.8 0.6 copy-start.19
  152.5 8.7 %collective-permute-start.14 = (bf16[3,64,256]{2,1,0:T(8,128)(2,1)}, bf16[3,64,256]{2,1,0:T(8,128)(2,1)S(1)}, u32[]{:S(2)}, u32[]{:S(2)}) collective-permute-start(bf16[3,64,256]{2,1,0:T(8,128)(2,1)} %get-tuple-element.16), channel_id=1, source_target_pairs={{0,1},{1,0},{2,3},{3,2},{4,5},{5,4},{6,7},{7,6},{8,9},{9,8},{10,11... | collective-permute-start | bytes 294920 | tf_op jit(solution)/shard_map/ppermute | solution.py:250
  162.8 16.2 %copy-start.10 = (f32[18,256]{1,0:T(8,128)S(1)}, f32[18,256]{1,0:T(8,128)}, u32[]{:S(2)}) copy-start(f32[18,256]{1,0:T(8,128)} %param.31) | copy-start | bytes 55300
  173.4 64.6 %all-to-all-start.1 = ((bf16[16,64,256]{2,1,0:T(8,128)(2,1)}), bf16[16,64,256]{2,1,0:T(8,128)(2,1)S(1)}, u32[]{:S(2)}, u32[]{:S(2)}) async-start(bf16[16,64,256]{2,1,0:T(8,128)(2,1)} %bitcast.14), calls=%async_computation.1 | async-start | bytes 1048576 | tf_op jit(solution)/shard_map/all_to_all | solution.py:254
  234.6 17.7 %copy-start.5 = (bf16[3,256,256]{2,1,0:T(8,128)(2,1)S(1)}, bf16[3,256,256]{2,1,0:T(8,128)(2,1)}, u32[]{:S(2)}) copy-start(bf16[3,256,256]{2,1,0:T(8,128)(2,1)} %get-tuple-element.15) | copy-start | bytes 1179652
  238.0 0.8 copy-start
  243.8 20.1 %all-to-all-start.2 = ((bf16[64,7,128]{2,1,0:T(8,128)(2,1)}), bf16[64,7,128]{2,1,0:T(8,128)(2,1)S(1)}, u32[]{:S(2)}, u32[]{:S(2)}) async-start(bf16[64,7,128]{2,1,0:T(8,128)(2,1)} %reshape.86), calls=%async_computation.2 | async-start | bytes 262144 | tf_op jit(solution)/shard_map/all_to_all | solution.py:254
  252.4 46.1 %collective-permute-start.12 = (bf16[3,256,256]{2,1,0:T(8,128)(2,1)S(1)}, bf16[3,256,256]{2,1,0:T(8,128)(2,1)S(1)}, u32[]{:S(2)}, u32[]{:S(2)}) collective-permute-start(bf16[3,256,256]{2,1,0:T(8,128)(2,1)S(1)} %copy-done.5), channel_id=1, source_target_pairs={{0,1},{1,0},{2,3},{3,2},{4,5},{5,4},{6,7},{7,6},{8,9},{9,8},{10,11... | collective-permute-start | bytes 1179656 | tf_op jit(solution)/shard_map/ppermute | solution.py:250
  280.7 26.2 %all-to-all-start.4 = ((f32[8,8,128]{2,1,0:T(8,128)}), f32[8,8,128]{2,1,0:T(8,128)S(1)}, u32[]{:S(2)}, u32[]{:S(2)}) async-start(f32[8,8,128]{2,1,0:T(8,128)} %broadcast_in_dim.67), calls=%async_computation.4 | async-start | bytes 65536 | tf_op jit(solution)/shard_map/all_to_all | solution.py:254
  306.9 6.9 %copy-start.11 = (f32[18,256]{1,0:T(8,128)S(1)}, f32[18,256]{1,0:T(8,128)}, u32[]{:S(2)}) copy-start(f32[18,256]{1,0:T(8,128)} %param.33) | copy-start | bytes 55300
  306.9 6.9 %copy-start.12 = (f32[18,256]{1,0:T(8,128)S(1)}, f32[18,256]{1,0:T(8,128)}, u32[]{:S(2)}) copy-start(f32[18,256]{1,0:T(8,128)} %param.35) | copy-start | bytes 55300
  307.0 31.2 %all-to-all-start = ((bf16[8,256,512]{2,1,0:T(8,128)(2,1)}), bf16[8,256,512]{2,1,0:T(8,128)(2,1)S(1)}, u32[]{:S(2)}, u32[]{:S(2)}) async-start(bf16[8,256,512]{2,1,0:T(8,128)(2,1)} %shard_map.228), calls=%async_computation | async-start | bytes 4194304 | tf_op jit(solution)/shard_map/all_to_all | solution.py:254
  311.9 28.9 %copy-start.13 = (f32[18,128]{1,0:T(8,128)S(1)}, f32[18,128]{1,0:T(8,128)}, u32[]{:S(2)}) copy-start(f32[18,128]{1,0:T(8,128)} %param.30) | copy-start | bytes 27652
  311.9 28.9 %copy-start.14 = (f32[18,128]{1,0:T(8,128)S(1)}, f32[18,128]{1,0:T(8,128)}, u32[]{:S(2)}) copy-start(f32[18,128]{1,0:T(8,128)} %param.32) | copy-start | bytes 27652
  311.9 28.9 %copy-start.15 = (f32[18,128]{1,0:T(8,128)S(1)}, f32[18,128]{1,0:T(8,128)}, u32[]{:S(2)}) copy-start(f32[18,128]{1,0:T(8,128)} %param.34) | copy-start | bytes 27652
  338.5 5.7 %collective-permute-start.13 = (bf16[256,256]{1,0:T(8,128)(2,1)S(1)}, bf16[256,256]{1,0:T(8,128)(2,1)S(1)}, u32[]{:S(2)}, u32[]{:S(2)}) collective-permute-start(bf16[256,256]{1,0:T(8,128)(2,1)S(1)} %broadcast_select_fusion.4), channel_id=1, source_target_pairs={{0,1},{1,0},{2,3},{3,2},{4,5},{5,4},{6,7},{7,6},{8,9},{9,8},{10,11... | collective-permute-start | bytes 393224 | tf_op jit(solution)/shard_map/ppermute | solution.py:250
Sparse Core Ops, SparseCore 0:
  10.2 34.4 all-gather.6
  47.8 93.7 all-gather.8

commit v2 on v1

--- a/solution.py
+++ b/solution.py
@@ -157,11 +157,11 @@
     def _():
         acc[...] = jnp.zeros_like(acc)
 
-    for n, g in enumerate((g0, g1)):
-        t = jnp.zeros((IMGTOK, TOK), f32)
-        for p in range(3):
-            t = t + nt(g[p], w[0, :, p].reshape(TOK, TOK))
-        acc[n] = acc[n] + nt(t.astype(bf16), pw[0])
+    t = jnp.zeros((2 * IMGTOK, TOK), f32)
+    for p in range(3):
+        both = jnp.concatenate([g0[p], g1[p]], axis=0)
+        t = t + nt(both, w[0, :, p].reshape(TOK, TOK))
+    acc[...] = acc[...] + nt(t.astype(bf16), pw[0])
 
     @pl.when(step == pl.num_programs(0) - 1)
     def _():
@@ -246,6 +246,11 @@
     return lax.ppermute(block, axis, route)
 
 
+def ringed(value, axis, distance):
+    count = lax.axis_size(axis)
+    return lax.ppermute(value, axis, [(i, (i + distance) % count) for i in range(count)])
+
+
 def swapped(value):
     return lax.ppermute(value, "yl", [(0, 1), (1, 0)])
 
@@ -326,20 +331,30 @@
 
     meta, present, offset = seen_range(device_index, doc_lengths, image_count, image_offset)
 
-    weights = lax.all_gather(qkv_weight, ("z", "yh"), axis=0).reshape(8, 4, 3, 64, TOK)
+    place_z = lax.axis_index("z")
+    quad = sent_to_all(qkv_weight, "yh")
+    weights = jnp.zeros((8, *quad.shape), quad.dtype)
+    weights = lax.dynamic_update_index_in_dim(weights, quad, place_z, 0)
+    up = down = quad
+    for k in range(1, 5):
+        up = ringed(up, "z", 1)
+        weights = lax.dynamic_update_index_in_dim(weights, up, (place_z - k) % 8, 0)
+        if k < 4:
+            down = ringed(down, "z", -1)
+            weights = lax.dynamic_update_index_in_dim(weights, down, (place_z + k) % 8, 0)
+
     half_patch = lax.dynamic_index_in_dim(
         patch_weight.reshape(PCH, 4, 2, 64), side, 2, keepdims=False
     ).reshape(PCH, TOK)
-    patch_half = lax.all_gather(half_patch, "head", axis=0)
+    patch_half = sent_to_all(half_patch, "head")
     rows = jnp.concatenate([conv_input.reshape(PCOLS, CIN), pre_act.reshape(PCOLS, CMID)], axis=1)
-    slots = lax.all_gather(rows, WIDE, axis=0)
+    slots = sent_to_all(rows, WIDE)
     slot = pick_entry(slab_owner, device_index)
     my_rows = lax.dynamic_index_in_dim(slots, slot, 0, keepdims=False)
-    picture = lax.all_gather(my_rows, "head", axis=0).reshape(IMGTOK, CIN + CMID)
-    kernel_all = lax.all_gather(kernel_second.astype(bf16), WIDE, axis=0)
-    kernel_mine = lax.dynamic_slice_in_dim(
-        kernel_all.reshape(CMID, 9, PCH), head_index * 16, 16, 0
-    ).transpose(1, 0, 2)
+    picture = sent_to_all(my_rows, "head").reshape(IMGTOK, CIN + CMID)
+    turned = [(a * 8 + b, b * 8 + a) for a in range(8) for b in range(8)]
+    kernel_rows = lax.ppermute(kernel_second.astype(bf16), ("head", "z"), turned)
+    kernel_mine = sent_to_all(kernel_rows, ("yh", "yl")).reshape(16, 9, PCH).transpose(1, 0, 2)
 
     conv_img = picture[:, :CIN]
     pre_img = picture[:, CIN:].astype(f32)
@@ -382,7 +397,7 @@
 
     patch_part = pl.pallas_call(
         patch_kernel,
-        out_shape=spec_of((2, IMGTOK, PCH), bf16),
+        out_shape=spec_of((2 * IMGTOK, PCH), bf16),
         grid=(8,),
         in_specs=[
             weight_block,
@@ -390,16 +405,11 @@
             fixed(3, IMGTOK, TOK),
             pl.BlockSpec((1, PCH, TOK), lambda i: (i, 0, 0)),
         ],
-        out_specs=fixed(2, IMGTOK, PCH),
-        scratch_shapes=[pltpu.VMEM((2, IMGTOK, PCH), f32)],
+        out_specs=fixed(2 * IMGTOK, PCH),
+        scratch_shapes=[pltpu.VMEM((2 * IMGTOK, PCH), f32)],
     )(weights, *in_order(image_grads, image_other), patch_half)
     pieces = exchanged(
-        jnp.broadcast_to(patch_part, (8, 2, IMGTOK, PCH)).reshape(16, IMGTOK, PCH), ("head", "yl")
-    )
-
-    flags = jnp.stack([head_index.astype(jnp.int32), present.astype(jnp.int32)])
-    partial = on_chip(conv_kernel, spec_of((64, LANES), bf16), 5, scalars=1)(
-        flags, pieces, kernel_mine, slope, left
+        jnp.broadcast_to(patch_part[None], (8, 2 * IMGTOK, PCH)).reshape(16, IMGTOK, PCH), ("head", "yl")
     )
 
     halves = pl.pallas_call(
@@ -409,17 +419,27 @@
         in_specs=[weight_block, fixed(3, TOK, TOK), fixed(3, TOK, TOK)],
         out_specs=pl.BlockSpec((1, TOK, 2 * TOK), lambda i: (i, 0, 0)),
     )(weights, *in_order(grads, grads_other))
-    summed = jnp.sum(exchanged(halves, "head").astype(f32), axis=0).astype(bf16)
+    pieces, halves = lax.optimization_barrier((pieces, halves))
+    traded = exchanged(halves, "head")
+
+    flags = jnp.stack([head_index.astype(jnp.int32), present.astype(jnp.int32)])
+    partial = on_chip(conv_kernel, spec_of((64, LANES), bf16), 5, scalars=1)(
+        flags, pieces, kernel_mine, slope, left
+    )
+
+    owned = exchanged(partial.reshape(64, 7, 128), WIDE)
+    owned = jnp.sum(owned.astype(f32), axis=0)
+    squares = jnp.broadcast_to(jnp.sum(owned * owned), (1, 128))
+    squares = jnp.sum(sent_to_all(squares, WIDE), axis=0)
+
+    summed = jnp.sum(traded.astype(f32), axis=0).astype(bf16)
+    summed, squares = lax.optimization_barrier((summed, squares))
     mine, theirs = in_order(summed[:, :TOK], summed[:, TOK:])
     arrived = swapped(theirs)
     even, odd = in_order(mine, arrived)
     input_grad_t = jnp.stack([even.reshape(4, 64, TOK), odd.reshape(4, 64, TOK)], axis=1)
     input_grad_t = input_grad_t.reshape(512, TOK)
 
-    owned = exchanged(partial.reshape(64, 7, 128), WIDE)
-    owned = jnp.sum(owned.astype(f32), axis=0)
-    squares = jnp.broadcast_to(jnp.sum(owned * owned), (1, 128))
-    squares = jnp.sum(sent_to_all(squares, WIDE), axis=0)
     together = sent_to_all(jnp.concatenate([owned, squares], axis=0), "head")
     total = jnp.sum(together[:, 7, 0])
     columns = together[:, :7].reshape(8, LANES)

time: 353 us -> 307 us (0.87)
  blocking collectives: 161 us -> 36.6 us
  starting transfers between devices: 73.1 us -> 140 us
  between operations: 19.3 us -> 5.99 us
  local copies, waits for them, and re-layouts: 10.4 us -> 21.7 us
  waiting for transfers between devices: 40 us -> 47.1 us
  other arithmetic: 14.3 us -> 21 us
    all_gather x3 -> x0, blocking collectives: 146 us -> none  [the longest x1 55.6 us: shards(): kernel_all = lax.all_gather(kernel_second.astype(bf16), WIDE, axis=0)]
    ppermute x0 -> x8, starting transfers between devices: none -> 43.4 us  [the longest x7 37.6 us: ringed(): lax.ppermute(value, axis, [(i, (i + distance) % count) for i in range(cou...]
    all_to_all x4 -> x8, starting transfers between devices: 36.7 us -> 65.1 us  [exchanged(): return lax.all_to_all(pieces, axis, split_axis=0, concat_axis=0, tiled=True)]
    all_to_all x1 -> x2, blocking collectives: 14.8 us -> 36.6 us  [exchanged(): return lax.all_to_all(pieces, axis, split_axis=0, concat_axis=0, tiled=True)]
    dynamic_update_slice x0 -> x8, local copies, waits for them, and re-layouts: none -> 6.24 us  [the longest x4 3.12 us: shards(): weights = lax.dynamic_update_index_in_dim(weights, up, (place_z - k) % 8, 0)]
    all_to_all x4 -> x8, waiting for transfers between devices: 32.2 us -> 37.7 us  [exchanged(): return lax.all_to_all(pieces, axis, split_axis=0, concat_axis=0, tiled=True)]
    broadcast_in_dim x1 -> x6, local copies, waits for them, and re-layouts: 0.62 us -> 5.37 us  [sent_to_all(): jnp.broadcast_to(value, (lax.axis_size(axis), *value.shape))]
  transfers between devices with their start and end apart: 21 -> 31, of which waited for: 5 -> 5; matrix products, arithmetic and copies ran while one was open for 5% -> 11% of each run, Pallas kernels for 6% -> 9%
where the time goes in v2:
time: 307 us; the launch traced here: 304 us
  starting transfers between devices  140 us (46%)
  waiting for transfers between devices  47.1 us (15%)
  blocking collectives  36.6 us (12%)
  Pallas kernels  31.9 us (10%)
  local copies, waits for them, and re-layouts  21.7 us (7%)
  other arithmetic  21 us (7%)
  between operations  5.99 us (2%)
    all_to_all x8, starting transfers between devices, exchanged(): return lax.all_to_all(pieces, axis, split_axis=0, concat_axis=0, tiled=True)  65.1 us
    all_to_all x8, waiting for transfers between devices, exchanged(): return lax.all_to_all(pieces, axis, split_axis=0, concat_axis=0, tiled=True)  37.7 us
    ppermute x7, starting transfers between devices, ringed(): lax.ppermute(value, axis, [(i, (i + distance) % count) for i in range(cou...  37.6 us
    all_to_all x2, blocking collectives, exchanged(): return lax.all_to_all(pieces, axis, split_axis=0, concat_axis=0, tiled=True)  36.6 us
    ppermute x12, starting transfers between devices, passed_along(): return lax.ppermute(block, axis, route)  23.2 us
    ppermute x3, waiting for transfers between devices, swapped(): return lax.ppermute(value, 'yl', [(0, 1), (1, 0)])  9.36 us
    ppermute x3, starting transfers between devices, swapped(): return lax.ppermute(value, 'yl', [(0, 1), (1, 0)])  7.85 us
    pallas_call x1, Pallas kernels, shards(): pl.pallas_call(grad_kernel, out_shape=spec_of((8, TOK, 2 * TOK), bf16), g...  7.54 us
  transfers between devices with their start and end apart: 31, of which 5 were waited for; matrix products, arithmetic and copies ran while one was open for 11% of the time, Pallas kernels for 9%

profile of v2, /device:TPU:1, one launch (start us, length us, event | category | flops | bytes accessed | tf_op | source)
XLA Modules:
  0.0 303.9 jit_solution(3577563138261733274)
XLA Ops:
  0.7 1.7 broadcast_in_dim.106
  2.4 7.6 %all-to-all-start = ((bf16[4,3,64,256]{3,2,1,0:T(8,128)(2,1)}), bf16[4,3,64,256]{3,2,1,0:T(8,128)(2,1)S(1)}, u32[]{:S(2)}, u32[]{:S(2)}) async-start(bf16[4,3,64,256]{3,2,1,0:T(8,128)(2,1)} %broadcast_in_dim.106), calls=%async_computation | async-start | bytes 786432 | tf_op jit(solution)/shard_map/all_to_all | solution.py:259
  11.0 1.3 collective-permute-start.7
  13.3 4.0 %collective-permute-start.11 = (bf16[2,256,256]{2,1,0:T(8,128)(2,1)S(1)}, bf16[2,256,256]{2,1,0:T(8,128)(2,1)S(1)}, u32[]{:S(2)}, u32[]{:S(2)}) collective-permute-start(bf16[2,256,256]{2,1,0:T(8,128)(2,1)S(1)} %pad_maximum_fusion.1), channel_id=1, source_target_pairs={{0,1},{1,2},{2,3},{3,4},{4,5},{5,6},{6,7},{7,8},{8,9},{9,10},{10,1... | collective-permute-start | bytes 786440 | tf_op jit(solution)/shard_map/ppermute | solution.py:246
  18.1 5.8 %collective-permute-start.21 = (bf16[18,256]{1,0:T(8,128)(2,1)S(1)}, bf16[18,256]{1,0:T(8,128)(2,1)S(1)}, u32[]{:S(2)}, u32[]{:S(2)}) collective-permute-start(bf16[18,256]{1,0:T(8,128)(2,1)S(1)} %convert_element_type.14), channel_id=1, source_target_pairs={{0,0},{8,64},{16,128},{24,192},{32,256},{40,320},{48,384},{56,448}... | collective-permute-start | bytes 27656 | tf_op jit(solution)/shard_map/ppermute | solution.py:356
  23.9 1.3 select_reduce_fusion.5
  25.2 1.3 select_reduce_fusion.4
  29.3 2.7 collective-permute-start.12
  36.1 16.4 %all-to-all-start.5 = ((bf16[64,8,256]{2,1,0:T(8,128)(2,1)}), bf16[64,8,256]{2,1,0:T(8,128)(2,1)S(1)}, u32[]{:S(2)}, u32[]{:S(2)}) async-start(bf16[64,8,256]{2,1,0:T(8,128)(2,1)} %broadcast_in_dim.125), calls=%async_computation.5 | async-start | bytes 524288 | tf_op jit(solution)/shard_map/all_to_all | solution.py:259
  52.7 3.7 %collective-permute-start.13 = (bf16[2,256,256]{2,1,0:T(8,128)(2,1)S(1)}, bf16[2,256,256]{2,1,0:T(8,128)(2,1)}, u32[]{:S(2)}, u32[]{:S(2)}) collective-permute-start(bf16[2,256,256]{2,1,0:T(8,128)(2,1)S(1)} %collective-permute-done.12.b2), channel_id=1, source_target_pairs={{0,1},{1,2},{2,3},{3,4},{4,5},{5,6},{6,7},{7,8},{8,9},{9,10},{10,1... | collective-permute-start | bytes 786440 | tf_op jit(solution)/shard_map/ppermute | solution.py:246
  57.2 1.3 collective-permute-start.9
  58.5 5.4 %collective-permute-start = (bf16[4,3,64,256]{3,2,1,0:T(8,128)(2,1)S(1)}, bf16[4,3,64,256]{3,2,1,0:T(8,128)(2,1)}, u32[]{:S(2)}, u32[]{:S(2)}) collective-permute-start(bf16[4,3,64,256]{3,2,1,0:T(8,128)(2,1)S(1)} %all-to-all-done), channel_id=1, source_target_pairs={{0,8},{8,16},{16,24},{24,32},{32,40},{40,48},{48,56},{56,0},{1,9},... | collective-permute-start | bytes 1179656 | tf_op jit(solution)/shard_map/ppermute | solution.py:251
  63.9 3.4 %collective-permute-start.1 = (bf16[4,3,64,256]{3,2,1,0:T(8,128)(2,1)S(1)}, bf16[4,3,64,256]{3,2,1,0:T(8,128)(2,1)}, u32[]{:S(2)}, u32[]{:S(2)}) collective-permute-start(bf16[4,3,64,256]{3,2,1,0:T(8,128)(2,1)S(1)} %all-to-all-done), channel_id=1, source_target_pairs={{0,56},{8,0},{16,8},{24,16},{32,24},{40,32},{48,40},{56,48},{1,57}... | collective-permute-start | bytes 1179656 | tf_op jit(solution)/shard_map/ppermute | solution.py:251
  70.6 2.4 collective-permute-start.14
  73.7 5.3 %all-to-all-start.4 = ((bf16[8,18,256]{2,1,0:T(8,128)(2,1)}), bf16[8,18,256]{2,1,0:T(8,128)(2,1)}, u32[]{:S(2)}, u32[]{:S(2)}) async-start(bf16[8,18,256]{2,1,0:T(8,128)(2,1)} %broadcast_in_dim.124), calls=%async_computation.4 | async-start | bytes 196608 | tf_op jit(solution)/shard_map/all_to_all | solution.py:259
  79.0 1.3 collective-permute-start.10
  80.8 3.7 %shard_map.225.stats = f32[8,256]{1,0:T(8,128)} custom-call(s32[8,256]{1,0:T(8,128)} %add_subtract_fusion.meta, bf16[256,256]{1,0:T(8,128)(2,1)} %q.3, bf16[256,256]{1,0:T(8,128)(2,1)} %g.3, bf16[256,256]{1,0:T(8,128)(2,1)} %k0.5, bf16[256,256]{1,0:T(8,128)(2,1)} %v0.5, bf16[2,256,256]{2,1,0:T(8,128)(2,1)} %copy-done.2, bf16[2,256,256]{2,1,0:T(8,128)(2,1)} %copy-done.3, ...), custom_call_target="tpu_custom_call" | custom-call | tf_op jit(solution)/shard_map/pallas_call | solution.py:368
  85.7 1.3 collective-permute-start.16
  88.4 1.4 collective-permute-start.18
  90.8 5.2 %shard_map.226 = (bf16[256,256]{1,0:T(8,128)(2,1)}, f32[256,256]{1,0:T(8,128)}, f32[256,256]{1,0:T(8,128)}) custom-call(s32[8,256]{1,0:T(8,128)} %add_subtract_fusion.meta, f32[8,256]{1,0:T(8,128)} %shard_map.225.stats, bf16[256,256]{1,0:T(8,128)(2,1)} %q.3, bf16[256,256]{1,0:T(8,128)(2,1)} %g.3, bf16[256,256]{1,0:T(8,128)(2,1)} %k0.5, bf16[256,256]{1,0:T(8,128)(2,1)} %v0.5, ...), custom_call_target="tpu_custom_call" | custom-call | tf_op jit(solution)/shard_map/pallas_call | solution.py:375
  96.0 12.4 %collective-permute-start.2 = (bf16[4,3,64,256]{3,2,1,0:T(8,128)(2,1)}, bf16[4,3,64,256]{3,2,1,0:T(8,128)(2,1)}, u32[]{:S(2)}, u32[]{:S(2)}) collective-permute-start(bf16[4,3,64,256]{3,2,1,0:T(8,128)(2,1)} %collective-permute-done), channel_id=1, source_target_pairs={{0,8},{8,16},{16,24},{24,32},{32,40},{40,48},{48,56},{56,0},{1,9},... | collective-permute-start | bytes 1179656 | tf_op jit(solution)/shard_map/ppermute | solution.py:251
  108.4 8.1 %collective-permute-start.3 = (bf16[4,3,64,256]{3,2,1,0:T(8,128)(2,1)}, bf16[4,3,64,256]{3,2,1,0:T(8,128)(2,1)}, u32[]{:S(2)}, u32[]{:S(2)}) collective-permute-start(bf16[4,3,64,256]{3,2,1,0:T(8,128)(2,1)} %collective-permute-done.1), channel_id=1, source_target_pairs={{0,56},{8,0},{16,8},{24,16},{32,24},{40,32},{48,40},{56,48},{1,57}... | collective-permute-start | bytes 1179656 | tf_op jit(solution)/shard_map/ppermute | solution.py:251
  117.1 5.1 %shard_map.227 = (bf16[3,256,256]{2,1,0:T(8,128)(2,1)}, bf16[3,64,256]{2,1,0:T(8,128)(2,1)}) custom-call(s32[1]{0:T(128)} %bitcast.8.start, s32[8,256]{1,0:T(8,128)} %add_subtract_fusion.meta, bf16[256,256]{1,0:T(8,128)(2,1)} %k0.5, bf16[256,256]{1,0:T(8,128)(2,1)} %v0.5, bf16[2,256,256]{2,1,0:T(8,128)(2,1)} %copy-done.5, bf16[2,256,256]{2,1,0:T(8,128)(2,1)} %copy-done.6, ...), custom_call_target="tpu_custom_call" | custom-call | tf_op jit(solution)/shard_map/pallas_call | solution.py:380
  122.3 2.2 collective-permute-start.19
  125.5 2.3 collective-permute-done.19
  127.8 1.6 broadcast_select_fusion.6
  129.4 1.9 collective-permute-start.4
  131.4 4.6 %collective-permute-start.5 = (bf16[4,3,64,256]{3,2,1,0:T(8,128)(2,1)}, bf16[4,3,64,256]{3,2,1,0:T(8,128)(2,1)}, u32[]{:S(2)}, u32[]{:S(2)}) collective-permute-start(bf16[4,3,64,256]{3,2,1,0:T(8,128)(2,1)} %collective-permute-done.3), channel_id=1, source_target_pairs={{0,56},{8,0},{16,8},{24,16},{32,24},{40,32},{48,40},{56,48},{1,57}... | collective-permute-start | bytes 1179656 | tf_op jit(solution)/shard_map/ppermute | solution.py:251
  137.0 13.8 %all-to-all-start.1 = ((bf16[8,256,256]{2,1,0:T(8,128)(2,1)}), bf16[8,256,256]{2,1,0:T(8,128)(2,1)}, u32[]{:S(2)}, u32[]{:S(2)}) async-start(bf16[8,256,256]{2,1,0:T(8,128)(2,1)} %broadcast_in_dim.122), calls=%async_computation.1 | async-start | bytes 2097152 | tf_op jit(solution)/shard_map/all_to_all | solution.py:259
  152.9 1.9 collective-permute-start.6
  156.9 9.0 %all-to-all-done.1.pw = bf16[8,256,256]{2,1,0:T(8,128)(2,1)} async-done(((bf16[8,256,256]{2,1,0:T(8,128)(2,1)}), bf16[8,256,256]{2,1,0:T(8,128)(2,1)}, u32[]{:S(2)}, u32[]{:S(2)}) %all-to-all-start.1) | async-done | bytes 1048608 | tf_op jit(solution)/shard_map/all_to_all | solution.py:259
  166.5 4.8 %all-to-all-start.6 = ((bf16[8,8,256]{2,1,0:T(8,128)(2,1)}), bf16[8,8,256]{2,1,0:T(8,128)(2,1)}, u32[]{:S(2)}, u32[]{:S(2)}) async-start(bf16[8,8,256]{2,1,0:T(8,128)(2,1)} %broadcast_in_dim.126), calls=%async_computation.6 | async-start | bytes 65536 | tf_op jit(solution)/shard_map/all_to_all | solution.py:259
  171.4 1.6 copy-done
  173.0 7.1 %shard_map.228 = bf16[128,256]{1,0:T(8,128)(2,1)} custom-call(bf16[8,4,3,64,256]{4,3,2,1,0:T(8,128)(2,1)} %copy-done, bf16[3,64,256]{2,1,0:T(8,128)(2,1)} %get-tuple-element.36.g0, bf16[3,64,256]{2,1,0:T(8,128)(2,1)} %get-tuple-element.35.g1, bf16[8,256,256]{2,1,0:T(8,128)(2,1)} %all-to-all-done.1.pw), custom_call_target="tpu_custom_call" | custom-call | tf_op jit(solution)/shard_map/pallas_call | solution.py:398
  180.1 1.7 broadcast_in_dim.123
  181.8 4.8 %all-to-all-start.2 = ((bf16[16,64,256]{2,1,0:T(8,128)(2,1)}), bf16[16,64,256]{2,1,0:T(8,128)(2,1)S(1)}, u32[]{:S(2)}, u32[]{:S(2)}) async-start(bf16[16,64,256]{2,1,0:T(8,128)(2,1)} %bitcast.16), calls=%async_computation.2 | async-start | bytes 1048576 | tf_op jit(solution)/shard_map/all_to_all | solution.py:259
  190.3 3.4 %collective-permute-start.20 = (bf16[3,256,256]{2,1,0:T(8,128)(2,1)}, bf16[3,256,256]{2,1,0:T(8,128)(2,1)S(1)}, u32[]{:S(2)}, u32[]{:S(2)}) collective-permute-start(bf16[3,256,256]{2,1,0:T(8,128)(2,1)} %get-tuple-element.20), channel_id=1, source_target_pairs={{0,1},{1,0},{2,3},{3,2},{4,5},{5,4},{6,7},{7,6},{8,9},{9,8},{10,11... | collective-permute-start | bytes 1179656 | tf_op jit(solution)/shard_map/ppermute | solution.py:255
  195.9 7.0 %collective-permute-done.20 = bf16[3,256,256]{2,1,0:T(8,128)(2,1)S(1)} collective-permute-done((bf16[3,256,256]{2,1,0:T(8,128)(2,1)}, bf16[3,256,256]{2,1,0:T(8,128)(2,1)S(1)}, u32[]{:S(2)}, u32[]{:S(2)}) %collective-permute-start.20) | collective-permute-done | bytes 393248 | tf_op jit(solution)/shard_map/ppermute | solution.py:255
  203.0 1.9 broadcast_select_fusion
  204.9 7.5 %shard_map.229 = bf16[8,256,512]{2,1,0:T(8,128)(2,1)} custom-call(bf16[8,4,3,64,256]{4,3,2,1,0:T(8,128)(2,1)} %copy-done, bf16[3,256,256]{2,1,0:T(8,128)(2,1)} %get-tuple-element.32.g0, bf16[3,256,256]{2,1,0:T(8,128)(2,1)} %get-tuple-element.31.g1), custom_call_target="tpu_custom_call" | custom-call | tf_op jit(solution)/shard_map/pallas_call | solution.py:415
  213.3 3.3 %shard_map.230 = bf16[64,896]{1,0:T(8,128)(2,1)} custom-call(s32[2]{0:T(128)} %pad_add_fusion.scalars, bf16[16,64,256]{2,1,0:T(8,128)(2,1)} %copy-done.1, bf16[9,16,256]{2,1,0:T(8,128)(2,1)} %bitcast.68, f32[64,16]{1,0:T(8,128)} %fusion.1.slope, bf16[4,64,64]{2,1,0:T(8,128)(2,1)} %maximum_bitcast_fusion.left), custom_call_target="tpu_custom_call" | custom-call | tf_op jit(solution)/shard_map/pallas_call | solution.py:426
  217.6 21.9 %all_to_all.50 = bf16[64,7,128]{2,1,0:T(8,128)(2,1)S(1)} all-to-all(bf16[64,7,128]{2,1,0:T(8,128)(2,1)S(1)} %reshape.86), channel_id=1, replica_groups=mesh['head'=8,'z'=8,'yh'=4,'yl'=2] {'z','yh','yl'}, dimensions={0} | all-to-all | bytes 229376 | tf_op jit(solution)/shard_map/all_to_all | solution.py:259
  240.9 14.7 %all_to_all.51 = f32[64,1,128]{2,1,0:T(1,128)S(1)} all-to-all(f32[64,1,128]{2,1,0:T(1,128)S(1)} %broadcast_in_dim_broadcast_in_dim.3), channel_id=1, replica_groups=mesh['head'=8,'z'=8,'yh'=4,'yl'=2] {'z','yh','yl'}, dimensions={0} | all-to-all | bytes 65536 | tf_op jit(solution)/shard_map/all_to_all | solution.py:259
  255.6 8.1 %all-to-all-start.3 = ((bf16[8,256,512]{2,1,0:T(8,128)(2,1)}), bf16[8,256,512]{2,1,0:T(8,128)(2,1)S(1)}, u32[]{:S(2)}, u32[]{:S(2)}) async-start(bf16[8,256,512]{2,1,0:T(8,128)(2,1)} %shard_map.229), calls=%async_computation.3 | async-start | bytes 4194304 | tf_op jit(solution)/shard_map/all_to_all | solution.py:259
  263.8 26.2 %all-to-all-done.3 = bf16[8,256,512]{2,1,0:T(8,128)(2,1)S(1)} async-done(((bf16[8,256,512]{2,1,0:T(8,128)(2,1)}), bf16[8,256,512]{2,1,0:T(8,128)(2,1)S(1)}, u32[]{:S(2)}, u32[]{:S(2)}) %all-to-all-start.3) | async-done | bytes 2097184 | tf_op jit(solution)/shard_map/all_to_all | solution.py:259
  291.0 4.2 %all-to-all-start.9 = ((f32[8,8,128]{2,1,0:T(8,128)}), f32[8,8,128]{2,1,0:T(8,128)S(1)}, u32[]{:S(2)}, u32[]{:S(2)}) async-start(f32[8,8,128]{2,1,0:T(8,128)} %broadcast_in_dim.127), calls=%async_computation.9 | async-start | bytes 65536 | tf_op jit(solution)/shard_map/all_to_all | solution.py:259
  295.2 2.2 collective-permute-start.22
  297.5 2.5 all-to-all-done.9
  (129 shorter events, 35.5 us)
Async XLA Ops:
  0.6 56.4 %copy-start.7 = (bf16[256,512]{1,0:T(8,128)(2,1)S(1)}, bf16[256,512]{1,0:T(8,128)(2,1)}, u32[]{:S(2)}) copy-start(bf16[256,512]{1,0:T(8,128)(2,1)} %param.27) | copy-start | bytes 786436
  0.6 66.6 %copy-start.16 = (s32[64]{0:T(128)S(1)}, s32[64]{0:T(128)}, u32[]{:S(2)}) copy-start(s32[64]{0:T(128)} %param.26) | copy-start | bytes 772
  2.4 32.9 %all-to-all-start = ((bf16[4,3,64,256]{3,2,1,0:T(8,128)(2,1)}), bf16[4,3,64,256]{3,2,1,0:T(8,128)(2,1)S(1)}, u32[]{:S(2)}, u32[]{:S(2)}) async-start(bf16[4,3,64,256]{3,2,1,0:T(8,128)(2,1)} %broadcast_in_dim.106), calls=%async_computation | async-start | bytes 786432 | tf_op jit(solution)/shard_map/all_to_all | solution.py:259
  11.0 23.0 %collective-permute-start.7 = (bf16[2,256,256]{2,1,0:T(8,128)(2,1)S(1)}, bf16[2,256,256]{2,1,0:T(8,128)(2,1)S(1)}, u32[]{:S(2)}, u32[]{:S(2)}) collective-permute-start(bf16[2,256,256]{2,1,0:T(8,128)(2,1)S(1)} %pad_maximum_fusion), channel_id=1, source_target_pairs={{1,0},{2,1},{3,2},{4,3},{5,4},{6,5},{7,6},{8,7},{9,8},{10,9},{11,1... | collective-permute-start | bytes 786440 | tf_op jit(solution)/shard_map/ppermute | solution.py:246
  13.3 16.0 %collective-permute-start.11 = (bf16[2,256,256]{2,1,0:T(8,128)(2,1)S(1)}, bf16[2,256,256]{2,1,0:T(8,128)(2,1)S(1)}, u32[]{:S(2)}, u32[]{:S(2)}) collective-permute-start(bf16[2,256,256]{2,1,0:T(8,128)(2,1)S(1)} %pad_maximum_fusion.1), channel_id=1, source_target_pairs={{0,1},{1,2},{2,3},{3,4},{4,5},{5,6},{6,7},{7,8},{8,9},{9,10},{10,1... | collective-permute-start | bytes 786440 | tf_op jit(solution)/shard_map/ppermute | solution.py:246
  18.1 55.0 %collective-permute-start.21 = (bf16[18,256]{1,0:T(8,128)(2,1)S(1)}, bf16[18,256]{1,0:T(8,128)(2,1)S(1)}, u32[]{:S(2)}, u32[]{:S(2)}) collective-permute-start(bf16[18,256]{1,0:T(8,128)(2,1)S(1)} %convert_element_type.14), channel_id=1, source_target_pairs={{0,0},{8,64},{16,128},{24,192},{32,256},{40,320},{48,384},{56,448}... | collective-permute-start | bytes 27656 | tf_op jit(solution)/shard_map/ppermute | solution.py:356
  29.3 49.7 %copy-start.2 = (bf16[2,256,256]{2,1,0:T(8,128)(2,1)}, bf16[2,256,256]{2,1,0:T(8,128)(2,1)S(1)}, u32[]{:S(2)}) copy-start(bf16[2,256,256]{2,1,0:T(8,128)(2,1)S(1)} %collective-permute-done.11.b1) | copy-start | bytes 786436
  29.3 23.4 %collective-permute-start.12 = (bf16[2,256,256]{2,1,0:T(8,128)(2,1)S(1)}, bf16[2,256,256]{2,1,0:T(8,128)(2,1)S(1)}, u32[]{:S(2)}, u32[]{:S(2)}) collective-permute-start(bf16[2,256,256]{2,1,0:T(8,128)(2,1)S(1)} %collective-permute-done.11.b1), channel_id=1, source_target_pairs={{0,1},{1,2},{2,3},{3,4},{4,5},{5,6},{6,7},{7,8},{8,9},{9,10},{10,1... | collective-permute-start | bytes 786440 | tf_op jit(solution)/shard_map/ppermute | solution.py:246
  34.0 45.0 %copy-start.5 = (bf16[2,256,256]{2,1,0:T(8,128)(2,1)}, bf16[2,256,256]{2,1,0:T(8,128)(2,1)S(1)}, u32[]{:S(2)}) copy-start(bf16[2,256,256]{2,1,0:T(8,128)(2,1)S(1)} %collective-permute-done.7.a1) | copy-start | bytes 786436
  34.0 23.1 %collective-permute-start.8 = (bf16[2,256,256]{2,1,0:T(8,128)(2,1)S(1)}, bf16[2,256,256]{2,1,0:T(8,128)(2,1)S(1)}, u32[]{:S(2)}, u32[]{:S(2)}) collective-permute-start(bf16[2,256,256]{2,1,0:T(8,128)(2,1)S(1)} %collective-permute-done.7.a1), channel_id=1, source_target_pairs={{1,0},{2,1},{3,2},{4,3},{5,4},{6,5},{7,6},{8,7},{9,8},{10,9},{11,1... | collective-permute-start | bytes 786440 | tf_op jit(solution)/shard_map/ppermute | solution.py:246
  36.1 37.0 %all-to-all-start.5 = ((bf16[64,8,256]{2,1,0:T(8,128)(2,1)}), bf16[64,8,256]{2,1,0:T(8,128)(2,1)S(1)}, u32[]{:S(2)}, u32[]{:S(2)}) async-start(bf16[64,8,256]{2,1,0:T(8,128)(2,1)} %broadcast_in_dim.125), calls=%async_computation.5 | async-start | bytes 524288 | tf_op jit(solution)/shard_map/all_to_all | solution.py:259
  52.7 26.4 %copy-start.3 = (bf16[2,256,256]{2,1,0:T(8,128)(2,1)}, bf16[2,256,256]{2,1,0:T(8,128)(2,1)S(1)}, u32[]{:S(2)}) copy-start(bf16[2,256,256]{2,1,0:T(8,128)(2,1)S(1)} %collective-permute-done.12.b2) | copy-start | bytes 786436
  52.7 17.9 %collective-permute-start.13 = (bf16[2,256,256]{2,1,0:T(8,128)(2,1)S(1)}, bf16[2,256,256]{2,1,0:T(8,128)(2,1)}, u32[]{:S(2)}, u32[]{:S(2)}) collective-permute-start(bf16[2,256,256]{2,1,0:T(8,128)(2,1)S(1)} %collective-permute-done.12.b2), channel_id=1, source_target_pairs={{0,1},{1,2},{2,3},{3,4},{4,5},{5,6},{6,7},{7,8},{8,9},{9,10},{10,1... | collective-permute-start | bytes 786440 | tf_op jit(solution)/shard_map/ppermute | solution.py:246
  57.2 21.9 %copy-start.6 = (bf16[2,256,256]{2,1,0:T(8,128)(2,1)}, bf16[2,256,256]{2,1,0:T(8,128)(2,1)S(1)}, u32[]{:S(2)}) copy-start(bf16[2,256,256]{2,1,0:T(8,128)(2,1)S(1)} %collective-permute-done.8.a2) | copy-start | bytes 786436
  57.2 21.8 %collective-permute-start.9 = (bf16[2,256,256]{2,1,0:T(8,128)(2,1)S(1)}, bf16[2,256,256]{2,1,0:T(8,128)(2,1)}, u32[]{:S(2)}, u32[]{:S(2)}) collective-permute-start(bf16[2,256,256]{2,1,0:T(8,128)(2,1)S(1)} %collective-permute-done.8.a2), channel_id=1, source_target_pairs={{1,0},{2,1},{3,2},{4,3},{5,4},{6,5},{7,6},{8,7},{9,8},{10,9},{11,1... | collective-permute-start | bytes 786440 | tf_op jit(solution)/shard_map/ppermute | solution.py:246
  58.5 28.6 %collective-permute-start = (bf16[4,3,64,256]{3,2,1,0:T(8,128)(2,1)S(1)}, bf16[4,3,64,256]{3,2,1,0:T(8,128)(2,1)}, u32[]{:S(2)}, u32[]{:S(2)}) collective-permute-start(bf16[4,3,64,256]{3,2,1,0:T(8,128)(2,1)S(1)} %all-to-all-done), channel_id=1, source_target_pairs={{0,8},{8,16},{16,24},{24,32},{32,40},{40,48},{48,56},{56,0},{1,9},... | collective-permute-start | bytes 1179656 | tf_op jit(solution)/shard_map/ppermute | solution.py:251
  63.9 24.5 %collective-permute-start.1 = (bf16[4,3,64,256]{3,2,1,0:T(8,128)(2,1)S(1)}, bf16[4,3,64,256]{3,2,1,0:T(8,128)(2,1)}, u32[]{:S(2)}, u32[]{:S(2)}) collective-permute-start(bf16[4,3,64,256]{3,2,1,0:T(8,128)(2,1)S(1)} %all-to-all-done), channel_id=1, source_target_pairs={{0,56},{8,0},{16,8},{24,16},{32,24},{40,32},{48,40},{56,48},{1,57}... | collective-permute-start | bytes 1179656 | tf_op jit(solution)/shard_map/ppermute | solution.py:251
  70.6 10.1 %collective-permute-start.14 = (bf16[2,256,256]{2,1,0:T(8,128)(2,1)}, bf16[2,256,256]{2,1,0:T(8,128)(2,1)}, u32[]{:S(2)}, u32[]{:S(2)}) collective-permute-start(bf16[2,256,256]{2,1,0:T(8,128)(2,1)} %collective-permute-done.13.b3), channel_id=1, source_target_pairs={{0,1},{1,2},{2,3},{3,4},{4,5},{5,6},{6,7},{7,8},{8,9},{9,10},{10,1... | collective-permute-start | bytes 786440 | tf_op jit(solution)/shard_map/ppermute | solution.py:246
  73.7 62.2 %all-to-all-start.4 = ((bf16[8,18,256]{2,1,0:T(8,128)(2,1)}), bf16[8,18,256]{2,1,0:T(8,128)(2,1)}, u32[]{:S(2)}, u32[]{:S(2)}) async-start(bf16[8,18,256]{2,1,0:T(8,128)(2,1)} %broadcast_in_dim.124), calls=%async_computation.4 | async-start | bytes 196608 | tf_op jit(solution)/shard_map/all_to_all | solution.py:259
  79.0 17.0 %collective-permute-start.10 = (bf16[2,256,256]{2,1,0:T(8,128)(2,1)}, bf16[2,256,256]{2,1,0:T(8,128)(2,1)}, u32[]{:S(2)}, u32[]{:S(2)}) collective-permute-start(bf16[2,256,256]{2,1,0:T(8,128)(2,1)} %collective-permute-done.9.a3), channel_id=1, source_target_pairs={{1,0},{2,1},{3,2},{4,3},{5,4},{6,5},{7,6},{8,7},{9,8},{10,9},{11,1... | collective-permute-start | bytes 786440 | tf_op jit(solution)/shard_map/ppermute | solution.py:246
  84.5 24.0 %collective-permute-start.15 = (f32[8,256]{1,0:T(8,128)}, f32[8,256]{1,0:T(8,128)S(1)}, u32[]{:S(2)}, u32[]{:S(2)}) collective-permute-start(f32[8,256]{1,0:T(8,128)} %shard_map.225.stats), channel_id=1, source_target_pairs={{1,0},{2,1},{3,2},{4,3},{5,4},{6,5},{7,6},{8,7},{9,8},{10,9},{11,1... | collective-permute-start | bytes 24584 | tf_op jit(solution)/shard_map/ppermute | solution.py:246
  85.7 30.8 %collective-permute-start.16 = (f32[8,256]{1,0:T(8,128)}, f32[8,256]{1,0:T(8,128)}, u32[]{:S(2)}, u32[]{:S(2)}) collective-permute-start(f32[8,256]{1,0:T(8,128)} %shard_map.225.stats), channel_id=1, source_target_pairs={{2,0},{3,1},{4,2},{5,3},{6,4},{7,5},{8,6},{9,7},{10,8},{11,9},{12,... | collective-permute-start | bytes 24584 | tf_op jit(solution)/shard_map/ppermute | solution.py:246
  87.1 29.5 %collective-permute-start.17 = (f32[8,256]{1,0:T(8,128)}, f32[8,256]{1,0:T(8,128)}, u32[]{:S(2)}, u32[]{:S(2)}) collective-permute-start(f32[8,256]{1,0:T(8,128)} %shard_map.225.stats), channel_id=1, source_target_pairs={{3,0},{4,1},{5,2},{6,3},{7,4},{8,5},{9,6},{10,7},{11,8},{12,9},{13... | collective-permute-start | bytes 24584 | tf_op jit(solution)/shard_map/ppermute | solution.py:246
  88.4 47.6 %copy-start.4 = (bf16[256,256]{1,0:T(8,128)(2,1)S(1)}, bf16[256,256]{1,0:T(8,128)(2,1)}, u32[]{:S(2)}) copy-start(bf16[256,256]{1,0:T(8,128)(2,1)} %copy.62) | copy-start | bytes 393220
  88.4 28.2 %collective-permute-start.18 = (f32[8,256]{1,0:T(8,128)}, f32[8,256]{1,0:T(8,128)S(1)}, u32[]{:S(2)}, u32[]{:S(2)}) collective-permute-start(f32[8,256]{1,0:T(8,128)} %shard_map.225.stats), channel_id=1, source_target_pairs={{4,0},{5,1},{6,2},{7,3},{8,4},{9,5},{10,6},{11,7},{12,8},{13,9},{1... | collective-permute-start | bytes 24584 | tf_op jit(solution)/shard_map/ppermute | solution.py:246
  96.0 33.4 %collective-permute-start.2 = (bf16[4,3,64,256]{3,2,1,0:T(8,128)(2,1)}, bf16[4,3,64,256]{3,2,1,0:T(8,128)(2,1)}, u32[]{:S(2)}, u32[]{:S(2)}) collective-permute-start(bf16[4,3,64,256]{3,2,1,0:T(8,128)(2,1)} %collective-permute-done), channel_id=1, source_target_pairs={{0,8},{8,16},{16,24},{24,32},{32,40},{40,48},{48,56},{56,0},{1,9},... | collective-permute-start | bytes 1179656 | tf_op jit(solution)/shard_map/ppermute | solution.py:251
  108.4 8.1 %copy-start.14 = (f32[8,256]{1,0:T(8,128)}, f32[8,256]{1,0:T(8,128)S(1)}, u32[]{:S(2)}) copy-start(f32[8,256]{1,0:T(8,128)S(1)} %collective-permute-done.15.s1) | copy-start | bytes 24580
  108.4 22.9 %collective-permute-start.3 = (bf16[4,3,64,256]{3,2,1,0:T(8,128)(2,1)}, bf16[4,3,64,256]{3,2,1,0:T(8,128)(2,1)}, u32[]{:S(2)}, u32[]{:S(2)}) collective-permute-start(bf16[4,3,64,256]{3,2,1,0:T(8,128)(2,1)} %collective-permute-done.1), channel_id=1, source_target_pairs={{0,56},{8,0},{16,8},{24,16},{32,24},{40,32},{48,40},{56,48},{1,57}... | collective-permute-start | bytes 1179656 | tf_op jit(solution)/shard_map/ppermute | solution.py:251
  116.5 0.6 copy-start.15
  122.3 5.6 %collective-permute-start.19 = (bf16[3,64,256]{2,1,0:T(8,128)(2,1)}, bf16[3,64,256]{2,1,0:T(8,128)(2,1)S(1)}, u32[]{:S(2)}, u32[]{:S(2)}) collective-permute-start(bf16[3,64,256]{2,1,0:T(8,128)(2,1)} %get-tuple-element.19), channel_id=1, source_target_pairs={{0,1},{1,0},{2,3},{3,2},{4,5},{5,4},{6,7},{7,6},{8,9},{9,8},{10,11... | collective-permute-start | bytes 294920 | tf_op jit(solution)/shard_map/ppermute | solution.py:255
  129.4 23.5 %collective-permute-start.4 = (bf16[4,3,64,256]{3,2,1,0:T(8,128)(2,1)}, bf16[4,3,64,256]{3,2,1,0:T(8,128)(2,1)}, u32[]{:S(2)}, u32[]{:S(2)}) collective-permute-start(bf16[4,3,64,256]{3,2,1,0:T(8,128)(2,1)} %collective-permute-done.2), channel_id=1, source_target_pairs={{0,8},{8,16},{16,24},{24,32},{32,40},{40,48},{48,56},{56,0},{1,9},... | collective-permute-start | bytes 1179656 | tf_op jit(solution)/shard_map/ppermute | solution.py:251
  131.4 24.5 %collective-permute-start.5 = (bf16[4,3,64,256]{3,2,1,0:T(8,128)(2,1)}, bf16[4,3,64,256]{3,2,1,0:T(8,128)(2,1)}, u32[]{:S(2)}, u32[]{:S(2)}) collective-permute-start(bf16[4,3,64,256]{3,2,1,0:T(8,128)(2,1)} %collective-permute-done.3), channel_id=1, source_target_pairs={{0,56},{8,0},{16,8},{24,16},{32,24},{40,32},{48,40},{56,48},{1,57}... | collective-permute-start | bytes 1179656 | tf_op jit(solution)/shard_map/ppermute | solution.py:251
  137.0 28.9 %all-to-all-start.1 = ((bf16[8,256,256]{2,1,0:T(8,128)(2,1)}), bf16[8,256,256]{2,1,0:T(8,128)(2,1)}, u32[]{:S(2)}, u32[]{:S(2)}) async-start(bf16[8,256,256]{2,1,0:T(8,128)(2,1)} %broadcast_in_dim.122), calls=%async_computation.1 | async-start | bytes 2097152 | tf_op jit(solution)/shard_map/all_to_all | solution.py:259
  152.9 18.4 %collective-permute-start.6 = (bf16[4,3,64,256]{3,2,1,0:T(8,128)(2,1)}, bf16[4,3,64,256]{3,2,1,0:T(8,128)(2,1)S(1)}, u32[]{:S(2)}, u32[]{:S(2)}) collective-permute-start(bf16[4,3,64,256]{3,2,1,0:T(8,128)(2,1)} %collective-permute-done.4), channel_id=1, source_target_pairs={{0,8},{8,16},{16,24},{24,32},{32,40},{40,48},{48,56},{56,0},{1,9},... | collective-permute-start | bytes 1179656 | tf_op jit(solution)/shard_map/ppermute | solution.py:251
  166.5 13.6 %all-to-all-start.6 = ((bf16[8,8,256]{2,1,0:T(8,128)(2,1)}), bf16[8,8,256]{2,1,0:T(8,128)(2,1)}, u32[]{:S(2)}, u32[]{:S(2)}) async-start(bf16[8,8,256]{2,1,0:T(8,128)(2,1)} %broadcast_in_dim.126), calls=%async_computation.6 | async-start | bytes 65536 | tf_op jit(solution)/shard_map/all_to_all | solution.py:259
  171.3 1.6 copy-start
  181.8 30.7 %all-to-all-start.2 = ((bf16[16,64,256]{2,1,0:T(8,128)(2,1)}), bf16[16,64,256]{2,1,0:T(8,128)(2,1)S(1)}, u32[]{:S(2)}, u32[]{:S(2)}) async-start(bf16[16,64,256]{2,1,0:T(8,128)(2,1)} %bitcast.16), calls=%async_computation.2 | async-start | bytes 1048576 | tf_op jit(solution)/shard_map/all_to_all | solution.py:259
  190.3 12.7 %collective-permute-start.20 = (bf16[3,256,256]{2,1,0:T(8,128)(2,1)}, bf16[3,256,256]{2,1,0:T(8,128)(2,1)S(1)}, u32[]{:S(2)}, u32[]{:S(2)}) collective-permute-start(bf16[3,256,256]{2,1,0:T(8,128)(2,1)} %get-tuple-element.20), channel_id=1, source_target_pairs={{0,1},{1,0},{2,3},{3,2},{4,5},{5,4},{6,7},{7,6},{8,9},{9,8},{10,11... | collective-permute-start | bytes 1179656 | tf_op jit(solution)/shard_map/ppermute | solution.py:255
  212.4 0.8 copy-start.1
  255.6 46.3 %copy-start.8 = (f32[18,256]{1,0:T(8,128)S(1)}, f32[18,256]{1,0:T(8,128)}, u32[]{:S(2)}) copy-start(f32[18,256]{1,0:T(8,128)} %param.31) | copy-start | bytes 55300
  255.6 46.3 %copy-start.9 = (f32[18,256]{1,0:T(8,128)S(1)}, f32[18,256]{1,0:T(8,128)}, u32[]{:S(2)}) copy-start(f32[18,256]{1,0:T(8,128)} %param.33) | copy-start | bytes 55300
  255.6 46.3 %copy-start.10 = (f32[18,256]{1,0:T(8,128)S(1)}, f32[18,256]{1,0:T(8,128)}, u32[]{:S(2)}) copy-start(f32[18,256]{1,0:T(8,128)} %param.35) | copy-start | bytes 55300
  255.6 46.9 %copy-start.11 = (f32[18,128]{1,0:T(8,128)S(1)}, f32[18,128]{1,0:T(8,128)}, u32[]{:S(2)}) copy-start(f32[18,128]{1,0:T(8,128)} %param.30) | copy-start | bytes 27652
  255.6 46.9 %copy-start.12 = (f32[18,128]{1,0:T(8,128)S(1)}, f32[18,128]{1,0:T(8,128)}, u32[]{:S(2)}) copy-start(f32[18,128]{1,0:T(8,128)} %param.32) | copy-start | bytes 27652
  255.6 46.9 %copy-start.13 = (f32[18,128]{1,0:T(8,128)S(1)}, f32[18,128]{1,0:T(8,128)}, u32[]{:S(2)}) copy-start(f32[18,128]{1,0:T(8,128)} %param.34) | copy-start | bytes 27652
  255.6 34.3 %all-to-all-start.3 = ((bf16[8,256,512]{2,1,0:T(8,128)(2,1)}), bf16[8,256,512]{2,1,0:T(8,128)(2,1)S(1)}, u32[]{:S(2)}, u32[]{:S(2)}) async-start(bf16[8,256,512]{2,1,0:T(8,128)(2,1)} %shard_map.229), calls=%async_computation.3 | async-start | bytes 4194304 | tf_op jit(solution)/shard_map/all_to_all | solution.py:259
  291.0 9.0 %all-to-all-start.9 = ((f32[8,8,128]{2,1,0:T(8,128)}), f32[8,8,128]{2,1,0:T(8,128)S(1)}, u32[]{:S(2)}, u32[]{:S(2)}) async-start(f32[8,8,128]{2,1,0:T(8,128)} %broadcast_in_dim.127), calls=%async_computation.9 | async-start | bytes 65536 | tf_op jit(solution)/shard_map/all_to_all | solution.py:259
  295.2 7.9 %collective-permute-start.22 = (bf16[256,256]{1,0:T(8,128)(2,1)S(1)}, bf16[256,256]{1,0:T(8,128)(2,1)S(1)}, u32[]{:S(2)}, u32[]{:S(2)}) collective-permute-start(bf16[256,256]{1,0:T(8,128)(2,1)S(1)} %broadcast_select_fusion.4), channel_id=1, source_target_pairs={{0,1},{1,0},{2,3},{3,2},{4,5},{5,4},{6,7},{7,6},{8,9},{9,8},{10,11... | collective-permute-start | bytes 393224 | tf_op jit(solution)/shard_map/ppermute | solution.py:255

commit v3 on v1

--- a/solution.py
+++ b/solution.py
@@ -17,7 +17,8 @@
 CIN = 128
 IMGTOK = 64
 TOK = 256
-WIDE = ("z", "yh", "yl")
+TALL = ("yh", "yl")
+WIDE = ("z", *TALL)
 LANES = 896
 
 neg_big = -1e30
@@ -150,30 +151,40 @@
         image[n] = nn(pick, out[n]).astype(bf16)
 
 
-def patch_kernel(w, g0, g1, pw, out, acc):
+def paired(flags, own, other):
+    first = flags[0] == 0
+    return jnp.where(first, own, other), jnp.where(first, other, own)
+
+
+def patch_kernel(flags, w, own, other, pw, out, acc):
     step = pl.program_id(0)
 
     @pl.when(step == 0)
     def _():
         acc[...] = jnp.zeros_like(acc)
 
-    for n, g in enumerate((g0, g1)):
-        t = jnp.zeros((IMGTOK, TOK), f32)
+    for n in range(2):
+        t = jnp.zeros((2 * IMGTOK, TOK), f32)
         for p in range(3):
-            t = t + nt(g[p], w[0, :, p].reshape(TOK, TOK))
-        acc[n] = acc[n] + nt(t.astype(bf16), pw[0])
+            both = jnp.concatenate(paired(flags, own[p], other[p]), axis=0)
+            t = t + nt(both, w[n, :, p].reshape(TOK, TOK))
+        acc[...] = acc[...] + nt(t.astype(bf16), pw[n, :PCH])
 
     @pl.when(step == pl.num_programs(0) - 1)
     def _():
-        out[...] = acc[...].astype(bf16)
-
-
-def grad_kernel(w, g0, g1, out):
-    for n, g in enumerate((g0, g1)):
-        t = jnp.zeros((TOK, TOK), f32)
-        for p in range(3):
-            t = t + nt(w[0, :, p].reshape(TOK, TOK), g[p])
-        out[0, :, n * TOK : (n + 1) * TOK] = t.astype(bf16)
+        total = acc[...].astype(bf16)
+        for n in range(8):
+            out[n] = total
+
+
+def grad_kernel(flags, w, own, other, mine, theirs):
+    core = flags[1]
+    for m, out in ((core, mine), (1 - core, theirs)):
+        for n in range(2):
+            t = jnp.zeros((TOK, TOK), f32)
+            for p in range(3):
+                t = t + nt(w[m, :, p].reshape(TOK, TOK), paired(flags, own[p], other[p])[n])
+            out[0, :, n * TOK : (n + 1) * TOK] = t.astype(bf16)
 
 
 def conv_kernel(scalars, pieces, k2, slope, left, out):
@@ -215,7 +226,8 @@
     for n in range(4):
         part = jnp.where((lane >= ends[n]) & (lane < ends[n + 1]), moved, zero)
         result = result + nn(left[n], part)
-    out[...] = result.astype(bf16)
+    for n in range(7):
+        out[:, n, :] = result[:, n * 128 : (n + 1) * 128].astype(bf16)
 
 
 def whole(space=None):
@@ -250,12 +262,20 @@
     return lax.ppermute(value, "yl", [(0, 1), (1, 0)])
 
 
+def once_here(value, reached):
+    return lax.optimization_barrier((value, reached))[0]
+
+
 def exchanged(pieces, axis):
     return lax.all_to_all(pieces, axis, split_axis=0, concat_axis=0, tiled=True)
 
 
 def sent_to_all(value, axis):
     return exchanged(jnp.broadcast_to(value, (lax.axis_size(axis), *value.shape)), axis)
+
+
+def summed_low(pieces):
+    return jnp.sum(pieces.astype(f32), axis=0).astype(bf16)
 
 
 def adam_update(param, mean, square, grad):
@@ -318,28 +338,47 @@
     before = jnp.stack([keys, values])
     after = jnp.stack([queries, out_grad])
     earlier, later = [], []
-    for _ in range(REACH):
+    meta, present, offset = seen_range(device_index, doc_lengths, image_count, image_offset)
+    for hop in range(REACH):
         before = passed_along(before, WIDE, 1)
         after = passed_along(after, WIDE, -1)
+        if hop == REACH - 2:
+            before, after, meta = lax.optimization_barrier((before, after, meta))
+        else:
+            before, after = lax.optimization_barrier((before, after))
         earlier.append(before)
         later.append(after)
 
-    meta, present, offset = seen_range(device_index, doc_lengths, image_count, image_offset)
-
-    weights = lax.all_gather(qkv_weight, ("z", "yh"), axis=0).reshape(8, 4, 3, 64, TOK)
+    stats = on_chip(
+        stats_kernel,
+        spec_of((8, TOK), f32),
+        9,
+        [pltpu.VMEM((REACH + 1, TOK, TOK), f32)],
+    )(meta, queries, out_grad, keys, values, *earlier)
+
+    quad = once_here(sent_to_all(qkv_weight, "yh"), earlier[0])
+    weights = lax.all_gather(quad, "z", axis=0)
+    slot_rows = jnp.concatenate(
+        [conv_input.reshape(PCOLS, CIN), pre_act.reshape(PCOLS, CMID)], axis=1
+    )
+    slot_rows = jnp.concatenate([slot_rows, kernel_second.astype(bf16)], axis=0)
+    along_z = sent_to_all(once_here(slot_rows, earlier[1]), "z")
+    kernel_rows = lax.dynamic_index_in_dim(along_z[:, PCOLS:], head_index, 0, keepdims=False)
+    slot_rows = along_z[:, :PCOLS].reshape(64, PCH)
+    along_y = jnp.concatenate([slot_rows, kernel_rows], axis=0)
+    along_y = sent_to_all(once_here(along_y, earlier[2]), TALL)
+    along_y = once_here(along_y, stats)
+    kernel_mine = along_y[:, 64:].reshape(16, 9, PCH).transpose(1, 0, 2)
+    slot = pick_entry(slab_owner, device_index)
+    my_rows = along_y[:, :64].reshape(8, 8, PCOLS, PCH)
+    my_rows = lax.dynamic_slice(
+        my_rows, (slot % 8, slot // 8, 0, 0), (1, 1, PCOLS, PCH)
+    ).reshape(PCOLS, PCH)
     half_patch = lax.dynamic_index_in_dim(
         patch_weight.reshape(PCH, 4, 2, 64), side, 2, keepdims=False
     ).reshape(PCH, TOK)
-    patch_half = lax.all_gather(half_patch, "head", axis=0)
-    rows = jnp.concatenate([conv_input.reshape(PCOLS, CIN), pre_act.reshape(PCOLS, CMID)], axis=1)
-    slots = lax.all_gather(rows, WIDE, axis=0)
-    slot = pick_entry(slab_owner, device_index)
-    my_rows = lax.dynamic_index_in_dim(slots, slot, 0, keepdims=False)
-    picture = lax.all_gather(my_rows, "head", axis=0).reshape(IMGTOK, CIN + CMID)
-    kernel_all = lax.all_gather(kernel_second.astype(bf16), WIDE, axis=0)
-    kernel_mine = lax.dynamic_slice_in_dim(
-        kernel_all.reshape(CMID, 9, PCH), head_index * 16, 16, 0
-    ).transpose(1, 0, 2)
+    along_head = sent_to_all(jnp.concatenate([half_patch, my_rows], axis=0), "head")
+    picture = along_head[:, PCH:].reshape(IMGTOK, CIN + CMID)
 
     conv_img = picture[:, :CIN]
     pre_img = picture[:, CIN:].astype(f32)
@@ -350,12 +389,6 @@
     slope = sig * (1.0 + pre_img * (1.0 - sig))
     slope = lax.dynamic_slice_in_dim(slope, head_index * 16, 16, 1)
 
-    stats = on_chip(
-        stats_kernel,
-        spec_of((8, TOK), f32),
-        9,
-        [pltpu.VMEM((REACH + 1, TOK, TOK), f32)],
-    )(meta, queries, out_grad, keys, values, *earlier)
     stats_later = [passed_along(stats, WIDE, -d) for d in range(1, REACH + 1)]
     dq, dk, dv = on_chip(
         own_kernel,
@@ -370,56 +403,79 @@
     )(offset[None], meta, keys, values, *later, *stats_later, dq, dk, dv)
 
     image_other = swapped(image_grads)
-    grads_other = swapped(grads)
+    grads_other = swapped(once_here(grads, image_other))
+    core = head_index % 2
+    flags = jnp.stack([side.astype(jnp.int32), core.astype(jnp.int32)])
 
     def in_order(own, other):
         return jnp.where(side == 0, own, other), jnp.where(side == 0, other, own)
 
-    weight_block = pl.BlockSpec((1, 4, 3, 64, TOK), lambda i: (i, 0, 0, 0, 0))
+    weight_block = pl.BlockSpec((2, 4, 3, 64, TOK), lambda i: (i, 0, 0, 0, 0))
+    out_block = pl.BlockSpec((1, TOK, 2 * TOK), lambda i: (i, 0, 0))
 
     def fixed(*shape):
         return pl.BlockSpec(shape, lambda i: (0,) * len(shape))
 
-    patch_part = pl.pallas_call(
+    pieces = pl.pallas_call(
         patch_kernel,
-        out_shape=spec_of((2, IMGTOK, PCH), bf16),
-        grid=(8,),
+        out_shape=spec_of((8, 2 * IMGTOK, PCH), bf16),
+        grid=(4,),
         in_specs=[
+            whole(pltpu.SMEM),
             weight_block,
             fixed(3, IMGTOK, TOK),
             fixed(3, IMGTOK, TOK),
-            pl.BlockSpec((1, PCH, TOK), lambda i: (i, 0, 0)),
+            pl.BlockSpec((2, PCH + PCOLS, TOK), lambda i: (i, 0, 0)),
         ],
-        out_specs=fixed(2, IMGTOK, PCH),
-        scratch_shapes=[pltpu.VMEM((2, IMGTOK, PCH), f32)],
-    )(weights, *in_order(image_grads, image_other), patch_half)
-    pieces = exchanged(
-        jnp.broadcast_to(patch_part, (8, 2, IMGTOK, PCH)).reshape(16, IMGTOK, PCH), ("head", "yl")
-    )
+        out_specs=fixed(8, 2 * IMGTOK, PCH),
+        scratch_shapes=[pltpu.VMEM((2 * IMGTOK, PCH), f32)],
+    )(flags, weights, image_grads, image_other, along_head)
+    pieces = exchanged(pieces.reshape(16, IMGTOK, PCH), ("head", "yl"))
+
+    mine, theirs = pl.pallas_call(
+        grad_kernel,
+        out_shape=[spec_of((4, TOK, 2 * TOK), bf16)] * 2,
+        grid=(4,),
+        in_specs=[
+            whole(pltpu.SMEM),
+            weight_block,
+            fixed(3, TOK, TOK),
+            fixed(3, TOK, TOK),
+        ],
+        out_specs=[out_block] * 2,
+    )(flags, weights, grads, grads_other)
+    pieces, theirs, left, slope, kernel_mine = lax.optimization_barrier(
+        (pieces, theirs, left, slope, kernel_mine)
+    )
+    arrived = lax.ppermute(theirs, "head", [(i, i ^ 1) for i in range(8)])
 
     flags = jnp.stack([head_index.astype(jnp.int32), present.astype(jnp.int32)])
-    partial = on_chip(conv_kernel, spec_of((64, LANES), bf16), 5, scalars=1)(
+    partial = on_chip(conv_kernel, spec_of((64, 7, 128), bf16), 5, scalars=1)(
         flags, pieces, kernel_mine, slope, left
     )
 
-    halves = pl.pallas_call(
-        grad_kernel,
-        out_shape=spec_of((8, TOK, 2 * TOK), bf16),
-        grid=(8,),
-        in_specs=[weight_block, fixed(3, TOK, TOK), fixed(3, TOK, TOK)],
-        out_specs=pl.BlockSpec((1, TOK, 2 * TOK), lambda i: (i, 0, 0)),
-    )(weights, *in_order(grads, grads_other))
-    summed = jnp.sum(exchanged(halves, "head").astype(f32), axis=0).astype(bf16)
+    owned = exchanged(partial, WIDE)
+
+    chip = (mine.astype(f32) + arrived.astype(f32)).astype(bf16)
+    place_x = head_index // 2
+    total = lax.dynamic_index_in_dim(chip, place_x, 0, keepdims=False).astype(f32)
+    slices = [
+        lax.dynamic_index_in_dim(chip, (place_x + d) % 4, 0, keepdims=False) for d in range(1, 4)
+    ]
+    owned = jnp.sum(once_here(owned, slices).astype(f32), axis=0)
+    for d, piece in zip(range(1, 4), slices):
+        piece = lax.ppermute(piece, "head", [(i, (i + 2 * d) % 8) for i in range(8)])
+        total = total + piece.astype(f32)
+
+    squares = jnp.broadcast_to(jnp.sum(owned * owned), (1, 128))
+    squares = jnp.sum(sent_to_all(squares, WIDE), axis=0)
+    summed = total.astype(bf16)
+    summed, squares = lax.optimization_barrier((summed, squares))
     mine, theirs = in_order(summed[:, :TOK], summed[:, TOK:])
-    arrived = swapped(theirs)
-    even, odd = in_order(mine, arrived)
+    even, odd = in_order(mine, swapped(theirs))
     input_grad_t = jnp.stack([even.reshape(4, 64, TOK), odd.reshape(4, 64, TOK)], axis=1)
     input_grad_t = input_grad_t.reshape(512, TOK)
 
-    owned = exchanged(partial.reshape(64, 7, 128), WIDE)
-    owned = jnp.sum(owned.astype(f32), axis=0)
-    squares = jnp.broadcast_to(jnp.sum(owned * owned), (1, 128))
-    squares = jnp.sum(sent_to_all(squares, WIDE), axis=0)
     together = sent_to_all(jnp.concatenate([owned, squares], axis=0), "head")
     total = jnp.sum(together[:, 7, 0])
     columns = together[:, :7].reshape(8, LANES)

time: 353 us -> 255 us (0.72)
  blocking collectives: 161 us -> 0 us
  starting transfers between devices: 73.1 us -> 130 us
  waiting for transfers between devices: 40 us -> 49.1 us
  Pallas kernels: 33.7 us -> 27.9 us
    all_gather x3 -> x0, blocking collectives: 146 us -> none  [the longest x1 55.6 us: shards(): kernel_all = lax.all_gather(kernel_second.astype(bf16), WIDE, axis=0)]
    all_to_all x4 -> x8, starting transfers between devices: 36.7 us -> 80.4 us  [exchanged(): return lax.all_to_all(pieces, axis, split_axis=0, concat_axis=0, tiled=True)]
    ppermute x12, waiting for transfers between devices: 1.2 us -> 19.3 us  [passed_along(): return lax.ppermute(block, axis, route)]
    all_to_all x4 -> x8, waiting for transfers between devices: 32.2 us -> 17.3 us  [exchanged(): return lax.all_to_all(pieces, axis, split_axis=0, concat_axis=0, tiled=True)]
    all_to_all x1 -> x0, blocking collectives: 14.8 us -> none  [exchanged(): return lax.all_to_all(pieces, axis, split_axis=0, concat_axis=0, tiled=True)]
    ppermute x0 -> x4, starting transfers between devices: none -> 12.8 us  [the longest x3 9.89 us: shards(): lax.ppermute(piece, 'head', [(i, (i + 2 * d) % 8) for i in range(8)])]
    ppermute x3, waiting for transfers between devices: 5.84 us -> 12.5 us  [swapped(): return lax.ppermute(value, 'yl', [(0, 1), (1, 0)])]
    pallas_call x3, Pallas kernels: 19.7 us -> 13.9 us  [the longest x1 5.25 us: shards(): pl.pallas_call(grad_kernel, out_shape=[spec_of((4, TOK, 2 * TOK), bf16)]...]
  transfers between devices with their start and end apart: 21 -> 28, of which waited for: 5 -> 11; matrix products, arithmetic and copies ran while one was open for 5% -> 8% of each run, Pallas kernels for 6% -> 9%
where the time goes in v3:
time: 255 us; the launch traced here: 253 us
  starting transfers between devices  130 us (51%)
  waiting for transfers between devices  49.1 us (19%)
  Pallas kernels  27.9 us (11%)
  between operations  20.3 us (8%)
  local copies, waits for them, and re-layouts  13.6 us (5%)
  other arithmetic  12.7 us (5%)
    all_to_all x8, starting transfers between devices, exchanged(): return lax.all_to_all(pieces, axis, split_axis=0, concat_axis=0, tiled=True)  80.4 us
    ppermute x12, starting transfers between devices, passed_along(): return lax.ppermute(block, axis, route)  26.9 us
    ppermute x12, waiting for transfers between devices, passed_along(): return lax.ppermute(block, axis, route)  19.3 us
    all_to_all x8, waiting for transfers between devices, exchanged(): return lax.all_to_all(pieces, axis, split_axis=0, concat_axis=0, tiled=True)  17.3 us
    ppermute x3, waiting for transfers between devices, swapped(): return lax.ppermute(value, 'yl', [(0, 1), (1, 0)])  12.5 us
    ppermute x3, starting transfers between devices, shards(): lax.ppermute(piece, 'head', [(i, (i + 2 * d) % 8) for i in range(8)])  9.89 us
    ppermute x3, starting transfers between devices, swapped(): return lax.ppermute(value, 'yl', [(0, 1), (1, 0)])  9.64 us
    pallas_call x1, Pallas kernels, shards(): pl.pallas_call(grad_kernel, out_shape=[spec_of((4, TOK, 2 * TOK), bf16)]...  5.25 us
  transfers between devices with their start and end apart: 28, of which 11 were waited for; matrix products, arithmetic and copies ran while one was open for 8% of the time, Pallas kernels for 9%

profile of v3, /device:TPU:1, one launch (start us, length us, event | category | flops | bytes accessed | tf_op | source)
XLA Modules:
  0.0 253.3 jit_solution(9769155587099353997)
XLA Ops:
  7.2 1.7 broadcast_in_dim.68
  8.9 7.8 %all-to-all-start = ((bf16[4,3,64,256]{3,2,1,0:T(8,128)(2,1)}), bf16[4,3,64,256]{3,2,1,0:T(8,128)(2,1)S(1)}, u32[]{:S(2)}, u32[]{:S(2)}) async-start(bf16[4,3,64,256]{3,2,1,0:T(8,128)(2,1)} %broadcast_in_dim.68), calls=%async_computation | async-start | bytes 786432 | tf_op jit(solution)/shard_map/all_to_all | solution.py:270
  17.7 1.3 collective-permute-start.1
  20.0 4.0 %collective-permute-start = (bf16[2,256,256]{2,1,0:T(8,128)(2,1)S(1)}, bf16[2,256,256]{2,1,0:T(8,128)(2,1)S(1)}, u32[]{:S(2)}, u32[]{:S(2)}) collective-permute-start(bf16[2,256,256]{2,1,0:T(8,128)(2,1)S(1)} %pad_maximum_fusion), channel_id=1, source_target_pairs={{0,1},{1,2},{2,3},{3,4},{4,5},{5,6},{6,7},{7,8},{8,9},{9,10},{10,1... | collective-permute-start | bytes 786440 | tf_op jit(solution)/shard_map/ppermute | solution.py:258
  24.0 7.5 %collective-permute-done.1.a1 = bf16[2,256,256]{2,1,0:T(8,128)(2,1)S(1)} collective-permute-done((bf16[2,256,256]{2,1,0:T(8,128)(2,1)S(1)}, bf16[2,256,256]{2,1,0:T(8,128)(2,1)S(1)}, u32[]{:S(2)}, u32[]{:S(2)}) %collective-permute-start.1) | collective-permute-done | bytes 262176 | tf_op jit(solution)/shard_map/ppermute | solution.py:258
  33.5 5.0 %collective-permute-start.2 = (bf16[2,256,256]{2,1,0:T(8,128)(2,1)S(1)}, bf16[2,256,256]{2,1,0:T(8,128)(2,1)S(1)}, u32[]{:S(2)}, u32[]{:S(2)}) collective-permute-start(bf16[2,256,256]{2,1,0:T(8,128)(2,1)S(1)} %collective-permute-done.b1), channel_id=1, source_target_pairs={{0,1},{1,2},{2,3},{3,4},{4,5},{5,6},{6,7},{7,8},{8,9},{9,10},{10,1... | collective-permute-start | bytes 786440 | tf_op jit(solution)/shard_map/ppermute | solution.py:258
  38.5 1.3 collective-permute-start.3
  43.4 4.0 %collective-permute-done.3.a2 = bf16[2,256,256]{2,1,0:T(8,128)(2,1)S(1)} collective-permute-done((bf16[2,256,256]{2,1,0:T(8,128)(2,1)S(1)}, bf16[2,256,256]{2,1,0:T(8,128)(2,1)S(1)}, u32[]{:S(2)}, u32[]{:S(2)}) %collective-permute-start.3) | collective-permute-done | bytes 262176 | tf_op jit(solution)/shard_map/ppermute | solution.py:258
  48.1 10.8 %all-to-all-start.1 = ((bf16[8,26,256]{2,1,0:T(8,128)(2,1)}), bf16[8,26,256]{2,1,0:T(8,128)(2,1)S(1)}, u32[]{:S(2)}, u32[]{:S(2)}) async-start(bf16[8,26,256]{2,1,0:T(8,128)(2,1)} %broadcast_in_dim.76), calls=%async_computation.1 | async-start | bytes 262144 | tf_op jit(solution)/shard_map/all_to_all | solution.py:270
  59.6 3.6 %collective-permute-start.4 = (bf16[2,256,256]{2,1,0:T(8,128)(2,1)S(1)}, bf16[2,256,256]{2,1,0:T(8,128)(2,1)S(1)}, u32[]{:S(2)}, u32[]{:S(2)}) collective-permute-start(bf16[2,256,256]{2,1,0:T(8,128)(2,1)S(1)} %collective-permute-done.2.b2), channel_id=1, source_target_pairs={{0,1},{1,2},{2,3},{3,4},{4,5},{5,6},{6,7},{7,8},{8,9},{9,10},{10,1... | collective-permute-start | bytes 786440 | tf_op jit(solution)/shard_map/ppermute | solution.py:258
  63.2 1.3 collective-permute-start.5
  64.5 3.9 %all-to-all-done.1 = bf16[8,26,256]{2,1,0:T(8,128)(2,1)S(1)} async-done(((bf16[8,26,256]{2,1,0:T(8,128)(2,1)}), bf16[8,26,256]{2,1,0:T(8,128)(2,1)S(1)}, u32[]{:S(2)}, u32[]{:S(2)}) %all-to-all-start.1) | async-done | bytes 106528 | tf_op jit(solution)/shard_map/all_to_all | solution.py:270
  68.5 2.7 %collective-permute-done.5.a3 = bf16[2,256,256]{2,1,0:T(8,128)(2,1)S(1)} collective-permute-done((bf16[2,256,256]{2,1,0:T(8,128)(2,1)S(1)}, bf16[2,256,256]{2,1,0:T(8,128)(2,1)S(1)}, u32[]{:S(2)}, u32[]{:S(2)}) %collective-permute-start.5) | collective-permute-done | bytes 262176 | tf_op jit(solution)/shard_map/ppermute | solution.py:258
  72.0 5.2 %all-to-all-start.2 = ((bf16[8,82,256]{2,1,0:T(8,128)(2,1)}), bf16[8,82,256]{2,1,0:T(8,128)(2,1)S(1)}, u32[]{:S(2)}, u32[]{:S(2)}) async-start(bf16[8,82,256]{2,1,0:T(8,128)(2,1)} %broadcast_in_dim.77), calls=%async_computation.2 | async-start | bytes 720896 | tf_op jit(solution)/shard_map/all_to_all | solution.py:270
  77.2 1.3 collective-permute-start.7
  78.5 4.0 %collective-permute-start.6 = (bf16[2,256,256]{2,1,0:T(8,128)(2,1)S(1)}, bf16[2,256,256]{2,1,0:T(8,128)(2,1)S(1)}, u32[]{:S(2)}, u32[]{:S(2)}) collective-permute-start(bf16[2,256,256]{2,1,0:T(8,128)(2,1)S(1)} %collective-permute-done.4.b3), channel_id=1, source_target_pairs={{0,1},{1,2},{2,3},{3,4},{4,5},{5,6},{6,7},{7,8},{8,9},{9,10},{10,1... | collective-permute-start | bytes 786440 | tf_op jit(solution)/shard_map/ppermute | solution.py:258
  85.3 2.7 %collective-permute-done.7.a4 = bf16[2,256,256]{2,1,0:T(8,128)(2,1)S(1)} collective-permute-done((bf16[2,256,256]{2,1,0:T(8,128)(2,1)S(1)}, bf16[2,256,256]{2,1,0:T(8,128)(2,1)S(1)}, u32[]{:S(2)}, u32[]{:S(2)}) %collective-permute-start.7) | collective-permute-done | bytes 262176 | tf_op jit(solution)/shard_map/ppermute | solution.py:258
  88.0 2.3 collective-permute-done.6.b4
  91.0 3.7 %shard_map.225.stats = f32[8,256]{1,0:T(8,128)} custom-call(s32[8,256]{1,0:T(8,128)} %add_subtract_fusion.meta, bf16[256,256]{1,0:T(8,128)(2,1)} %q.3, bf16[256,256]{1,0:T(8,128)(2,1)} %g.3, bf16[256,256]{1,0:T(8,128)(2,1)} %k0.5, bf16[256,256]{1,0:T(8,128)(2,1)} %v0.5, bf16[2,256,256]{2,1,0:T(8,128)(2,1)} %copy-done.3, bf16[2,256,256]{2,1,0:T(8,128)(2,1)} %copy-done.4, ...), custom_call_target="tpu_custom_call" | custom-call | tf_op jit(solution)/shard_map/pallas_call | solution.py:352
  95.0 1.1 broadcast_in_dim.78
  96.0 7.9 %all-to-all-start.3 = ((bf16[8,264,256]{2,1,0:T(8,128)(2,1)}), bf16[8,264,256]{2,1,0:T(8,128)(2,1)S(1)}, u32[]{:S(2)}, u32[]{:S(2)}) async-start(bf16[8,264,256]{2,1,0:T(8,128)(2,1)} %broadcast_in_dim.78), calls=%async_computation.3 | async-start | bytes 2162688 | tf_op jit(solution)/shard_map/all_to_all | solution.py:270
  104.0 1.3 collective-permute-start.11
  105.3 1.3 collective-permute-start.10
  106.6 1.3 collective-permute-start.9
  107.9 1.3 collective-permute-start.8
  109.2 5.2 %shard_map.226 = (bf16[256,256]{1,0:T(8,128)(2,1)}, f32[256,256]{1,0:T(8,128)}, f32[256,256]{1,0:T(8,128)}) custom-call(s32[8,256]{1,0:T(8,128)} %add_subtract_fusion.meta, f32[8,256]{1,0:T(8,128)} %shard_map.225.stats, bf16[256,256]{1,0:T(8,128)(2,1)} %q.3, bf16[256,256]{1,0:T(8,128)(2,1)} %g.3, bf16[256,256]{1,0:T(8,128)(2,1)} %k0.5, bf16[256,256]{1,0:T(8,128)(2,1)} %v0.5, ...), custom_call_target="tpu_custom_call" | custom-call | tf_op jit(solution)/shard_map/pallas_call | solution.py:393
  115.0 5.2 %shard_map.227 = (bf16[3,256,256]{2,1,0:T(8,128)(2,1)}, bf16[3,64,256]{2,1,0:T(8,128)(2,1)}) custom-call(s32[1]{0:T(128)} %bitcast.7.start, s32[8,256]{1,0:T(8,128)} %add_subtract_fusion.meta, bf16[256,256]{1,0:T(8,128)(2,1)} %k0.5, bf16[256,256]{1,0:T(8,128)(2,1)} %v0.5, bf16[2,256,256]{2,1,0:T(8,128)(2,1)} %copy-done.9, bf16[2,256,256]{2,1,0:T(8,128)(2,1)} %copy-done.10, ...), custom_call_target="tpu_custom_call" | custom-call | tf_op jit(solution)/shard_map/pallas_call | solution.py:398
  120.2 4.1 %collective-permute-start.12 = (bf16[3,64,256]{2,1,0:T(8,128)(2,1)}, bf16[3,64,256]{2,1,0:T(8,128)(2,1)S(1)}, u32[]{:S(2)}, u32[]{:S(2)}) collective-permute-start(bf16[3,64,256]{2,1,0:T(8,128)(2,1)} %get-tuple-element.50.own), channel_id=1, source_target_pairs={{0,1},{1,0},{2,3},{3,2},{4,5},{5,4},{6,7},{7,6},{8,9},{9,8},{10,11... | collective-permute-start | bytes 294920 | tf_op jit(solution)/shard_map/ppermute | solution.py:262
  124.9 2.6 %collective-permute-done.12.other = bf16[3,64,256]{2,1,0:T(8,128)(2,1)S(1)} collective-permute-done((bf16[3,64,256]{2,1,0:T(8,128)(2,1)}, bf16[3,64,256]{2,1,0:T(8,128)(2,1)S(1)}, u32[]{:S(2)}, u32[]{:S(2)}) %collective-permute-start.12) | collective-permute-done | bytes 98336 | tf_op jit(solution)/shard_map/ppermute | solution.py:262
  128.6 5.0 %shard_map.229 = bf16[8,128,256]{2,1,0:T(8,128)(2,1)} custom-call(s32[2]{0:T(128)} %pad_add_fusion.flags, bf16[8,4,3,64,256]{4,3,2,1,0:T(8,128)(2,1)} %bitcast.60, bf16[3,64,256]{2,1,0:T(8,128)(2,1)} %get-tuple-element.50.own, bf16[3,64,256]{2,1,0:T(8,128)(2,1)} %copy-done.15, bf16[8,264,256]{2,1,0:T(8,128)(2,1)} %copy-done), custom_call_target="tpu_custom_call" | custom-call | tf_op jit(solution)/shard_map/pallas_call | solution.py:419
  133.7 6.3 %all-to-all-start.4 = ((bf16[16,64,256]{2,1,0:T(8,128)(2,1)}), bf16[16,64,256]{2,1,0:T(8,128)(2,1)S(1)}, u32[]{:S(2)}, u32[]{:S(2)}) async-start(bf16[16,64,256]{2,1,0:T(8,128)(2,1)} %bitcast.62), calls=%async_computation.4 | async-start | bytes 1048576 | tf_op jit(solution)/shard_map/all_to_all | solution.py:270
  140.0 3.3 %collective-permute-start.13 = (bf16[3,256,256]{2,1,0:T(8,128)(2,1)S(1)}, bf16[3,256,256]{2,1,0:T(8,128)(2,1)S(1)}, u32[]{:S(2)}, u32[]{:S(2)}) collective-permute-start(bf16[3,256,256]{2,1,0:T(8,128)(2,1)S(1)} %copy-done.7), channel_id=1, source_target_pairs={{0,1},{1,0},{2,3},{3,2},{4,5},{5,4},{6,7},{7,6},{8,9},{9,8},{10,11... | collective-permute-start | bytes 1179656 | tf_op jit(solution)/shard_map/ppermute | solution.py:262
  146.3 9.9 %collective-permute-done.13.other = bf16[3,256,256]{2,1,0:T(8,128)(2,1)S(1)} collective-permute-done((bf16[3,256,256]{2,1,0:T(8,128)(2,1)S(1)}, bf16[3,256,256]{2,1,0:T(8,128)(2,1)S(1)}, u32[]{:S(2)}, u32[]{:S(2)}) %collective-permute-start.13) | collective-permute-done | bytes 393248 | tf_op jit(solution)/shard_map/ppermute | solution.py:262
  157.0 5.3 %shard_map.228 = (bf16[4,256,512]{2,1,0:T(8,128)(2,1)}, bf16[4,256,512]{2,1,0:T(8,128)(2,1)}) custom-call(s32[2]{0:T(128)} %pad_add_fusion.flags, bf16[8,4,3,64,256]{4,3,2,1,0:T(8,128)(2,1)} %bitcast.61, bf16[3,256,256]{2,1,0:T(8,128)(2,1)} %get-tuple-element.51.own, bf16[3,256,256]{2,1,0:T(8,128)(2,1)} %copy-done.8), custom_call_target="tpu_custom_call" | custom-call | tf_op jit(solution)/shard_map/pallas_call | solution.py:435
  162.2 2.9 %collective-permute-start.14 = (bf16[4,256,512]{2,1,0:T(8,128)(2,1)}, bf16[4,256,512]{2,1,0:T(8,128)(2,1)S(1)}, u32[]{:S(2)}, u32[]{:S(2)}) collective-permute-start(bf16[4,256,512]{2,1,0:T(8,128)(2,1)} %get-tuple-element.57), channel_id=1, source_target_pairs={{0,64},{64,0},{128,192},{192,128},{256,320},{320,256},{384,448},{4... | collective-permute-start | bytes 3145736 | tf_op jit(solution)/shard_map/ppermute | solution.py:450
  165.2 1.2 pad_add_fusion.1.scalars
  166.4 3.6 %shard_map.230 = bf16[64,7,128]{2,1,0:T(8,128)(2,1)} custom-call(s32[2]{0:T(128)} %pad_add_fusion.1.scalars, bf16[16,64,256]{2,1,0:T(8,128)(2,1)} %copy-done.1, bf16[9,16,256]{2,1,0:T(8,128)(2,1)} %bitcast.73, f32[64,16]{1,0:T(8,128)} %fusion.4.slope, bf16[4,64,64]{2,1,0:T(8,128)(2,1)} %maximum_bitcast_fusion.left), custom_call_target="tpu_custom_call" | custom-call | tf_op jit(solution)/shard_map/pallas_call | solution.py:453
  170.0 24.2 %all-to-all-start.5 = ((bf16[64,7,128]{2,1,0:T(8,128)(2,1)}), bf16[64,7,128]{2,1,0:T(8,128)(2,1)S(1)}, u32[]{:S(2)}, u32[]{:S(2)}) async-start(bf16[64,7,128]{2,1,0:T(8,128)(2,1)} %shard_map.230), calls=%async_computation.5 | async-start | bytes 262144 | tf_op jit(solution)/shard_map/all_to_all | solution.py:270
  194.3 1.5 add_convert_fusion
  195.9 3.2 %collective-permute-start.15 = (bf16[256,512]{1,0:T(8,128)(2,1)S(1)}, bf16[256,512]{1,0:T(8,128)(2,1)S(1)}, u32[]{:S(2)}, u32[]{:S(2)}) collective-permute-start(bf16[256,512]{1,0:T(8,128)(2,1)S(1)} %get-tuple-element.71), channel_id=1, source_target_pairs={{0,128},{64,192},{128,256},{192,320},{256,384},{320,448},{384,0},{... | collective-permute-start | bytes 786440 | tf_op jit(solution)/shard_map/ppermute | solution.py:467
  199.1 3.3 %collective-permute-start.17 = (bf16[256,512]{1,0:T(8,128)(2,1)S(1)}, bf16[256,512]{1,0:T(8,128)(2,1)S(1)}, u32[]{:S(2)}, u32[]{:S(2)}) collective-permute-start(bf16[256,512]{1,0:T(8,128)(2,1)S(1)} %get-tuple-element.72), channel_id=1, source_target_pairs={{0,384},{64,448},{128,0},{192,64},{256,128},{320,192},{384,256},{4... | collective-permute-start | bytes 786440 | tf_op jit(solution)/shard_map/ppermute | solution.py:467
  202.4 3.4 %collective-permute-start.16 = (bf16[256,512]{1,0:T(8,128)(2,1)S(1)}, bf16[256,512]{1,0:T(8,128)(2,1)S(1)}, u32[]{:S(2)}, u32[]{:S(2)}) collective-permute-start(bf16[256,512]{1,0:T(8,128)(2,1)S(1)} %get-tuple-element.73), channel_id=1, source_target_pairs={{0,256},{64,320},{128,384},{192,448},{256,0},{320,64},{384,128},{4... | collective-permute-start | bytes 786440 | tf_op jit(solution)/shard_map/ppermute | solution.py:467
  206.6 1.3 broadcast_in_dim_broadcast_in_dim.3
  207.9 12.1 %all-to-all-start.6 = ((f32[64,1,128]{2,1,0:T(1,128)}), f32[64,1,128]{2,1,0:T(1,128)S(1)}, u32[]{:S(2)}, u32[]{:S(2)}) async-start(f32[64,1,128]{2,1,0:T(1,128)} %broadcast_in_dim_broadcast_in_dim.3), calls=%async_computation.6 | async-start | bytes 65536 | tf_op jit(solution)/shard_map/all_to_all | solution.py:270
  220.0 10.8 %all-to-all-done.6 = f32[64,1,128]{2,1,0:T(1,128)S(1)} async-done(((f32[64,1,128]{2,1,0:T(1,128)}), f32[64,1,128]{2,1,0:T(1,128)S(1)}, u32[]{:S(2)}, u32[]{:S(2)}) %all-to-all-start.6) | async-done | bytes 32800 | tf_op jit(solution)/shard_map/all_to_all | solution.py:270
  231.6 6.1 %all-to-all-start.7 = ((f32[8,8,128]{2,1,0:T(8,128)}), f32[8,8,128]{2,1,0:T(8,128)S(1)}, u32[]{:S(2)}, u32[]{:S(2)}) async-start(f32[8,8,128]{2,1,0:T(8,128)} %broadcast_in_dim.79), calls=%async_computation.7 | async-start | bytes 65536 | tf_op jit(solution)/shard_map/all_to_all | solution.py:270
  237.7 2.2 collective-permute-start.18
  239.9 2.5 all-to-all-done.7
  (150 shorter events, 19.7 us)
Async XLA Ops:
  7.2 25.2 %copy-start.30 = (s32[32]{0:T(128)S(1)}, s32[32]{0:T(128)}, u32[]{:S(2)}) copy-start(s32[32]{0:T(128)} %param.23) | copy-start | bytes 388
  7.2 25.4 %copy-start.14 = (f32[18,256]{1,0:T(8,128)S(1)}, f32[18,256]{1,0:T(8,128)}, u32[]{:S(2)}) copy-start(f32[18,256]{1,0:T(8,128)} %param.31) | copy-start | bytes 55300
  7.2 25.4 %copy-start.28 = (s32[64]{0:T(128)S(1)}, s32[64]{0:T(128)}, u32[]{:S(2)}) copy-start(s32[64]{0:T(128)} %param.26) | copy-start | bytes 772
  7.2 25.4 %copy-start.29 = (s32[64]{0:T(128)S(1)}, s32[64]{0:T(128)}, u32[]{:S(2)}) copy-start(s32[64]{0:T(128)} %param.24) | copy-start | bytes 772
  7.2 26.1 %copy-start.26 = (bf16[1,1,8,128]{3,2,1,0:T(8,128)(2,1)S(1)}, bf16[1,1,8,128]{3,2,1,0:T(8,128)(2,1)}, u32[]{:S(2)}) copy-start(bf16[1,1,8,128]{3,2,1,0:T(8,128)(2,1)} %param.29) | copy-start | bytes 6148
  7.2 26.1 %copy-start.27 = (bf16[1,1,8,128]{3,2,1,0:T(8,128)(2,1)S(1)}, bf16[1,1,8,128]{3,2,1,0:T(8,128)(2,1)}, u32[]{:S(2)}) copy-start(bf16[1,1,8,128]{3,2,1,0:T(8,128)(2,1)} %param.28) | copy-start | bytes 6148
  7.2 32.6 %copy-start.31 = (s32[64]{0:T(128)S(1)}, s32[64]{0:T(128)}, u32[]{:S(2)}) copy-start(s32[64]{0:T(128)} %param.25) | copy-start | bytes 772
  8.9 76.2 %copy-start.13 = (bf16[256,512]{1,0:T(8,128)(2,1)S(1)}, bf16[256,512]{1,0:T(8,128)(2,1)}, u32[]{:S(2)}) copy-start(bf16[256,512]{1,0:T(8,128)(2,1)} %param.27) | copy-start | bytes 786436
  8.9 22.6 %all-to-all-start = ((bf16[4,3,64,256]{3,2,1,0:T(8,128)(2,1)}), bf16[4,3,64,256]{3,2,1,0:T(8,128)(2,1)S(1)}, u32[]{:S(2)}, u32[]{:S(2)}) async-start(bf16[4,3,64,256]{3,2,1,0:T(8,128)(2,1)} %broadcast_in_dim.68), calls=%async_computation | async-start | bytes 786432 | tf_op jit(solution)/shard_map/all_to_all | solution.py:270
  16.7 110.9 %all-gather.3.cloned.1.call-start = ((), (), s32[]{:S(2)}) async-start(), calls=%async_computation.8 | async-start | bytes 3538944 | tf_op jit(solution)/shard_map/all_gather | solution.py:360
  17.7 13.8 %collective-permute-start.1 = (bf16[2,256,256]{2,1,0:T(8,128)(2,1)S(1)}, bf16[2,256,256]{2,1,0:T(8,128)(2,1)S(1)}, u32[]{:S(2)}, u32[]{:S(2)}) collective-permute-start(bf16[2,256,256]{2,1,0:T(8,128)(2,1)S(1)} %pad_maximum_fusion.1), channel_id=1, source_target_pairs={{1,0},{2,1},{3,2},{4,3},{5,4},{6,5},{7,6},{8,7},{9,8},{10,9},{11,1... | collective-permute-start | bytes 786440 | tf_op jit(solution)/shard_map/ppermute | solution.py:258
  20.0 11.6 %collective-permute-start = (bf16[2,256,256]{2,1,0:T(8,128)(2,1)S(1)}, bf16[2,256,256]{2,1,0:T(8,128)(2,1)S(1)}, u32[]{:S(2)}, u32[]{:S(2)}) collective-permute-start(bf16[2,256,256]{2,1,0:T(8,128)(2,1)S(1)} %pad_maximum_fusion), channel_id=1, source_target_pairs={{0,1},{1,2},{2,3},{3,4},{4,5},{5,6},{6,7},{7,8},{8,9},{9,10},{10,1... | collective-permute-start | bytes 786440 | tf_op jit(solution)/shard_map/ppermute | solution.py:258
  31.6 82.9 %copy-start.9 = (bf16[2,256,256]{2,1,0:T(8,128)(2,1)}, bf16[2,256,256]{2,1,0:T(8,128)(2,1)S(1)}, u32[]{:S(2)}) copy-start(bf16[2,256,256]{2,1,0:T(8,128)(2,1)S(1)} %collective-permute-done.1.a1) | copy-start | bytes 786436
  31.6 58.7 %copy-start.3 = (bf16[2,256,256]{2,1,0:T(8,128)(2,1)}, bf16[2,256,256]{2,1,0:T(8,128)(2,1)S(1)}, u32[]{:S(2)}) copy-start(bf16[2,256,256]{2,1,0:T(8,128)(2,1)S(1)} %collective-permute-done.b1) | copy-start | bytes 786436
  33.5 13.9 %collective-permute-start.2 = (bf16[2,256,256]{2,1,0:T(8,128)(2,1)S(1)}, bf16[2,256,256]{2,1,0:T(8,128)(2,1)S(1)}, u32[]{:S(2)}, u32[]{:S(2)}) collective-permute-start(bf16[2,256,256]{2,1,0:T(8,128)(2,1)S(1)} %collective-permute-done.b1), channel_id=1, source_target_pairs={{0,1},{1,2},{2,3},{3,4},{4,5},{5,6},{6,7},{7,8},{8,9},{9,10},{10,1... | collective-permute-start | bytes 786440 | tf_op jit(solution)/shard_map/ppermute | solution.py:258
  38.5 8.9 %collective-permute-start.3 = (bf16[2,256,256]{2,1,0:T(8,128)(2,1)S(1)}, bf16[2,256,256]{2,1,0:T(8,128)(2,1)S(1)}, u32[]{:S(2)}, u32[]{:S(2)}) collective-permute-start(bf16[2,256,256]{2,1,0:T(8,128)(2,1)S(1)} %collective-permute-done.1.a1), channel_id=1, source_target_pairs={{1,0},{2,1},{3,2},{4,3},{5,4},{6,5},{7,6},{8,7},{9,8},{10,9},{11,1... | collective-permute-start | bytes 786440 | tf_op jit(solution)/shard_map/ppermute | solution.py:258
  47.4 47.3 %copy-start.10 = (bf16[2,256,256]{2,1,0:T(8,128)(2,1)}, bf16[2,256,256]{2,1,0:T(8,128)(2,1)S(1)}, u32[]{:S(2)}) copy-start(bf16[2,256,256]{2,1,0:T(8,128)(2,1)S(1)} %collective-permute-done.3.a2) | copy-start | bytes 786436
  47.4 42.9 %copy-start.4 = (bf16[2,256,256]{2,1,0:T(8,128)(2,1)}, bf16[2,256,256]{2,1,0:T(8,128)(2,1)S(1)}, u32[]{:S(2)}) copy-start(bf16[2,256,256]{2,1,0:T(8,128)(2,1)S(1)} %collective-permute-done.2.b2) | copy-start | bytes 786436
  48.1 20.3 %all-to-all-start.1 = ((bf16[8,26,256]{2,1,0:T(8,128)(2,1)}), bf16[8,26,256]{2,1,0:T(8,128)(2,1)S(1)}, u32[]{:S(2)}, u32[]{:S(2)}) async-start(bf16[8,26,256]{2,1,0:T(8,128)(2,1)} %broadcast_in_dim.76), calls=%async_computation.1 | async-start | bytes 262144 | tf_op jit(solution)/shard_map/all_to_all | solution.py:270
  59.6 11.5 %collective-permute-start.4 = (bf16[2,256,256]{2,1,0:T(8,128)(2,1)S(1)}, bf16[2,256,256]{2,1,0:T(8,128)(2,1)S(1)}, u32[]{:S(2)}, u32[]{:S(2)}) collective-permute-start(bf16[2,256,256]{2,1,0:T(8,128)(2,1)S(1)} %collective-permute-done.2.b2), channel_id=1, source_target_pairs={{0,1},{1,2},{2,3},{3,4},{4,5},{5,6},{6,7},{7,8},{8,9},{9,10},{10,1... | collective-permute-start | bytes 786440 | tf_op jit(solution)/shard_map/ppermute | solution.py:258
  63.2 7.9 %collective-permute-start.5 = (bf16[2,256,256]{2,1,0:T(8,128)(2,1)S(1)}, bf16[2,256,256]{2,1,0:T(8,128)(2,1)S(1)}, u32[]{:S(2)}, u32[]{:S(2)}) collective-permute-start(bf16[2,256,256]{2,1,0:T(8,128)(2,1)S(1)} %collective-permute-done.3.a2), channel_id=1, source_target_pairs={{1,0},{2,1},{3,2},{4,3},{5,4},{6,5},{7,6},{8,7},{9,8},{10,9},{11,1... | collective-permute-start | bytes 786440 | tf_op jit(solution)/shard_map/ppermute | solution.py:258
  71.1 23.7 %copy-start.11 = (bf16[2,256,256]{2,1,0:T(8,128)(2,1)}, bf16[2,256,256]{2,1,0:T(8,128)(2,1)S(1)}, u32[]{:S(2)}) copy-start(bf16[2,256,256]{2,1,0:T(8,128)(2,1)S(1)} %collective-permute-done.5.a3) | copy-start | bytes 786436
  71.2 19.1 %copy-start.5 = (bf16[2,256,256]{2,1,0:T(8,128)(2,1)}, bf16[2,256,256]{2,1,0:T(8,128)(2,1)S(1)}, u32[]{:S(2)}) copy-start(bf16[2,256,256]{2,1,0:T(8,128)(2,1)S(1)} %collective-permute-done.4.b3) | copy-start | bytes 786436
  72.0 22.6 %all-to-all-start.2 = ((bf16[8,82,256]{2,1,0:T(8,128)(2,1)}), bf16[8,82,256]{2,1,0:T(8,128)(2,1)S(1)}, u32[]{:S(2)}, u32[]{:S(2)}) async-start(bf16[8,82,256]{2,1,0:T(8,128)(2,1)} %broadcast_in_dim.77), calls=%async_computation.2 | async-start | bytes 720896 | tf_op jit(solution)/shard_map/all_to_all | solution.py:270
  77.2 10.8 %collective-permute-start.7 = (bf16[2,256,256]{2,1,0:T(8,128)(2,1)S(1)}, bf16[2,256,256]{2,1,0:T(8,128)(2,1)S(1)}, u32[]{:S(2)}, u32[]{:S(2)}) collective-permute-start(bf16[2,256,256]{2,1,0:T(8,128)(2,1)S(1)} %collective-permute-done.5.a3), channel_id=1, source_target_pairs={{1,0},{2,1},{3,2},{4,3},{5,4},{6,5},{7,6},{8,7},{9,8},{10,9},{11,1... | collective-permute-start | bytes 786440 | tf_op jit(solution)/shard_map/ppermute | solution.py:258
  78.5 11.8 %collective-permute-start.6 = (bf16[2,256,256]{2,1,0:T(8,128)(2,1)S(1)}, bf16[2,256,256]{2,1,0:T(8,128)(2,1)S(1)}, u32[]{:S(2)}, u32[]{:S(2)}) collective-permute-start(bf16[2,256,256]{2,1,0:T(8,128)(2,1)S(1)} %collective-permute-done.4.b3), channel_id=1, source_target_pairs={{0,1},{1,2},{2,3},{3,4},{4,5},{5,6},{6,7},{7,8},{8,9},{9,10},{10,1... | collective-permute-start | bytes 786440 | tf_op jit(solution)/shard_map/ppermute | solution.py:258
  88.0 26.5 %copy-start.12 = (bf16[2,256,256]{2,1,0:T(8,128)(2,1)}, bf16[2,256,256]{2,1,0:T(8,128)(2,1)S(1)}, u32[]{:S(2)}) copy-start(bf16[2,256,256]{2,1,0:T(8,128)(2,1)S(1)} %collective-permute-done.7.a4) | copy-start | bytes 786436
  96.0 31.5 %all-to-all-start.3 = ((bf16[8,264,256]{2,1,0:T(8,128)(2,1)}), bf16[8,264,256]{2,1,0:T(8,128)(2,1)S(1)}, u32[]{:S(2)}, u32[]{:S(2)}) async-start(bf16[8,264,256]{2,1,0:T(8,128)(2,1)} %broadcast_in_dim.78), calls=%async_computation.3 | async-start | bytes 2162688 | tf_op jit(solution)/shard_map/all_to_all | solution.py:270
  104.0 10.4 %collective-permute-start.11 = (f32[8,256]{1,0:T(8,128)S(1)}, f32[8,256]{1,0:T(8,128)S(1)}, u32[]{:S(2)}, u32[]{:S(2)}) collective-permute-start(f32[8,256]{1,0:T(8,128)S(1)} %copy-done.16), channel_id=1, source_target_pairs={{4,0},{5,1},{6,2},{7,3},{8,4},{9,5},{10,6},{11,7},{12,8},{13,9},{1... | collective-permute-start | bytes 24584 | tf_op jit(solution)/shard_map/ppermute | solution.py:258
  105.3 9.1 %collective-permute-start.10 = (f32[8,256]{1,0:T(8,128)S(1)}, f32[8,256]{1,0:T(8,128)S(1)}, u32[]{:S(2)}, u32[]{:S(2)}) collective-permute-start(f32[8,256]{1,0:T(8,128)S(1)} %copy-done.16), channel_id=1, source_target_pairs={{3,0},{4,1},{5,2},{6,3},{7,4},{8,5},{9,6},{10,7},{11,8},{12,9},{13... | collective-permute-start | bytes 24584 | tf_op jit(solution)/shard_map/ppermute | solution.py:258
  106.6 7.8 %collective-permute-start.9 = (f32[8,256]{1,0:T(8,128)S(1)}, f32[8,256]{1,0:T(8,128)S(1)}, u32[]{:S(2)}, u32[]{:S(2)}) collective-permute-start(f32[8,256]{1,0:T(8,128)S(1)} %copy-done.16), channel_id=1, source_target_pairs={{2,0},{3,1},{4,2},{5,3},{6,4},{7,5},{8,6},{9,7},{10,8},{11,9},{12,... | collective-permute-start | bytes 24584 | tf_op jit(solution)/shard_map/ppermute | solution.py:258
  107.9 6.5 %collective-permute-start.8 = (f32[8,256]{1,0:T(8,128)S(1)}, f32[8,256]{1,0:T(8,128)S(1)}, u32[]{:S(2)}, u32[]{:S(2)}) collective-permute-start(f32[8,256]{1,0:T(8,128)S(1)} %copy-done.16), channel_id=1, source_target_pairs={{1,0},{2,1},{3,2},{4,3},{5,4},{6,5},{7,6},{8,7},{9,8},{10,9},{11,1... | collective-permute-start | bytes 24584 | tf_op jit(solution)/shard_map/ppermute | solution.py:258
  120.2 7.4 %collective-permute-start.12 = (bf16[3,64,256]{2,1,0:T(8,128)(2,1)}, bf16[3,64,256]{2,1,0:T(8,128)(2,1)S(1)}, u32[]{:S(2)}, u32[]{:S(2)}) collective-permute-start(bf16[3,64,256]{2,1,0:T(8,128)(2,1)} %get-tuple-element.50.own), channel_id=1, source_target_pairs={{0,1},{1,0},{2,3},{3,2},{4,5},{5,4},{6,7},{7,6},{8,9},{9,8},{10,11... | collective-permute-start | bytes 294920 | tf_op jit(solution)/shard_map/ppermute | solution.py:262
  133.7 28.6 %all-to-all-start.4 = ((bf16[16,64,256]{2,1,0:T(8,128)(2,1)}), bf16[16,64,256]{2,1,0:T(8,128)(2,1)S(1)}, u32[]{:S(2)}, u32[]{:S(2)}) async-start(bf16[16,64,256]{2,1,0:T(8,128)(2,1)} %bitcast.62), calls=%async_computation.4 | async-start | bytes 1048576 | tf_op jit(solution)/shard_map/all_to_all | solution.py:270
  140.0 16.3 %collective-permute-start.13 = (bf16[3,256,256]{2,1,0:T(8,128)(2,1)S(1)}, bf16[3,256,256]{2,1,0:T(8,128)(2,1)S(1)}, u32[]{:S(2)}, u32[]{:S(2)}) collective-permute-start(bf16[3,256,256]{2,1,0:T(8,128)(2,1)S(1)} %copy-done.7), channel_id=1, source_target_pairs={{0,1},{1,0},{2,3},{3,2},{4,5},{5,4},{6,7},{7,6},{8,9},{9,8},{10,11... | collective-permute-start | bytes 1179656 | tf_op jit(solution)/shard_map/ppermute | solution.py:262
  162.2 32.0 %collective-permute-start.14 = (bf16[4,256,512]{2,1,0:T(8,128)(2,1)}, bf16[4,256,512]{2,1,0:T(8,128)(2,1)S(1)}, u32[]{:S(2)}, u32[]{:S(2)}) collective-permute-start(bf16[4,256,512]{2,1,0:T(8,128)(2,1)} %get-tuple-element.57), channel_id=1, source_target_pairs={{0,64},{64,0},{128,192},{192,128},{256,320},{320,256},{384,448},{4... | collective-permute-start | bytes 3145736 | tf_op jit(solution)/shard_map/ppermute | solution.py:450
  170.0 35.9 %all-to-all-start.5 = ((bf16[64,7,128]{2,1,0:T(8,128)(2,1)}), bf16[64,7,128]{2,1,0:T(8,128)(2,1)S(1)}, u32[]{:S(2)}, u32[]{:S(2)}) async-start(bf16[64,7,128]{2,1,0:T(8,128)(2,1)} %shard_map.230), calls=%async_computation.5 | async-start | bytes 262144 | tf_op jit(solution)/shard_map/all_to_all | solution.py:270
  195.8 48.5 %copy-start.17 = (f32[18,256]{1,0:T(8,128)S(1)}, f32[18,256]{1,0:T(8,128)}, u32[]{:S(2)}) copy-start(f32[18,256]{1,0:T(8,128)} %param.33) | copy-start | bytes 55300
  195.8 48.5 %copy-start.18 = (f32[18,256]{1,0:T(8,128)S(1)}, f32[18,256]{1,0:T(8,128)}, u32[]{:S(2)}) copy-start(f32[18,256]{1,0:T(8,128)} %param.35) | copy-start | bytes 55300
  195.8 49.2 %copy-start.19 = (f32[18,128]{1,0:T(8,128)S(1)}, f32[18,128]{1,0:T(8,128)}, u32[]{:S(2)}) copy-start(f32[18,128]{1,0:T(8,128)} %param.30) | copy-start | bytes 27652
  195.8 49.2 %copy-start.20 = (f32[18,128]{1,0:T(8,128)S(1)}, f32[18,128]{1,0:T(8,128)}, u32[]{:S(2)}) copy-start(f32[18,128]{1,0:T(8,128)} %param.32) | copy-start | bytes 27652
  195.8 49.1 %copy-start.21 = (f32[18,128]{1,0:T(8,128)S(1)}, f32[18,128]{1,0:T(8,128)}, u32[]{:S(2)}) copy-start(f32[18,128]{1,0:T(8,128)} %param.34) | copy-start | bytes 27652
  195.9 34.8 %collective-permute-start.15 = (bf16[256,512]{1,0:T(8,128)(2,1)S(1)}, bf16[256,512]{1,0:T(8,128)(2,1)S(1)}, u32[]{:S(2)}, u32[]{:S(2)}) collective-permute-start(bf16[256,512]{1,0:T(8,128)(2,1)S(1)} %get-tuple-element.71), channel_id=1, source_target_pairs={{0,128},{64,192},{128,256},{192,320},{256,384},{320,448},{384,0},{... | collective-permute-start | bytes 786440 | tf_op jit(solution)/shard_map/ppermute | solution.py:467
  199.1 31.7 %collective-permute-start.17 = (bf16[256,512]{1,0:T(8,128)(2,1)S(1)}, bf16[256,512]{1,0:T(8,128)(2,1)S(1)}, u32[]{:S(2)}, u32[]{:S(2)}) collective-permute-start(bf16[256,512]{1,0:T(8,128)(2,1)S(1)} %get-tuple-element.72), channel_id=1, source_target_pairs={{0,384},{64,448},{128,0},{192,64},{256,128},{320,192},{384,256},{4... | collective-permute-start | bytes 786440 | tf_op jit(solution)/shard_map/ppermute | solution.py:467
  202.4 28.4 %collective-permute-start.16 = (bf16[256,512]{1,0:T(8,128)(2,1)S(1)}, bf16[256,512]{1,0:T(8,128)(2,1)S(1)}, u32[]{:S(2)}, u32[]{:S(2)}) collective-permute-start(bf16[256,512]{1,0:T(8,128)(2,1)S(1)} %get-tuple-element.73), channel_id=1, source_target_pairs={{0,256},{64,320},{128,384},{192,448},{256,0},{320,64},{384,128},{4... | collective-permute-start | bytes 786440 | tf_op jit(solution)/shard_map/ppermute | solution.py:467
  207.9 22.9 %all-to-all-start.6 = ((f32[64,1,128]{2,1,0:T(1,128)}), f32[64,1,128]{2,1,0:T(1,128)S(1)}, u32[]{:S(2)}, u32[]{:S(2)}) async-start(f32[64,1,128]{2,1,0:T(1,128)} %broadcast_in_dim_broadcast_in_dim.3), calls=%async_computation.6 | async-start | bytes 65536 | tf_op jit(solution)/shard_map/all_to_all | solution.py:270
  231.6 10.8 %all-to-all-start.7 = ((f32[8,8,128]{2,1,0:T(8,128)}), f32[8,8,128]{2,1,0:T(8,128)S(1)}, u32[]{:S(2)}, u32[]{:S(2)}) async-start(f32[8,8,128]{2,1,0:T(8,128)} %broadcast_in_dim.79), calls=%async_computation.7 | async-start | bytes 65536 | tf_op jit(solution)/shard_map/all_to_all | solution.py:270
  237.7 7.9 %collective-permute-start.18 = (bf16[256,256]{1,0:T(8,128)(2,1)S(1)}, bf16[256,256]{1,0:T(8,128)(2,1)S(1)}, u32[]{:S(2)}, u32[]{:S(2)}) collective-permute-start(bf16[256,256]{1,0:T(8,128)(2,1)S(1)} %broadcast_select_fusion.2), channel_id=1, source_target_pairs={{0,1},{1,0},{2,3},{3,2},{4,5},{5,4},{6,7},{7,6},{8,9},{9,8},{10,11... | collective-permute-start | bytes 393224 | tf_op jit(solution)/shard_map/ppermute | solution.py:262
  (12 other events, 31.2 us)
Sparse Core Ops, SparseCore 0:
  32.5 61.4 all-gather.2

commit v4 on v3

--- a/solution.py
+++ b/solution.py
@@ -8,9 +8,9 @@
 from jax.sharding import Mesh
 from jax.sharding import PartitionSpec as P
 
+
 HD = 128
 REACH = 4
-PROWS = 8
 PCOLS = 8
 PCH = 256
 CMID = 128
@@ -177,14 +177,13 @@
             out[n] = total
 
 
-def grad_kernel(flags, w, own, other, mine, theirs):
-    core = flags[1]
-    for m, out in ((core, mine), (1 - core, theirs)):
+def grad_kernel(flags, w, own, other, out):
+    for m in range(2):
         for n in range(2):
             t = jnp.zeros((TOK, TOK), f32)
             for p in range(3):
                 t = t + nt(w[m, :, p].reshape(TOK, TOK), paired(flags, own[p], other[p])[n])
-            out[0, :, n * TOK : (n + 1) * TOK] = t.astype(bf16)
+            out[m, :, n * TOK : (n + 1) * TOK] = t.astype(bf16)
 
 
 def conv_kernel(scalars, pieces, k2, slope, left, out):
@@ -274,10 +273,6 @@
     return exchanged(jnp.broadcast_to(value, (lax.axis_size(axis), *value.shape)), axis)
 
 
-def summed_low(pieces):
-    return jnp.sum(pieces.astype(f32), axis=0).astype(bf16)
-
-
 def adam_update(param, mean, square, grad):
     new_mean = beta_one * mean + (1.0 - beta_one) * grad
     new_square = beta_two * square + (1.0 - beta_two) * grad * grad
@@ -356,18 +351,20 @@
         [pltpu.VMEM((REACH + 1, TOK, TOK), f32)],
     )(meta, queries, out_grad, keys, values, *earlier)
 
-    quad = once_here(sent_to_all(qkv_weight, "yh"), earlier[0])
+    quad = sent_to_all(qkv_weight, "yh")
+    quad = once_here(quad, earlier[0])
     weights = lax.all_gather(quad, "z", axis=0)
     slot_rows = jnp.concatenate(
         [conv_input.reshape(PCOLS, CIN), pre_act.reshape(PCOLS, CMID)], axis=1
     )
     slot_rows = jnp.concatenate([slot_rows, kernel_second.astype(bf16)], axis=0)
-    along_z = sent_to_all(once_here(slot_rows, earlier[1]), "z")
+    along_z = sent_to_all(once_here(slot_rows, quad), "z")
+    along_z = once_here(along_z, earlier[1])
     kernel_rows = lax.dynamic_index_in_dim(along_z[:, PCOLS:], head_index, 0, keepdims=False)
     slot_rows = along_z[:, :PCOLS].reshape(64, PCH)
     along_y = jnp.concatenate([slot_rows, kernel_rows], axis=0)
-    along_y = sent_to_all(once_here(along_y, earlier[2]), TALL)
-    along_y = once_here(along_y, stats)
+    along_y = sent_to_all(along_y, TALL)
+    along_y = once_here(along_y, earlier[2])
     kernel_mine = along_y[:, 64:].reshape(16, 9, PCH).transpose(1, 0, 2)
     slot = pick_entry(slab_owner, device_index)
     my_rows = along_y[:, :64].reshape(8, 8, PCOLS, PCH)
@@ -404,14 +401,9 @@
 
     image_other = swapped(image_grads)
     grads_other = swapped(once_here(grads, image_other))
-    core = head_index % 2
-    flags = jnp.stack([side.astype(jnp.int32), core.astype(jnp.int32)])
-
-    def in_order(own, other):
-        return jnp.where(side == 0, own, other), jnp.where(side == 0, other, own)
+    flags = side.astype(jnp.int32)[None]
 
     weight_block = pl.BlockSpec((2, 4, 3, 64, TOK), lambda i: (i, 0, 0, 0, 0))
-    out_block = pl.BlockSpec((1, TOK, 2 * TOK), lambda i: (i, 0, 0))
 
     def fixed(*shape):
         return pl.BlockSpec(shape, lambda i: (0,) * len(shape))
@@ -432,9 +424,16 @@
     )(flags, weights, image_grads, image_other, along_head)
     pieces = exchanged(pieces.reshape(16, IMGTOK, PCH), ("head", "yl"))
 
-    mine, theirs = pl.pallas_call(
+    present = jnp.stack([head_index.astype(jnp.int32), present.astype(jnp.int32)])
+    partial = on_chip(conv_kernel, spec_of((64, 7, 128), bf16), 5, scalars=1)(
+        present, pieces, kernel_mine, slope, left
+    )
+
+    owned = exchanged(partial, WIDE)
+
+    halves = pl.pallas_call(
         grad_kernel,
-        out_shape=[spec_of((4, TOK, 2 * TOK), bf16)] * 2,
+        out_shape=spec_of((8, TOK, 2 * TOK), bf16),
         grid=(4,),
         in_specs=[
             whole(pltpu.SMEM),
@@ -442,37 +441,18 @@
             fixed(3, TOK, TOK),
             fixed(3, TOK, TOK),
         ],
-        out_specs=[out_block] * 2,
+        out_specs=pl.BlockSpec((2, TOK, 2 * TOK), lambda i: (i, 0, 0)),
     )(flags, weights, grads, grads_other)
-    pieces, theirs, left, slope, kernel_mine = lax.optimization_barrier(
-        (pieces, theirs, left, slope, kernel_mine)
-    )
-    arrived = lax.ppermute(theirs, "head", [(i, i ^ 1) for i in range(8)])
-
-    flags = jnp.stack([head_index.astype(jnp.int32), present.astype(jnp.int32)])
-    partial = on_chip(conv_kernel, spec_of((64, 7, 128), bf16), 5, scalars=1)(
-        flags, pieces, kernel_mine, slope, left
-    )
-
-    owned = exchanged(partial, WIDE)
-
-    chip = (mine.astype(f32) + arrived.astype(f32)).astype(bf16)
-    place_x = head_index // 2
-    total = lax.dynamic_index_in_dim(chip, place_x, 0, keepdims=False).astype(f32)
-    slices = [
-        lax.dynamic_index_in_dim(chip, (place_x + d) % 4, 0, keepdims=False) for d in range(1, 4)
-    ]
-    owned = jnp.sum(once_here(owned, slices).astype(f32), axis=0)
-    for d, piece in zip(range(1, 4), slices):
-        piece = lax.ppermute(piece, "head", [(i, (i + 2 * d) % 8) for i in range(8)])
-        total = total + piece.astype(f32)
+    owned = jnp.sum(once_here(owned, halves).astype(f32), axis=0)
+    summed = lax.psum_scatter(halves, "head", scatter_dimension=0)
 
     squares = jnp.broadcast_to(jnp.sum(owned * owned), (1, 128))
     squares = jnp.sum(sent_to_all(squares, WIDE), axis=0)
-    summed = total.astype(bf16)
-    summed, squares = lax.optimization_barrier((summed, squares))
-    mine, theirs = in_order(summed[:, :TOK], summed[:, TOK:])
-    even, odd = in_order(mine, swapped(theirs))
+    theirs = jnp.where(side == 0, summed[:, TOK:], summed[:, :TOK])
+    arrived = swapped(theirs)
+    mine = jnp.where(side == 0, summed[:, :TOK], summed[:, TOK:])
+    even = jnp.where(side == 0, mine, arrived)
+    odd = jnp.where(side == 0, arrived, mine)
     input_grad_t = jnp.stack([even.reshape(4, 64, TOK), odd.reshape(4, 64, TOK)], axis=1)
     input_grad_t = input_grad_t.reshape(512, TOK)
 
@@ -518,6 +498,7 @@
         P(WIDE, None),
         P(WIDE, None),
     )
+
     return jax.shard_map(
         shards,
         mesh=split,

time: 255 us -> 264 us (1.035)
  blocking collectives: 0 us -> 41.1 us
  starting transfers between devices: 130 us -> 92.6 us
  waiting for transfers between devices: 49.1 us -> 56.8 us
    all_to_all x0 -> x2, blocking collectives: none -> 41.1 us  [exchanged(): return lax.all_to_all(pieces, axis, split_axis=0, concat_axis=0, tiled=True)]
    all_to_all x8 -> x6, starting transfers between devices: 80.4 us -> 57.7 us  [exchanged(): return lax.all_to_all(pieces, axis, split_axis=0, concat_axis=0, tiled=True)]
    all_to_all x8 -> x6, waiting for transfers between devices: 17.3 us -> 31.1 us  [exchanged(): return lax.all_to_all(pieces, axis, split_axis=0, concat_axis=0, tiled=True)]
    ppermute x4 -> x0, starting transfers between devices: 12.8 us -> none  [the longest x3 9.89 us: shards(): lax.ppermute(piece, 'head', [(i, (i + 2 * d) % 8) for i in range(8)])]
    ppermute x3, waiting for transfers between devices: 12.5 us -> 5.49 us  [swapped(): return lax.ppermute(value, 'yl', [(0, 1), (1, 0)])]
  transfers between devices with their start and end apart: 28 -> 23, of which waited for: 11 -> 11; matrix products, arithmetic and copies ran while one was open for 8% -> 6% of each run, Pallas kernels for 9% -> 11%
where the time goes in v4:
time: 264 us; the launch traced here: 263 us
  starting transfers between devices  92.6 us (35%)
  waiting for transfers between devices  56.8 us (22%)
  blocking collectives  41.1 us (16%)
  Pallas kernels  28.1 us (11%)
  between operations  20.1 us (8%)
  local copies, waits for them, and re-layouts  13.6 us (5%)
  other arithmetic  10.5 us (4%)
    all_to_all x6, starting transfers between devices, exchanged(): return lax.all_to_all(pieces, axis, split_axis=0, concat_axis=0, tiled=True)  57.7 us
    all_to_all x2, blocking collectives, exchanged(): return lax.all_to_all(pieces, axis, split_axis=0, concat_axis=0, tiled=True)  41.1 us
    all_to_all x6, waiting for transfers between devices, exchanged(): return lax.all_to_all(pieces, axis, split_axis=0, concat_axis=0, tiled=True)  31.1 us
    ppermute x12, starting transfers between devices, passed_along(): return lax.ppermute(block, axis, route)  25.4 us
    ppermute x12, waiting for transfers between devices, passed_along(): return lax.ppermute(block, axis, route)  20.2 us
    ppermute x3, starting transfers between devices, swapped(): return lax.ppermute(value, 'yl', [(0, 1), (1, 0)])  9.55 us
    ppermute x3, waiting for transfers between devices, swapped(): return lax.ppermute(value, 'yl', [(0, 1), (1, 0)])  5.49 us
    pallas_call x1, Pallas kernels, shards(): pl.pallas_call(grad_kernel, out_shape=spec_of((8, TOK, 2 * TOK), bf16), g...  5.47 us
  transfers between devices with their start and end apart: 23, of which 11 were waited for; matrix products, arithmetic and copies ran while one was open for 6% of the time, Pallas kernels for 11%

profile of v4, /device:TPU:1, one launch (start us, length us, event | category | flops | bytes accessed | tf_op | source)
XLA Modules:
  0.0 262.8 jit_solution(15484591400770652493)
XLA Ops:
  7.2 1.7 broadcast_in_dim.72
  9.0 7.8 %all-to-all-start = ((bf16[4,3,64,256]{3,2,1,0:T(8,128)(2,1)}), bf16[4,3,64,256]{3,2,1,0:T(8,128)(2,1)S(1)}, u32[]{:S(2)}, u32[]{:S(2)}) async-start(bf16[4,3,64,256]{3,2,1,0:T(8,128)(2,1)} %broadcast_in_dim.72), calls=%async_computation | async-start | bytes 786432 | tf_op jit(solution)/shard_map/all_to_all | solution.py:269
  16.8 2.3 collective-permute-start
  19.2 1.3 collective-permute-start.1
  20.5 7.5 %collective-permute-done.b1 = bf16[2,256,256]{2,1,0:T(8,128)(2,1)S(1)} collective-permute-done((bf16[2,256,256]{2,1,0:T(8,128)(2,1)S(1)}, bf16[2,256,256]{2,1,0:T(8,128)(2,1)S(1)}, u32[]{:S(2)}, u32[]{:S(2)}) %collective-permute-start) | collective-permute-done | bytes 262176 | tf_op jit(solution)/shard_map/ppermute | solution.py:257
  28.0 3.7 %collective-permute-done.1.a1 = bf16[2,256,256]{2,1,0:T(8,128)(2,1)S(1)} collective-permute-done((bf16[2,256,256]{2,1,0:T(8,128)(2,1)S(1)}, bf16[2,256,256]{2,1,0:T(8,128)(2,1)S(1)}, u32[]{:S(2)}, u32[]{:S(2)}) %collective-permute-start.1) | collective-permute-done | bytes 262176 | tf_op jit(solution)/shard_map/ppermute | solution.py:257
  33.5 4.4 %collective-permute-start.2 = (bf16[2,256,256]{2,1,0:T(8,128)(2,1)S(1)}, bf16[2,256,256]{2,1,0:T(8,128)(2,1)S(1)}, u32[]{:S(2)}, u32[]{:S(2)}) collective-permute-start(bf16[2,256,256]{2,1,0:T(8,128)(2,1)S(1)} %collective-permute-done.b1), channel_id=1, source_target_pairs={{0,1},{1,2},{2,3},{3,4},{4,5},{5,6},{6,7},{7,8},{8,9},{9,10},{10,1... | collective-permute-start | bytes 786440 | tf_op jit(solution)/shard_map/ppermute | solution.py:257
  37.9 1.3 collective-permute-start.3
  42.8 3.6 %collective-permute-done.3.a2 = bf16[2,256,256]{2,1,0:T(8,128)(2,1)S(1)} collective-permute-done((bf16[2,256,256]{2,1,0:T(8,128)(2,1)S(1)}, bf16[2,256,256]{2,1,0:T(8,128)(2,1)S(1)}, u32[]{:S(2)}, u32[]{:S(2)}) %collective-permute-start.3) | collective-permute-done | bytes 262176 | tf_op jit(solution)/shard_map/ppermute | solution.py:257
  46.3 2.8 %collective-permute-start.4 = (bf16[2,256,256]{2,1,0:T(8,128)(2,1)S(1)}, bf16[2,256,256]{2,1,0:T(8,128)(2,1)S(1)}, u32[]{:S(2)}, u32[]{:S(2)}) collective-permute-start(bf16[2,256,256]{2,1,0:T(8,128)(2,1)S(1)} %collective-permute-done.2.b2), channel_id=1, source_target_pairs={{0,1},{1,2},{2,3},{3,4},{4,5},{5,6},{6,7},{7,8},{8,9},{9,10},{10,1... | collective-permute-start | bytes 786440 | tf_op jit(solution)/shard_map/ppermute | solution.py:257
  49.2 1.3 collective-permute-start.5
  51.4 1.1 collective-permute-done.4.b3
  52.5 4.2 %collective-permute-done.5.a3 = bf16[2,256,256]{2,1,0:T(8,128)(2,1)S(1)} collective-permute-done((bf16[2,256,256]{2,1,0:T(8,128)(2,1)S(1)}, bf16[2,256,256]{2,1,0:T(8,128)(2,1)S(1)}, u32[]{:S(2)}, u32[]{:S(2)}) %collective-permute-start.5) | collective-permute-done | bytes 262176 | tf_op jit(solution)/shard_map/ppermute | solution.py:257
  56.7 5.5 %collective-permute-start.6 = (bf16[2,256,256]{2,1,0:T(8,128)(2,1)S(1)}, bf16[2,256,256]{2,1,0:T(8,128)(2,1)S(1)}, u32[]{:S(2)}, u32[]{:S(2)}) collective-permute-start(bf16[2,256,256]{2,1,0:T(8,128)(2,1)S(1)} %collective-permute-done.4.b3), channel_id=1, source_target_pairs={{0,1},{1,2},{2,3},{3,4},{4,5},{5,6},{6,7},{7,8},{8,9},{9,10},{10,1... | collective-permute-start | bytes 786440 | tf_op jit(solution)/shard_map/ppermute | solution.py:257
  62.2 1.3 collective-permute-start.7
  64.2 17.7 %all-to-all-start.1 = ((bf16[8,26,256]{2,1,0:T(8,128)(2,1)}), bf16[8,26,256]{2,1,0:T(8,128)(2,1)S(1)}, u32[]{:S(2)}, u32[]{:S(2)}) async-start(bf16[8,26,256]{2,1,0:T(8,128)(2,1)} %broadcast_in_dim.80), calls=%async_computation.2 | async-start | bytes 262144 | tf_op jit(solution)/shard_map/all_to_all | solution.py:269
  82.6 3.7 %shard_map.225.stats = f32[8,256]{1,0:T(8,128)} custom-call(s32[8,256]{1,0:T(8,128)} %add_subtract_fusion.meta, bf16[256,256]{1,0:T(8,128)(2,1)} %q.3, bf16[256,256]{1,0:T(8,128)(2,1)} %g.3, bf16[256,256]{1,0:T(8,128)(2,1)} %k0.5, bf16[256,256]{1,0:T(8,128)(2,1)} %v0.5, bf16[2,256,256]{2,1,0:T(8,128)(2,1)} %copy-done.7, bf16[2,256,256]{2,1,0:T(8,128)(2,1)} %copy-done.8, ...), custom_call_target="tpu_custom_call" | custom-call | tf_op jit(solution)/shard_map/pallas_call | solution.py:347
  86.3 1.3 collective-permute-start.10
  87.6 1.3 collective-permute-start.11
  88.9 1.3 collective-permute-start.8
  90.2 1.3 collective-permute-start.9
  91.6 5.2 %shard_map.226 = (bf16[256,256]{1,0:T(8,128)(2,1)}, f32[256,256]{1,0:T(8,128)}, f32[256,256]{1,0:T(8,128)}) custom-call(s32[8,256]{1,0:T(8,128)} %add_subtract_fusion.meta, f32[8,256]{1,0:T(8,128)} %shard_map.225.stats, bf16[256,256]{1,0:T(8,128)(2,1)} %q.3, bf16[256,256]{1,0:T(8,128)(2,1)} %g.3, bf16[256,256]{1,0:T(8,128)(2,1)} %k0.5, bf16[256,256]{1,0:T(8,128)(2,1)} %v0.5, ...), custom_call_target="tpu_custom_call" | custom-call | tf_op jit(solution)/shard_map/pallas_call | solution.py:390
  97.4 5.1 %shard_map.227 = (bf16[3,256,256]{2,1,0:T(8,128)(2,1)}, bf16[3,64,256]{2,1,0:T(8,128)(2,1)}) custom-call(s32[1]{0:T(128)} %bitcast.6.start, s32[8,256]{1,0:T(8,128)} %add_subtract_fusion.meta, bf16[256,256]{1,0:T(8,128)(2,1)} %k0.5, bf16[256,256]{1,0:T(8,128)(2,1)} %v0.5, bf16[2,256,256]{2,1,0:T(8,128)(2,1)} %copy-done.12, bf16[2,256,256]{2,1,0:T(8,128)(2,1)} %copy-done.13, ...), custom_call_target="tpu_custom_call" | custom-call | tf_op jit(solution)/shard_map/pallas_call | solution.py:395
  102.5 4.0 %collective-permute-start.12 = (bf16[3,64,256]{2,1,0:T(8,128)(2,1)}, bf16[3,64,256]{2,1,0:T(8,128)(2,1)S(1)}, u32[]{:S(2)}, u32[]{:S(2)}) collective-permute-start(bf16[3,64,256]{2,1,0:T(8,128)(2,1)} %get-tuple-element.41.own), channel_id=1, source_target_pairs={{0,1},{1,0},{2,3},{3,2},{4,5},{5,4},{6,7},{7,6},{8,9},{9,8},{10,11... | collective-permute-start | bytes 294920 | tf_op jit(solution)/shard_map/ppermute | solution.py:261
  106.6 2.2 collective-permute-done.12.other
  108.7 3.4 %collective-permute-start.13 = (bf16[3,256,256]{2,1,0:T(8,128)(2,1)}, bf16[3,256,256]{2,1,0:T(8,128)(2,1)S(1)}, u32[]{:S(2)}, u32[]{:S(2)}) collective-permute-start(bf16[3,256,256]{2,1,0:T(8,128)(2,1)} %get-tuple-element.42.own), channel_id=1, source_target_pairs={{0,1},{1,0},{2,3},{3,2},{4,5},{5,4},{6,7},{7,6},{8,9},{9,8},{10,11... | collective-permute-start | bytes 1179656 | tf_op jit(solution)/shard_map/ppermute | solution.py:261
  112.1 0.8 broadcast_in_dim.81
  112.9 8.9 %all-to-all-start.2 = ((bf16[8,82,256]{2,1,0:T(8,128)(2,1)}), bf16[8,82,256]{2,1,0:T(8,128)(2,1)S(1)}, u32[]{:S(2)}, u32[]{:S(2)}) async-start(bf16[8,82,256]{2,1,0:T(8,128)(2,1)} %broadcast_in_dim.81), calls=%async_computation.3 | async-start | bytes 720896 | tf_op jit(solution)/shard_map/all_to_all | solution.py:269
  122.6 5.5 %shard_map.228 = bf16[8,256,512]{2,1,0:T(8,128)(2,1)} custom-call(s32[1]{0:T(128)} %bitcast.flags, bf16[8,4,3,64,256]{4,3,2,1,0:T(8,128)(2,1)} %bitcast.51, bf16[3,256,256]{2,1,0:T(8,128)(2,1)} %get-tuple-element.42.own, bf16[3,256,256]{2,1,0:T(8,128)(2,1)} %copy-done.11), custom_call_target="tpu_custom_call" | custom-call | tf_op jit(solution)/shard_map/pallas_call | solution.py:434
  130.8 2.3 all-to-all-done.2
  133.5 1.1 broadcast_in_dim.82
  134.6 12.4 %all-to-all-start.3 = ((bf16[8,264,256]{2,1,0:T(8,128)(2,1)}), bf16[8,264,256]{2,1,0:T(8,128)(2,1)S(1)}, u32[]{:S(2)}, u32[]{:S(2)}) async-start(bf16[8,264,256]{2,1,0:T(8,128)(2,1)} %broadcast_in_dim.82), calls=%async_computation.4 | async-start | bytes 2162688 | tf_op jit(solution)/shard_map/all_to_all | solution.py:269
  147.0 17.8 %all-to-all-done.3.pw = bf16[8,264,256]{2,1,0:T(8,128)(2,1)S(1)} async-done(((bf16[8,264,256]{2,1,0:T(8,128)(2,1)}), bf16[8,264,256]{2,1,0:T(8,128)(2,1)S(1)}, u32[]{:S(2)}, u32[]{:S(2)}) %all-to-all-start.3) | async-done | bytes 1081376 | tf_op jit(solution)/shard_map/all_to_all | solution.py:269
  164.9 1.0 copy-done
  165.9 4.9 %shard_map.229 = bf16[8,128,256]{2,1,0:T(8,128)(2,1)} custom-call(s32[1]{0:T(128)} %bitcast.flags, bf16[8,4,3,64,256]{4,3,2,1,0:T(8,128)(2,1)} %bitcast.52, bf16[3,64,256]{2,1,0:T(8,128)(2,1)} %get-tuple-element.41.own, bf16[3,64,256]{2,1,0:T(8,128)(2,1)} %copy-done.18, bf16[8,264,256]{2,1,0:T(8,128)(2,1)} %copy-done), custom_call_target="tpu_custom_call" | custom-call | tf_op jit(solution)/shard_map/pallas_call | solution.py:411
  170.8 4.9 %all-to-all-start.4 = ((bf16[16,64,256]{2,1,0:T(8,128)(2,1)}), bf16[16,64,256]{2,1,0:T(8,128)(2,1)S(1)}, u32[]{:S(2)}, u32[]{:S(2)}) async-start(bf16[16,64,256]{2,1,0:T(8,128)(2,1)} %bitcast.53), calls=%async_computation.5 | async-start | bytes 1048576 | tf_op jit(solution)/shard_map/all_to_all | solution.py:269
  175.7 1.3 pad_add_fusion.scalars
  180.1 6.2 %all-to-all-done.4.pieces = bf16[16,64,256]{2,1,0:T(8,128)(2,1)S(1)} async-done(((bf16[16,64,256]{2,1,0:T(8,128)(2,1)}), bf16[16,64,256]{2,1,0:T(8,128)(2,1)S(1)}, u32[]{:S(2)}, u32[]{:S(2)}) %all-to-all-start.4) | async-done | bytes 524320 | tf_op jit(solution)/shard_map/all_to_all | solution.py:269
  186.3 0.8 copy-done.3
  187.1 3.6 %shard_map.230 = bf16[64,7,128]{2,1,0:T(8,128)(2,1)} custom-call(s32[2]{0:T(128)} %pad_add_fusion.scalars, bf16[16,64,256]{2,1,0:T(8,128)(2,1)} %copy-done.3, bf16[9,16,256]{2,1,0:T(8,128)(2,1)} %bitcast.66, f32[64,16]{1,0:T(8,128)} %fusion.1.slope, bf16[4,64,64]{2,1,0:T(8,128)(2,1)} %maximum_bitcast_fusion.left), custom_call_target="tpu_custom_call" | custom-call | tf_op jit(solution)/shard_map/pallas_call | solution.py:428
  190.7 26.0 %all_to_all.40 = bf16[64,7,128]{2,1,0:T(8,128)(2,1)S(1)} all-to-all(bf16[64,7,128]{2,1,0:T(8,128)(2,1)} %shard_map.230), channel_id=1, replica_groups=mesh['head'=8,'z'=8,'yh'=4,'yl'=2] {'z','yh','yl'}, dimensions={0} | all-to-all | bytes 229376 | tf_op jit(solution)/shard_map/all_to_all | solution.py:269
  218.1 15.1 %all_to_all.41 = f32[64,1,128]{2,1,0:T(1,128)S(1)} all-to-all(f32[64,1,128]{2,1,0:T(1,128)S(1)} %broadcast_in_dim_broadcast_in_dim.3), channel_id=1, replica_groups=mesh['head'=8,'z'=8,'yh'=4,'yl'=2] {'z','yh','yl'}, dimensions={0} | all-to-all | bytes 65536 | tf_op jit(solution)/shard_map/all_to_all | solution.py:269
  233.8 5.9 %all-to-all-start.7 = ((f32[8,8,128]{2,1,0:T(8,128)}), f32[8,8,128]{2,1,0:T(8,128)S(1)}, u32[]{:S(2)}, u32[]{:S(2)}) async-start(f32[8,8,128]{2,1,0:T(8,128)} %broadcast_in_dim.83), calls=%async_computation.8 | async-start | bytes 65536 | tf_op jit(solution)/shard_map/all_to_all | solution.py:269
  239.7 4.7 %all-to-all-done.7 = f32[8,8,128]{2,1,0:T(8,128)S(1)} async-done(((f32[8,8,128]{2,1,0:T(8,128)}), f32[8,8,128]{2,1,0:T(8,128)S(1)}, u32[]{:S(2)}, u32[]{:S(2)}) %all-to-all-start.7) | async-done | bytes 32800 | tf_op jit(solution)/shard_map/all_to_all | solution.py:269
  247.0 1.0 broadcast_select_fusion.2
  248.0 2.2 collective-permute-start.14
  250.9 3.3 %collective-permute-done.14 = bf16[256,256]{1,0:T(8,128)(2,1)S(1)} collective-permute-done((bf16[256,256]{1,0:T(8,128)(2,1)S(1)}, bf16[256,256]{1,0:T(8,128)(2,1)S(1)}, u32[]{:S(2)}, u32[]{:S(2)}) %collective-permute-start.14) | collective-permute-done | bytes 131104 | tf_op jit(solution)/shard_map/ppermute | solution.py:261
  254.2 1.0 broadcast_select_fusion.1
  (143 shorter events, 15.6 us)
Async XLA Ops:
  7.2 9.6 %copy-start.1 = (bf16[256,256]{1,0:T(8,128)(2,1)S(1)}, bf16[256,256]{1,0:T(8,128)(2,1)}, u32[]{:S(2)}) copy-start(bf16[256,256]{1,0:T(8,128)(2,1)} %k0.5) | copy-start | bytes 393220
  7.2 9.6 %copy-start.2 = (bf16[256,256]{1,0:T(8,128)(2,1)S(1)}, bf16[256,256]{1,0:T(8,128)(2,1)}, u32[]{:S(2)}) copy-start(bf16[256,256]{1,0:T(8,128)(2,1)} %v0.5) | copy-start | bytes 393220
  7.2 12.0 %copy-start.6 = (bf16[256,256]{1,0:T(8,128)(2,1)S(1)}, bf16[256,256]{1,0:T(8,128)(2,1)}, u32[]{:S(2)}) copy-start(bf16[256,256]{1,0:T(8,128)(2,1)} %q.3) | copy-start | bytes 393220
  7.2 12.0 %copy-start.5 = (bf16[256,256]{1,0:T(8,128)(2,1)S(1)}, bf16[256,256]{1,0:T(8,128)(2,1)}, u32[]{:S(2)}) copy-start(bf16[256,256]{1,0:T(8,128)(2,1)} %g.3) | copy-start | bytes 393220
  9.0 23.6 %copy-start.30 = (s32[64]{0:T(128)S(1)}, s32[64]{0:T(128)}, u32[]{:S(2)}) copy-start(s32[64]{0:T(128)} %param.26) | copy-start | bytes 772
  9.0 23.6 %copy-start.31 = (s32[64]{0:T(128)S(1)}, s32[64]{0:T(128)}, u32[]{:S(2)}) copy-start(s32[64]{0:T(128)} %param.24) | copy-start | bytes 772
  9.0 24.3 %copy-start.33 = (s32[32]{0:T(128)S(1)}, s32[32]{0:T(128)}, u32[]{:S(2)}) copy-start(s32[32]{0:T(128)} %param.23) | copy-start | bytes 388
  9.0 30.3 %copy-start.32 = (s32[64]{0:T(128)S(1)}, s32[64]{0:T(128)}, u32[]{:S(2)}) copy-start(s32[64]{0:T(128)} %param.25) | copy-start | bytes 772
  9.0 41.7 %copy-start.17 = (f32[18,256]{1,0:T(8,128)S(1)}, f32[18,256]{1,0:T(8,128)}, u32[]{:S(2)}) copy-start(f32[18,256]{1,0:T(8,128)} %param.31) | copy-start | bytes 55300
  9.0 54.5 %copy-start.28 = (bf16[1,1,8,128]{3,2,1,0:T(8,128)(2,1)S(1)}, bf16[1,1,8,128]{3,2,1,0:T(8,128)(2,1)}, u32[]{:S(2)}) copy-start(bf16[1,1,8,128]{3,2,1,0:T(8,128)(2,1)} %param.29) | copy-start | bytes 6148
  9.0 54.5 %copy-start.29 = (bf16[1,1,8,128]{3,2,1,0:T(8,128)(2,1)S(1)}, bf16[1,1,8,128]{3,2,1,0:T(8,128)(2,1)}, u32[]{:S(2)}) copy-start(bf16[1,1,8,128]{3,2,1,0:T(8,128)(2,1)} %param.28) | copy-start | bytes 6148
  9.0 22.7 %all-to-all-start = ((bf16[4,3,64,256]{3,2,1,0:T(8,128)(2,1)}), bf16[4,3,64,256]{3,2,1,0:T(8,128)(2,1)S(1)}, u32[]{:S(2)}, u32[]{:S(2)}) async-start(bf16[4,3,64,256]{3,2,1,0:T(8,128)(2,1)} %broadcast_in_dim.72), calls=%async_computation | async-start | bytes 786432 | tf_op jit(solution)/shard_map/all_to_all | solution.py:269
  16.8 105.1 %all-gather.3.cloned.1.call-start = ((), (), s32[]{:S(2)}) async-start(), calls=%async_computation.10 | async-start | bytes 3538944 | tf_op jit(solution)/shard_map/all_gather | solution.py:356
  16.8 11.2 %collective-permute-start = (bf16[2,256,256]{2,1,0:T(8,128)(2,1)S(1)}, bf16[2,256,256]{2,1,0:T(8,128)(2,1)S(1)}, u32[]{:S(2)}, u32[]{:S(2)}) collective-permute-start(bf16[2,256,256]{2,1,0:T(8,128)(2,1)S(1)} %pad_maximum_fusion), channel_id=1, source_target_pairs={{0,1},{1,2},{2,3},{3,4},{4,5},{5,6},{6,7},{7,8},{8,9},{9,10},{10,1... | collective-permute-start | bytes 786440 | tf_op jit(solution)/shard_map/ppermute | solution.py:257
  19.2 12.5 %collective-permute-start.1 = (bf16[2,256,256]{2,1,0:T(8,128)(2,1)S(1)}, bf16[2,256,256]{2,1,0:T(8,128)(2,1)S(1)}, u32[]{:S(2)}, u32[]{:S(2)}) collective-permute-start(bf16[2,256,256]{2,1,0:T(8,128)(2,1)S(1)} %pad_maximum_fusion.1), channel_id=1, source_target_pairs={{1,0},{2,1},{3,2},{4,3},{5,4},{6,5},{7,6},{8,7},{9,8},{10,9},{11,1... | collective-permute-start | bytes 786440 | tf_op jit(solution)/shard_map/ppermute | solution.py:257
  28.0 53.9 %copy-start.7 = (bf16[2,256,256]{2,1,0:T(8,128)(2,1)}, bf16[2,256,256]{2,1,0:T(8,128)(2,1)S(1)}, u32[]{:S(2)}) copy-start(bf16[2,256,256]{2,1,0:T(8,128)(2,1)S(1)} %collective-permute-done.b1) | copy-start | bytes 786436
  31.7 65.1 %copy-start.12 = (bf16[2,256,256]{2,1,0:T(8,128)(2,1)}, bf16[2,256,256]{2,1,0:T(8,128)(2,1)S(1)}, u32[]{:S(2)}) copy-start(bf16[2,256,256]{2,1,0:T(8,128)(2,1)S(1)} %collective-permute-done.1.a1) | copy-start | bytes 786436
  33.5 9.2 %collective-permute-start.2 = (bf16[2,256,256]{2,1,0:T(8,128)(2,1)S(1)}, bf16[2,256,256]{2,1,0:T(8,128)(2,1)S(1)}, u32[]{:S(2)}, u32[]{:S(2)}) collective-permute-start(bf16[2,256,256]{2,1,0:T(8,128)(2,1)S(1)} %collective-permute-done.b1), channel_id=1, source_target_pairs={{0,1},{1,2},{2,3},{3,4},{4,5},{5,6},{6,7},{7,8},{8,9},{9,10},{10,1... | collective-permute-start | bytes 786440 | tf_op jit(solution)/shard_map/ppermute | solution.py:257
  37.9 8.4 %collective-permute-start.3 = (bf16[2,256,256]{2,1,0:T(8,128)(2,1)S(1)}, bf16[2,256,256]{2,1,0:T(8,128)(2,1)S(1)}, u32[]{:S(2)}, u32[]{:S(2)}) collective-permute-start(bf16[2,256,256]{2,1,0:T(8,128)(2,1)S(1)} %collective-permute-done.1.a1), channel_id=1, source_target_pairs={{1,0},{2,1},{3,2},{4,3},{5,4},{6,5},{7,6},{8,7},{9,8},{10,9},{11,1... | collective-permute-start | bytes 786440 | tf_op jit(solution)/shard_map/ppermute | solution.py:257
  42.7 39.2 %copy-start.8 = (bf16[2,256,256]{2,1,0:T(8,128)(2,1)}, bf16[2,256,256]{2,1,0:T(8,128)(2,1)S(1)}, u32[]{:S(2)}) copy-start(bf16[2,256,256]{2,1,0:T(8,128)(2,1)S(1)} %collective-permute-done.2.b2) | copy-start | bytes 786436
  46.3 50.5 %copy-start.13 = (bf16[2,256,256]{2,1,0:T(8,128)(2,1)}, bf16[2,256,256]{2,1,0:T(8,128)(2,1)S(1)}, u32[]{:S(2)}) copy-start(bf16[2,256,256]{2,1,0:T(8,128)(2,1)S(1)} %collective-permute-done.3.a2) | copy-start | bytes 786436
  46.3 6.1 %collective-permute-start.4 = (bf16[2,256,256]{2,1,0:T(8,128)(2,1)S(1)}, bf16[2,256,256]{2,1,0:T(8,128)(2,1)S(1)}, u32[]{:S(2)}, u32[]{:S(2)}) collective-permute-start(bf16[2,256,256]{2,1,0:T(8,128)(2,1)S(1)} %collective-permute-done.2.b2), channel_id=1, source_target_pairs={{0,1},{1,2},{2,3},{3,4},{4,5},{5,6},{6,7},{7,8},{8,9},{9,10},{10,1... | collective-permute-start | bytes 786440 | tf_op jit(solution)/shard_map/ppermute | solution.py:257
  49.2 7.5 %collective-permute-start.5 = (bf16[2,256,256]{2,1,0:T(8,128)(2,1)S(1)}, bf16[2,256,256]{2,1,0:T(8,128)(2,1)S(1)}, u32[]{:S(2)}, u32[]{:S(2)}) collective-permute-start(bf16[2,256,256]{2,1,0:T(8,128)(2,1)S(1)} %collective-permute-done.3.a2), channel_id=1, source_target_pairs={{1,0},{2,1},{3,2},{4,3},{5,4},{6,5},{7,6},{8,7},{9,8},{10,9},{11,1... | collective-permute-start | bytes 786440 | tf_op jit(solution)/shard_map/ppermute | solution.py:257
  52.5 29.5 %copy-start.9 = (bf16[2,256,256]{2,1,0:T(8,128)(2,1)}, bf16[2,256,256]{2,1,0:T(8,128)(2,1)S(1)}, u32[]{:S(2)}) copy-start(bf16[2,256,256]{2,1,0:T(8,128)(2,1)S(1)} %collective-permute-done.4.b3) | copy-start | bytes 786436
  56.7 40.2 %copy-start.14 = (bf16[2,256,256]{2,1,0:T(8,128)(2,1)}, bf16[2,256,256]{2,1,0:T(8,128)(2,1)S(1)}, u32[]{:S(2)}) copy-start(bf16[2,256,256]{2,1,0:T(8,128)(2,1)S(1)} %collective-permute-done.5.a3) | copy-start | bytes 786436
  56.7 25.2 %collective-permute-start.6 = (bf16[2,256,256]{2,1,0:T(8,128)(2,1)S(1)}, bf16[2,256,256]{2,1,0:T(8,128)(2,1)S(1)}, u32[]{:S(2)}, u32[]{:S(2)}) collective-permute-start(bf16[2,256,256]{2,1,0:T(8,128)(2,1)S(1)} %collective-permute-done.4.b3), channel_id=1, source_target_pairs={{0,1},{1,2},{2,3},{3,4},{4,5},{5,6},{6,7},{7,8},{8,9},{9,10},{10,1... | collective-permute-start | bytes 786440 | tf_op jit(solution)/shard_map/ppermute | solution.py:257
  62.2 19.7 %collective-permute-start.7 = (bf16[2,256,256]{2,1,0:T(8,128)(2,1)S(1)}, bf16[2,256,256]{2,1,0:T(8,128)(2,1)S(1)}, u32[]{:S(2)}, u32[]{:S(2)}) collective-permute-start(bf16[2,256,256]{2,1,0:T(8,128)(2,1)S(1)} %collective-permute-done.5.a3), channel_id=1, source_target_pairs={{1,0},{2,1},{3,2},{4,3},{5,4},{6,5},{7,6},{8,7},{9,8},{10,9},{11,1... | collective-permute-start | bytes 786440 | tf_op jit(solution)/shard_map/ppermute | solution.py:257
  64.2 27.4 %all-to-all-start.1 = ((bf16[8,26,256]{2,1,0:T(8,128)(2,1)}), bf16[8,26,256]{2,1,0:T(8,128)(2,1)S(1)}, u32[]{:S(2)}, u32[]{:S(2)}) async-start(bf16[8,26,256]{2,1,0:T(8,128)(2,1)} %broadcast_in_dim.80), calls=%async_computation.2 | async-start | bytes 262144 | tf_op jit(solution)/shard_map/all_to_all | solution.py:269
  82.6 14.1 %copy-start.15 = (bf16[2,256,256]{2,1,0:T(8,128)(2,1)}, bf16[2,256,256]{2,1,0:T(8,128)(2,1)S(1)}, u32[]{:S(2)}) copy-start(bf16[2,256,256]{2,1,0:T(8,128)(2,1)S(1)} %collective-permute-done.7.a4) | copy-start | bytes 786436
  86.3 10.4 %collective-permute-start.10 = (f32[8,256]{1,0:T(8,128)}, f32[8,256]{1,0:T(8,128)S(1)}, u32[]{:S(2)}, u32[]{:S(2)}) collective-permute-start(f32[8,256]{1,0:T(8,128)} %shard_map.225.stats), channel_id=1, source_target_pairs={{3,0},{4,1},{5,2},{6,3},{7,4},{8,5},{9,6},{10,7},{11,8},{12,9},{13... | collective-permute-start | bytes 24584 | tf_op jit(solution)/shard_map/ppermute | solution.py:257
  87.6 9.1 %collective-permute-start.11 = (f32[8,256]{1,0:T(8,128)}, f32[8,256]{1,0:T(8,128)S(1)}, u32[]{:S(2)}, u32[]{:S(2)}) collective-permute-start(f32[8,256]{1,0:T(8,128)} %shard_map.225.stats), channel_id=1, source_target_pairs={{4,0},{5,1},{6,2},{7,3},{8,4},{9,5},{10,6},{11,7},{12,8},{13,9},{1... | collective-permute-start | bytes 24584 | tf_op jit(solution)/shard_map/ppermute | solution.py:257
  88.9 7.8 %collective-permute-start.8 = (f32[8,256]{1,0:T(8,128)}, f32[8,256]{1,0:T(8,128)S(1)}, u32[]{:S(2)}, u32[]{:S(2)}) collective-permute-start(f32[8,256]{1,0:T(8,128)} %shard_map.225.stats), channel_id=1, source_target_pairs={{1,0},{2,1},{3,2},{4,3},{5,4},{6,5},{7,6},{8,7},{9,8},{10,9},{11,1... | collective-permute-start | bytes 24584 | tf_op jit(solution)/shard_map/ppermute | solution.py:257
  90.2 6.6 %collective-permute-start.9 = (f32[8,256]{1,0:T(8,128)}, f32[8,256]{1,0:T(8,128)S(1)}, u32[]{:S(2)}, u32[]{:S(2)}) collective-permute-start(f32[8,256]{1,0:T(8,128)} %shard_map.225.stats), channel_id=1, source_target_pairs={{2,0},{3,1},{4,2},{5,3},{6,4},{7,5},{8,6},{9,7},{10,8},{11,9},{12,... | collective-permute-start | bytes 24584 | tf_op jit(solution)/shard_map/ppermute | solution.py:257
  102.5 6.2 %collective-permute-start.12 = (bf16[3,64,256]{2,1,0:T(8,128)(2,1)}, bf16[3,64,256]{2,1,0:T(8,128)(2,1)S(1)}, u32[]{:S(2)}, u32[]{:S(2)}) collective-permute-start(bf16[3,64,256]{2,1,0:T(8,128)(2,1)} %get-tuple-element.41.own), channel_id=1, source_target_pairs={{0,1},{1,0},{2,3},{3,2},{4,5},{5,4},{6,7},{7,6},{8,9},{9,8},{10,11... | collective-permute-start | bytes 294920 | tf_op jit(solution)/shard_map/ppermute | solution.py:261
  108.7 19.4 %copy-start.18 = (bf16[3,64,256]{2,1,0:T(8,128)(2,1)}, bf16[3,64,256]{2,1,0:T(8,128)(2,1)S(1)}, u32[]{:S(2)}) copy-start(bf16[3,64,256]{2,1,0:T(8,128)(2,1)S(1)} %collective-permute-done.12.other) | copy-start | bytes 294916
  108.7 13.2 %collective-permute-start.13 = (bf16[3,256,256]{2,1,0:T(8,128)(2,1)}, bf16[3,256,256]{2,1,0:T(8,128)(2,1)S(1)}, u32[]{:S(2)}, u32[]{:S(2)}) collective-permute-start(bf16[3,256,256]{2,1,0:T(8,128)(2,1)} %get-tuple-element.42.own), channel_id=1, source_target_pairs={{0,1},{1,0},{2,3},{3,2},{4,5},{5,4},{6,7},{7,6},{8,9},{9,8},{10,11... | collective-permute-start | bytes 1179656 | tf_op jit(solution)/shard_map/ppermute | solution.py:261
  112.9 20.3 %all-to-all-start.2 = ((bf16[8,82,256]{2,1,0:T(8,128)(2,1)}), bf16[8,82,256]{2,1,0:T(8,128)(2,1)S(1)}, u32[]{:S(2)}, u32[]{:S(2)}) async-start(bf16[8,82,256]{2,1,0:T(8,128)(2,1)} %broadcast_in_dim.81), calls=%async_computation.3 | async-start | bytes 720896 | tf_op jit(solution)/shard_map/all_to_all | solution.py:269
  121.8 125.2 %reduce-scatter.2.cloned.1.call-start = ((), (), s32[]{:S(2)}) async-start(), calls=%async_computation.9 | async-start | bytes 2359296 | tf_op jit(solution)/shard_map/reduce_scatter | solution.py:447
  128.1 2.5 copy-start.16
  134.6 30.3 %all-to-all-start.3 = ((bf16[8,264,256]{2,1,0:T(8,128)(2,1)}), bf16[8,264,256]{2,1,0:T(8,128)(2,1)S(1)}, u32[]{:S(2)}, u32[]{:S(2)}) async-start(bf16[8,264,256]{2,1,0:T(8,128)(2,1)} %broadcast_in_dim.82), calls=%async_computation.4 | async-start | bytes 2162688 | tf_op jit(solution)/shard_map/all_to_all | solution.py:269
  170.8 15.5 %all-to-all-start.4 = ((bf16[16,64,256]{2,1,0:T(8,128)(2,1)}), bf16[16,64,256]{2,1,0:T(8,128)(2,1)S(1)}, u32[]{:S(2)}, u32[]{:S(2)}) async-start(bf16[16,64,256]{2,1,0:T(8,128)(2,1)} %bitcast.53), calls=%async_computation.5 | async-start | bytes 1048576 | tf_op jit(solution)/shard_map/all_to_all | solution.py:269
  187.1 59.3 %copy-start.19 = (f32[18,256]{1,0:T(8,128)S(1)}, f32[18,256]{1,0:T(8,128)}, u32[]{:S(2)}) copy-start(f32[18,256]{1,0:T(8,128)} %param.33) | copy-start | bytes 55300
  187.1 59.3 %copy-start.20 = (f32[18,256]{1,0:T(8,128)S(1)}, f32[18,256]{1,0:T(8,128)}, u32[]{:S(2)}) copy-start(f32[18,256]{1,0:T(8,128)} %param.35) | copy-start | bytes 55300
  190.7 59.5 %copy-start.21 = (f32[18,128]{1,0:T(8,128)S(1)}, f32[18,128]{1,0:T(8,128)}, u32[]{:S(2)}) copy-start(f32[18,128]{1,0:T(8,128)} %param.30) | copy-start | bytes 27652
  190.7 59.5 %copy-start.22 = (f32[18,128]{1,0:T(8,128)S(1)}, f32[18,128]{1,0:T(8,128)}, u32[]{:S(2)}) copy-start(f32[18,128]{1,0:T(8,128)} %param.32) | copy-start | bytes 27652
  190.7 59.6 %copy-start.23 = (f32[18,128]{1,0:T(8,128)S(1)}, f32[18,128]{1,0:T(8,128)}, u32[]{:S(2)}) copy-start(f32[18,128]{1,0:T(8,128)} %param.34) | copy-start | bytes 27652
  233.8 10.6 %all-to-all-start.7 = ((f32[8,8,128]{2,1,0:T(8,128)}), f32[8,8,128]{2,1,0:T(8,128)S(1)}, u32[]{:S(2)}, u32[]{:S(2)}) async-start(f32[8,8,128]{2,1,0:T(8,128)} %broadcast_in_dim.83), calls=%async_computation.8 | async-start | bytes 65536 | tf_op jit(solution)/shard_map/all_to_all | solution.py:269
  248.0 6.2 %collective-permute-start.14 = (bf16[256,256]{1,0:T(8,128)(2,1)S(1)}, bf16[256,256]{1,0:T(8,128)(2,1)S(1)}, u32[]{:S(2)}, u32[]{:S(2)}) collective-permute-start(bf16[256,256]{1,0:T(8,128)(2,1)S(1)} %broadcast_select_fusion.2), channel_id=1, source_target_pairs={{0,1},{1,0},{2,3},{3,2},{4,5},{5,4},{6,7},{7,6},{8,9},{9,8},{10,11... | collective-permute-start | bytes 393224 | tf_op jit(solution)/shard_map/ppermute | solution.py:261
  (9 other events, 6.4 us)
Sparse Core Ops, SparseCore 0:
  32.6 66.5 all-gather.2
  128.3 51.9 reduce-scatter.1

commit v5 on v4

--- a/solution.py
+++ b/solution.py
@@ -186,7 +186,7 @@
             out[m, :, n * TOK : (n + 1) * TOK] = t.astype(bf16)
 
 
-def conv_kernel(scalars, pieces, k2, slope, left, out):
+def conv_kernel(scalars, pieces, k2, picture, out):
     head = scalars[0]
     present = scalars[1].astype(f32)
     total = jnp.zeros((IMGTOK, PCH), f32)
@@ -203,7 +203,12 @@
     dact = jnp.zeros((IMGTOK, 16), f32)
     for o in range(9):
         dact = dact + nt(nn(shifts[o], incoming).astype(bf16), k2[o])
-    dpre = (dact * slope[...]).astype(bf16)
+    pre = picture[:, CIN:].astype(f32)
+    sig = 1.0 / (1.0 + jnp.exp(-pre))
+    act = (pre * sig).astype(bf16)
+    slope = sig * (1.0 + pre * (1.0 - sig))
+    slope = pltpu.roll(slope, (CMID - 16 * head) % CMID, 1)[:, :16]
+    dpre = (dact * slope).astype(bf16)
     ch = lax.broadcasted_iota(jnp.int32, (PCH, LANES), 0)
     lane = lax.broadcasted_iota(jnp.int32, (PCH, LANES), 1)
     spread = jnp.where((lane < 576) & ((lane & 31) == ch - 32 * head), 1.0, 0.0).astype(bf16)
@@ -224,7 +229,11 @@
     result = jnp.zeros((IMGTOK, LANES), f32)
     for n in range(4):
         part = jnp.where((lane >= ends[n]) & (lane < ends[n + 1]), moved, zero)
-        result = result + nn(left[n], part)
+        row = lax.broadcasted_iota(jnp.int32, (64, CMID), 0)
+        col = lax.broadcasted_iota(jnp.int32, (64, CMID), 1)
+        own = jnp.where(col == 2 * row + n % 2, 1.0, 0.0).astype(bf16)
+        source = act if n < 2 else picture[:, :CIN]
+        result = result + nn(nt(own, source).astype(bf16), part)
     for n in range(7):
         out[:, n, :] = result[:, n * 128 : (n + 1) * 128].astype(bf16)
 
@@ -337,7 +346,7 @@
     for hop in range(REACH):
         before = passed_along(before, WIDE, 1)
         after = passed_along(after, WIDE, -1)
-        if hop == REACH - 2:
+        if hop == 0:
             before, after, meta = lax.optimization_barrier((before, after, meta))
         else:
             before, after = lax.optimization_barrier((before, after))
@@ -377,15 +386,6 @@
     along_head = sent_to_all(jnp.concatenate([half_patch, my_rows], axis=0), "head")
     picture = along_head[:, PCH:].reshape(IMGTOK, CIN + CMID)
 
-    conv_img = picture[:, :CIN]
-    pre_img = picture[:, CIN:].astype(f32)
-    act = jax.nn.silu(pre_img).astype(bf16)
-    left = jnp.concatenate([act.T.reshape(64, 2, 64), conv_img.T.reshape(64, 2, 64)], axis=1)
-    left = left.transpose(1, 0, 2)
-    sig = jax.nn.sigmoid(pre_img)
-    slope = sig * (1.0 + pre_img * (1.0 - sig))
-    slope = lax.dynamic_slice_in_dim(slope, head_index * 16, 16, 1)
-
     stats_later = [passed_along(stats, WIDE, -d) for d in range(1, REACH + 1)]
     dq, dk, dv = on_chip(
         own_kernel,
@@ -425,8 +425,8 @@
     pieces = exchanged(pieces.reshape(16, IMGTOK, PCH), ("head", "yl"))
 
     present = jnp.stack([head_index.astype(jnp.int32), present.astype(jnp.int32)])
-    partial = on_chip(conv_kernel, spec_of((64, 7, 128), bf16), 5, scalars=1)(
-        present, pieces, kernel_mine, slope, left
+    partial = on_chip(conv_kernel, spec_of((64, 7, 128), bf16), 4, scalars=1)(
+        present, pieces, kernel_mine, picture
     )
 
     owned = exchanged(partial, WIDE)

time: 264 us -> 262 us (level)
  blocking collectives: 41.1 us -> 71.7 us
  starting transfers between devices: 92.6 us -> 76 us
  waiting for transfers between devices: 56.8 us -> 42.9 us
  local copies, waits for them, and re-layouts: 13.6 us -> 10.9 us
    all_to_all x2 -> x3, blocking collectives: 41.1 us -> 71.7 us  [exchanged(): return lax.all_to_all(pieces, axis, split_axis=0, concat_axis=0, tiled=True)]
    all_to_all x6 -> x5, starting transfers between devices: 57.7 us -> 43.8 us  [exchanged(): return lax.all_to_all(pieces, axis, split_axis=0, concat_axis=0, tiled=True)]
    all_to_all x6 -> x5, waiting for transfers between devices: 31.1 us -> 21.4 us  [exchanged(): return lax.all_to_all(pieces, axis, split_axis=0, concat_axis=0, tiled=True)]
    ppermute x12, waiting for transfers between devices: 20.2 us -> 16 us  [passed_along(): return lax.ppermute(block, axis, route)]
    ppermute x12, starting transfers between devices: 25.4 us -> 22.6 us  [passed_along(): return lax.ppermute(block, axis, route)]
  transfers between devices with their start and end apart: 23 -> 22, of which waited for: 11 -> 10; matrix products, arithmetic and copies ran while one was open for 6% -> 6% of each run, Pallas kernels for 11% -> 11%
where the time goes in v5:
time: 262 us; the launch traced here: 260 us
  starting transfers between devices  76 us (29%)
  blocking collectives  71.7 us (27%)
  waiting for transfers between devices  42.9 us (16%)
  Pallas kernels  28.1 us (11%)
  between operations  19.9 us (8%)
  other arithmetic  11 us (4%)
  local copies, waits for them, and re-layouts  10.9 us (4%)
    all_to_all x3, blocking collectives, exchanged(): return lax.all_to_all(pieces, axis, split_axis=0, concat_axis=0, tiled=True)  71.7 us
    all_to_all x5, starting transfers between devices, exchanged(): return lax.all_to_all(pieces, axis, split_axis=0, concat_axis=0, tiled=True)  43.8 us
    ppermute x12, starting transfers between devices, passed_along(): return lax.ppermute(block, axis, route)  22.6 us
    all_to_all x5, waiting for transfers between devices, exchanged(): return lax.all_to_all(pieces, axis, split_axis=0, concat_axis=0, tiled=True)  21.4 us
    ppermute x12, waiting for transfers between devices, passed_along(): return lax.ppermute(block, axis, route)  16 us
    ppermute x3, starting transfers between devices, swapped(): return lax.ppermute(value, 'yl', [(0, 1), (1, 0)])  9.54 us
    ppermute x3, waiting for transfers between devices, swapped(): return lax.ppermute(value, 'yl', [(0, 1), (1, 0)])  5.49 us
    pallas_call x1, Pallas kernels, shards(): pl.pallas_call(grad_kernel, out_shape=spec_of((8, TOK, 2 * TOK), bf16), g...  5.43 us
  transfers between devices with their start and end apart: 22, of which 10 were waited for; matrix products, arithmetic and copies ran while one was open for 6% of the time, Pallas kernels for 11%

profile of v5, /device:TPU:1, one launch (start us, length us, event | category | flops | bytes accessed | tf_op | source)
XLA Modules:
  0.0 260.4 jit_solution(12379068201466666611)
XLA Ops:
  7.2 1.1 pad_maximum_fusion
  8.3 4.0 %collective-permute-start = (bf16[2,256,256]{2,1,0:T(8,128)(2,1)S(1)}, bf16[2,256,256]{2,1,0:T(8,128)(2,1)S(1)}, u32[]{:S(2)}, u32[]{:S(2)}) collective-permute-start(bf16[2,256,256]{2,1,0:T(8,128)(2,1)S(1)} %pad_maximum_fusion), channel_id=1, source_target_pairs={{0,1},{1,2},{2,3},{3,4},{4,5},{5,6},{6,7},{7,8},{8,9},{9,10},{10,1... | collective-permute-start | bytes 786440 | tf_op jit(solution)/shard_map/ppermute | solution.py:266
  12.4 1.0 pad_maximum_fusion.1
  13.4 1.3 collective-permute-start.1
  14.7 0.8 broadcast_in_dim.72
  15.4 8.8 %all-to-all-start = ((bf16[4,3,64,256]{3,2,1,0:T(8,128)(2,1)}), bf16[4,3,64,256]{3,2,1,0:T(8,128)(2,1)S(1)}, u32[]{:S(2)}, u32[]{:S(2)}) async-start(bf16[4,3,64,256]{3,2,1,0:T(8,128)(2,1)} %broadcast_in_dim.72), calls=%async_computation | async-start | bytes 786432 | tf_op jit(solution)/shard_map/all_to_all | solution.py:278
  29.3 5.9 %all-to-all-done = bf16[4,3,64,256]{3,2,1,0:T(8,128)(2,1)S(1)} async-done(((bf16[4,3,64,256]{3,2,1,0:T(8,128)(2,1)}), bf16[4,3,64,256]{3,2,1,0:T(8,128)(2,1)S(1)}, u32[]{:S(2)}, u32[]{:S(2)}) %all-to-all-start) | async-done | bytes 393248 | tf_op jit(solution)/shard_map/all_to_all | solution.py:278
  36.0 1.3 collective-permute-start.2
  37.4 1.3 collective-permute-start.3
  38.7 2.0 collective-permute-done.2.b2
  40.6 7.8 %collective-permute-done.3.a2 = bf16[2,256,256]{2,1,0:T(8,128)(2,1)S(1)} collective-permute-done((bf16[2,256,256]{2,1,0:T(8,128)(2,1)S(1)}, bf16[2,256,256]{2,1,0:T(8,128)(2,1)S(1)}, u32[]{:S(2)}, u32[]{:S(2)}) %collective-permute-start.3) | collective-permute-done | bytes 262176 | tf_op jit(solution)/shard_map/ppermute | solution.py:266
  48.4 3.1 %collective-permute-start.4 = (bf16[2,256,256]{2,1,0:T(8,128)(2,1)S(1)}, bf16[2,256,256]{2,1,0:T(8,128)(2,1)S(1)}, u32[]{:S(2)}, u32[]{:S(2)}) collective-permute-start(bf16[2,256,256]{2,1,0:T(8,128)(2,1)S(1)} %collective-permute-done.2.b2), channel_id=1, source_target_pairs={{0,1},{1,2},{2,3},{3,4},{4,5},{5,6},{6,7},{7,8},{8,9},{9,10},{10,1... | collective-permute-start | bytes 786440 | tf_op jit(solution)/shard_map/ppermute | solution.py:266
  51.5 1.3 collective-permute-start.5
  52.8 2.0 collective-permute-done.4.b3
  54.8 4.2 %collective-permute-done.5.a3 = bf16[2,256,256]{2,1,0:T(8,128)(2,1)S(1)} collective-permute-done((bf16[2,256,256]{2,1,0:T(8,128)(2,1)S(1)}, bf16[2,256,256]{2,1,0:T(8,128)(2,1)S(1)}, u32[]{:S(2)}, u32[]{:S(2)}) %collective-permute-start.5) | collective-permute-done | bytes 262176 | tf_op jit(solution)/shard_map/ppermute | solution.py:266
  59.0 3.9 %collective-permute-start.6 = (bf16[2,256,256]{2,1,0:T(8,128)(2,1)S(1)}, bf16[2,256,256]{2,1,0:T(8,128)(2,1)S(1)}, u32[]{:S(2)}, u32[]{:S(2)}) collective-permute-start(bf16[2,256,256]{2,1,0:T(8,128)(2,1)S(1)} %collective-permute-done.4.b3), channel_id=1, source_target_pairs={{0,1},{1,2},{2,3},{3,4},{4,5},{5,6},{6,7},{7,8},{8,9},{9,10},{10,1... | collective-permute-start | bytes 786440 | tf_op jit(solution)/shard_map/ppermute | solution.py:266
  62.9 1.3 collective-permute-start.7
  64.9 15.9 %all-to-all-start.1 = ((bf16[8,26,256]{2,1,0:T(8,128)(2,1)}), bf16[8,26,256]{2,1,0:T(8,128)(2,1)S(1)}, u32[]{:S(2)}, u32[]{:S(2)}) async-start(bf16[8,26,256]{2,1,0:T(8,128)(2,1)} %broadcast_in_dim.80), calls=%async_computation.2 | async-start | bytes 262144 | tf_op jit(solution)/shard_map/all_to_all | solution.py:278
  81.6 3.8 %shard_map.225.stats = f32[8,256]{1,0:T(8,128)} custom-call(s32[8,256]{1,0:T(8,128)} %add_subtract_fusion.meta, bf16[256,256]{1,0:T(8,128)(2,1)} %q.3, bf16[256,256]{1,0:T(8,128)(2,1)} %g.3, bf16[256,256]{1,0:T(8,128)(2,1)} %k0.5, bf16[256,256]{1,0:T(8,128)(2,1)} %v0.5, bf16[2,256,256]{2,1,0:T(8,128)(2,1)} %copy-done.2, bf16[2,256,256]{2,1,0:T(8,128)(2,1)} %copy-done.3, ...), custom_call_target="tpu_custom_call" | custom-call | tf_op jit(solution)/shard_map/pallas_call | solution.py:356
  85.4 1.3 collective-permute-start.10
  86.6 1.3 collective-permute-start.11
  87.9 1.3 collective-permute-start.8
  89.2 1.3 collective-permute-start.9
  90.6 5.2 %shard_map.226 = (bf16[256,256]{1,0:T(8,128)(2,1)}, f32[256,256]{1,0:T(8,128)}, f32[256,256]{1,0:T(8,128)}) custom-call(s32[8,256]{1,0:T(8,128)} %add_subtract_fusion.meta, f32[8,256]{1,0:T(8,128)} %shard_map.225.stats, bf16[256,256]{1,0:T(8,128)(2,1)} %q.3, bf16[256,256]{1,0:T(8,128)(2,1)} %g.3, bf16[256,256]{1,0:T(8,128)(2,1)} %k0.5, bf16[256,256]{1,0:T(8,128)(2,1)} %v0.5, ...), custom_call_target="tpu_custom_call" | custom-call | tf_op jit(solution)/shard_map/pallas_call | solution.py:390
  96.4 5.1 %shard_map.227 = (bf16[3,256,256]{2,1,0:T(8,128)(2,1)}, bf16[3,64,256]{2,1,0:T(8,128)(2,1)}) custom-call(s32[1]{0:T(128)} %bitcast.7.start, s32[8,256]{1,0:T(8,128)} %add_subtract_fusion.meta, bf16[256,256]{1,0:T(8,128)(2,1)} %k0.5, bf16[256,256]{1,0:T(8,128)(2,1)} %v0.5, bf16[2,256,256]{2,1,0:T(8,128)(2,1)} %copy-done.7, bf16[2,256,256]{2,1,0:T(8,128)(2,1)} %copy-done.8, ...), custom_call_target="tpu_custom_call" | custom-call | tf_op jit(solution)/shard_map/pallas_call | solution.py:395
  101.5 4.0 %collective-permute-start.12 = (bf16[3,64,256]{2,1,0:T(8,128)(2,1)}, bf16[3,64,256]{2,1,0:T(8,128)(2,1)S(1)}, u32[]{:S(2)}, u32[]{:S(2)}) collective-permute-start(bf16[3,64,256]{2,1,0:T(8,128)(2,1)} %get-tuple-element.41.own), channel_id=1, source_target_pairs={{0,1},{1,0},{2,3},{3,2},{4,5},{5,4},{6,7},{7,6},{8,9},{9,8},{10,11... | collective-permute-start | bytes 294920 | tf_op jit(solution)/shard_map/ppermute | solution.py:270
  105.5 2.2 collective-permute-done.12.other
  107.7 3.4 %collective-permute-start.13 = (bf16[3,256,256]{2,1,0:T(8,128)(2,1)}, bf16[3,256,256]{2,1,0:T(8,128)(2,1)S(1)}, u32[]{:S(2)}, u32[]{:S(2)}) collective-permute-start(bf16[3,256,256]{2,1,0:T(8,128)(2,1)} %get-tuple-element.42.own), channel_id=1, source_target_pairs={{0,1},{1,0},{2,3},{3,2},{4,5},{5,4},{6,7},{7,6},{8,9},{9,8},{10,11... | collective-permute-start | bytes 1179656 | tf_op jit(solution)/shard_map/ppermute | solution.py:270
  111.1 0.8 broadcast_in_dim.81
  111.9 8.9 %all-to-all-start.2 = ((bf16[8,82,256]{2,1,0:T(8,128)(2,1)}), bf16[8,82,256]{2,1,0:T(8,128)(2,1)S(1)}, u32[]{:S(2)}, u32[]{:S(2)}) async-start(bf16[8,82,256]{2,1,0:T(8,128)(2,1)} %broadcast_in_dim.81), calls=%async_computation.3 | async-start | bytes 720896 | tf_op jit(solution)/shard_map/all_to_all | solution.py:278
  121.6 5.4 %shard_map.228 = bf16[8,256,512]{2,1,0:T(8,128)(2,1)} custom-call(s32[1]{0:T(128)} %bitcast.flags, bf16[8,4,3,64,256]{4,3,2,1,0:T(8,128)(2,1)} %bitcast.43, bf16[3,256,256]{2,1,0:T(8,128)(2,1)} %get-tuple-element.42.own, bf16[3,256,256]{2,1,0:T(8,128)(2,1)} %copy-done.6), custom_call_target="tpu_custom_call" | custom-call | tf_op jit(solution)/shard_map/pallas_call | solution.py:434
  129.8 3.3 %all-to-all-done.2 = bf16[8,82,256]{2,1,0:T(8,128)(2,1)S(1)} async-done(((bf16[8,82,256]{2,1,0:T(8,128)(2,1)}), bf16[8,82,256]{2,1,0:T(8,128)(2,1)S(1)}, u32[]{:S(2)}, u32[]{:S(2)}) %all-to-all-start.2) | async-done | bytes 335904 | tf_op jit(solution)/shard_map/all_to_all | solution.py:278
  133.4 31.6 %all_to_all.40.pw = bf16[8,264,256]{2,1,0:T(8,128)(2,1)} all-to-all(bf16[8,264,256]{2,1,0:T(8,128)(2,1)S(1)} %broadcast_in_dim.82), channel_id=1, replica_groups=mesh['head'=8,'z'=8,'yh'=4,'yl'=2] {'head'}, dimensions={0} | all-to-all | bytes 2162688 | tf_op jit(solution)/shard_map/all_to_all | solution.py:278
  165.1 5.0 %shard_map.229 = bf16[8,128,256]{2,1,0:T(8,128)(2,1)} custom-call(s32[1]{0:T(128)} %bitcast.flags, bf16[8,4,3,64,256]{4,3,2,1,0:T(8,128)(2,1)} %bitcast.44, bf16[3,64,256]{2,1,0:T(8,128)(2,1)} %get-tuple-element.41.own, bf16[3,64,256]{2,1,0:T(8,128)(2,1)} %copy-done.14, bf16[8,264,256]{2,1,0:T(8,128)(2,1)} %all_to_all.40.pw), custom_call_target="tpu_custom_call" | custom-call | tf_op jit(solution)/shard_map/pallas_call | solution.py:411
  170.0 4.1 %all-to-all-start.4 = ((bf16[16,64,256]{2,1,0:T(8,128)(2,1)}), bf16[16,64,256]{2,1,0:T(8,128)(2,1)S(1)}, u32[]{:S(2)}, u32[]{:S(2)}) async-start(bf16[16,64,256]{2,1,0:T(8,128)(2,1)} %bitcast.45), calls=%async_computation.5 | async-start | bytes 1048576 | tf_op jit(solution)/shard_map/all_to_all | solution.py:278
  174.1 1.2 pad_add_fusion.scalars
  176.0 1.4 slice_bitcast_fusion.1.picture
  177.4 7.5 %all-to-all-done.4.pieces = bf16[16,64,256]{2,1,0:T(8,128)(2,1)S(1)} async-done(((bf16[16,64,256]{2,1,0:T(8,128)(2,1)}), bf16[16,64,256]{2,1,0:T(8,128)(2,1)S(1)}, u32[]{:S(2)}, u32[]{:S(2)}) %all-to-all-start.4) | async-done | bytes 524320 | tf_op jit(solution)/shard_map/all_to_all | solution.py:278
  184.9 0.8 copy-done
  185.7 3.6 %shard_map.230 = bf16[64,7,128]{2,1,0:T(8,128)(2,1)} custom-call(s32[2]{0:T(128)} %pad_add_fusion.scalars, bf16[16,64,256]{2,1,0:T(8,128)(2,1)} %copy-done, bf16[9,16,256]{2,1,0:T(8,128)(2,1)} %bitcast.58, bf16[64,256]{1,0:T(8,128)(2,1)} %slice_bitcast_fusion.1.picture), custom_call_target="tpu_custom_call" | custom-call | tf_op jit(solution)/shard_map/pallas_call | solution.py:428
  189.3 25.0 %all_to_all.41 = bf16[64,7,128]{2,1,0:T(8,128)(2,1)S(1)} all-to-all(bf16[64,7,128]{2,1,0:T(8,128)(2,1)} %shard_map.230), channel_id=1, replica_groups=mesh['head'=8,'z'=8,'yh'=4,'yl'=2] {'z','yh','yl'}, dimensions={0} | all-to-all | bytes 229376 | tf_op jit(solution)/shard_map/all_to_all | solution.py:278
  215.6 15.0 %all_to_all.42 = f32[64,1,128]{2,1,0:T(1,128)S(1)} all-to-all(f32[64,1,128]{2,1,0:T(1,128)S(1)} %broadcast_in_dim_broadcast_in_dim.3), channel_id=1, replica_groups=mesh['head'=8,'z'=8,'yh'=4,'yl'=2] {'z','yh','yl'}, dimensions={0} | all-to-all | bytes 65536 | tf_op jit(solution)/shard_map/all_to_all | solution.py:278
  231.3 6.0 %all-to-all-start.7 = ((f32[8,8,128]{2,1,0:T(8,128)}), f32[8,8,128]{2,1,0:T(8,128)S(1)}, u32[]{:S(2)}, u32[]{:S(2)}) async-start(f32[8,8,128]{2,1,0:T(8,128)} %broadcast_in_dim.83), calls=%async_computation.8 | async-start | bytes 65536 | tf_op jit(solution)/shard_map/all_to_all | solution.py:278
  237.3 4.7 %all-to-all-done.7 = f32[8,8,128]{2,1,0:T(8,128)S(1)} async-done(((f32[8,8,128]{2,1,0:T(8,128)}), f32[8,8,128]{2,1,0:T(8,128)S(1)}, u32[]{:S(2)}, u32[]{:S(2)}) %all-to-all-start.7) | async-done | bytes 32800 | tf_op jit(solution)/shard_map/all_to_all | solution.py:278
  244.6 1.0 broadcast_select_fusion.2
  245.6 2.2 collective-permute-start.14
  248.5 3.3 %collective-permute-done.14 = bf16[256,256]{1,0:T(8,128)(2,1)S(1)} collective-permute-done((bf16[256,256]{1,0:T(8,128)(2,1)S(1)}, bf16[256,256]{1,0:T(8,128)(2,1)S(1)}, u32[]{:S(2)}, u32[]{:S(2)}) %collective-permute-start.14) | collective-permute-done | bytes 131104 | tf_op jit(solution)/shard_map/ppermute | solution.py:270
  251.8 1.0 broadcast_select_fusion.1
  (126 shorter events, 13.1 us)
Async XLA Ops:
  7.2 7.5 %copy-start.13 = (bf16[3,64,256]{2,1,0:T(8,128)(2,1)S(1)}, bf16[3,64,256]{2,1,0:T(8,128)(2,1)}, u32[]{:S(2)}) copy-start(bf16[3,64,256]{2,1,0:T(8,128)(2,1)} %param.22) | copy-start | bytes 294916
  7.2 17.1 %copy-start.29 = (s32[32]{0:T(128)S(1)}, s32[32]{0:T(128)}, u32[]{:S(2)}) copy-start(s32[32]{0:T(128)} %param.23) | copy-start | bytes 388
  7.2 17.3 %copy-start.26 = (s32[64]{0:T(128)S(1)}, s32[64]{0:T(128)}, u32[]{:S(2)}) copy-start(s32[64]{0:T(128)} %param.26) | copy-start | bytes 772
  7.2 17.3 %copy-start.27 = (s32[64]{0:T(128)S(1)}, s32[64]{0:T(128)}, u32[]{:S(2)}) copy-start(s32[64]{0:T(128)} %param.24) | copy-start | bytes 772
  7.2 18.0 %copy-start.28 = (s32[64]{0:T(128)S(1)}, s32[64]{0:T(128)}, u32[]{:S(2)}) copy-start(s32[64]{0:T(128)} %param.25) | copy-start | bytes 772
  8.3 21.0 %collective-permute-start = (bf16[2,256,256]{2,1,0:T(8,128)(2,1)S(1)}, bf16[2,256,256]{2,1,0:T(8,128)(2,1)S(1)}, u32[]{:S(2)}, u32[]{:S(2)}) collective-permute-start(bf16[2,256,256]{2,1,0:T(8,128)(2,1)S(1)} %pad_maximum_fusion), channel_id=1, source_target_pairs={{0,1},{1,2},{2,3},{3,4},{4,5},{5,6},{6,7},{7,8},{8,9},{9,10},{10,1... | collective-permute-start | bytes 786440 | tf_op jit(solution)/shard_map/ppermute | solution.py:266
  12.3 40.5 %copy-start.12 = (f32[18,256]{1,0:T(8,128)S(1)}, f32[18,256]{1,0:T(8,128)}, u32[]{:S(2)}) copy-start(f32[18,256]{1,0:T(8,128)} %param.31) | copy-start | bytes 55300
  12.3 51.9 %copy-start.24 = (bf16[1,1,8,128]{3,2,1,0:T(8,128)(2,1)S(1)}, bf16[1,1,8,128]{3,2,1,0:T(8,128)(2,1)}, u32[]{:S(2)}) copy-start(bf16[1,1,8,128]{3,2,1,0:T(8,128)(2,1)} %param.29) | copy-start | bytes 6148
  12.3 51.9 %copy-start.25 = (bf16[1,1,8,128]{3,2,1,0:T(8,128)(2,1)S(1)}, bf16[1,1,8,128]{3,2,1,0:T(8,128)(2,1)}, u32[]{:S(2)}) copy-start(bf16[1,1,8,128]{3,2,1,0:T(8,128)(2,1)} %param.28) | copy-start | bytes 6148
  13.4 16.0 %collective-permute-start.1 = (bf16[2,256,256]{2,1,0:T(8,128)(2,1)S(1)}, bf16[2,256,256]{2,1,0:T(8,128)(2,1)S(1)}, u32[]{:S(2)}, u32[]{:S(2)}) collective-permute-start(bf16[2,256,256]{2,1,0:T(8,128)(2,1)S(1)} %pad_maximum_fusion.1), channel_id=1, source_target_pairs={{1,0},{2,1},{3,2},{4,3},{5,4},{6,5},{7,6},{8,7},{9,8},{10,9},{11,1... | collective-permute-start | bytes 786440 | tf_op jit(solution)/shard_map/ppermute | solution.py:266
  15.4 19.8 %all-to-all-start = ((bf16[4,3,64,256]{3,2,1,0:T(8,128)(2,1)}), bf16[4,3,64,256]{3,2,1,0:T(8,128)(2,1)S(1)}, u32[]{:S(2)}, u32[]{:S(2)}) async-start(bf16[4,3,64,256]{3,2,1,0:T(8,128)(2,1)} %broadcast_in_dim.72), calls=%async_computation | async-start | bytes 786432 | tf_op jit(solution)/shard_map/all_to_all | solution.py:278
  24.2 96.6 %all-gather.3.cloned.1.call-start = ((), (), s32[]{:S(2)}) async-start(), calls=%async_computation.10 | async-start | bytes 3538944 | tf_op jit(solution)/shard_map/all_gather | solution.py:365
  29.3 51.6 %copy-start.2 = (bf16[2,256,256]{2,1,0:T(8,128)(2,1)}, bf16[2,256,256]{2,1,0:T(8,128)(2,1)S(1)}, u32[]{:S(2)}) copy-start(bf16[2,256,256]{2,1,0:T(8,128)(2,1)S(1)} %collective-permute-done.b1) | copy-start | bytes 786436
  29.3 66.5 %copy-start.7 = (bf16[2,256,256]{2,1,0:T(8,128)(2,1)}, bf16[2,256,256]{2,1,0:T(8,128)(2,1)S(1)}, u32[]{:S(2)}) copy-start(bf16[2,256,256]{2,1,0:T(8,128)(2,1)S(1)} %collective-permute-done.1.a1) | copy-start | bytes 786436
  35.3 0.8 copy-start.1
  36.0 4.6 %collective-permute-start.2 = (bf16[2,256,256]{2,1,0:T(8,128)(2,1)S(1)}, bf16[2,256,256]{2,1,0:T(8,128)(2,1)S(1)}, u32[]{:S(2)}, u32[]{:S(2)}) collective-permute-start(bf16[2,256,256]{2,1,0:T(8,128)(2,1)S(1)} %collective-permute-done.b1), channel_id=1, source_target_pairs={{0,1},{1,2},{2,3},{3,4},{4,5},{5,6},{6,7},{7,8},{8,9},{9,10},{10,1... | collective-permute-start | bytes 786440 | tf_op jit(solution)/shard_map/ppermute | solution.py:266
  37.4 11.1 %collective-permute-start.3 = (bf16[2,256,256]{2,1,0:T(8,128)(2,1)S(1)}, bf16[2,256,256]{2,1,0:T(8,128)(2,1)S(1)}, u32[]{:S(2)}, u32[]{:S(2)}) collective-permute-start(bf16[2,256,256]{2,1,0:T(8,128)(2,1)S(1)} %collective-permute-done.1.a1), channel_id=1, source_target_pairs={{1,0},{2,1},{3,2},{4,3},{5,4},{6,5},{7,6},{8,7},{9,8},{10,9},{11,1... | collective-permute-start | bytes 786440 | tf_op jit(solution)/shard_map/ppermute | solution.py:266
  40.6 40.3 %copy-start.3 = (bf16[2,256,256]{2,1,0:T(8,128)(2,1)}, bf16[2,256,256]{2,1,0:T(8,128)(2,1)S(1)}, u32[]{:S(2)}) copy-start(bf16[2,256,256]{2,1,0:T(8,128)(2,1)S(1)} %collective-permute-done.2.b2) | copy-start | bytes 786436
  48.4 47.4 %copy-start.8 = (bf16[2,256,256]{2,1,0:T(8,128)(2,1)}, bf16[2,256,256]{2,1,0:T(8,128)(2,1)S(1)}, u32[]{:S(2)}) copy-start(bf16[2,256,256]{2,1,0:T(8,128)(2,1)S(1)} %collective-permute-done.3.a2) | copy-start | bytes 786436
  48.4 6.4 %collective-permute-start.4 = (bf16[2,256,256]{2,1,0:T(8,128)(2,1)S(1)}, bf16[2,256,256]{2,1,0:T(8,128)(2,1)S(1)}, u32[]{:S(2)}, u32[]{:S(2)}) collective-permute-start(bf16[2,256,256]{2,1,0:T(8,128)(2,1)S(1)} %collective-permute-done.2.b2), channel_id=1, source_target_pairs={{0,1},{1,2},{2,3},{3,4},{4,5},{5,6},{6,7},{7,8},{8,9},{9,10},{10,1... | collective-permute-start | bytes 786440 | tf_op jit(solution)/shard_map/ppermute | solution.py:266
  51.5 7.5 %collective-permute-start.5 = (bf16[2,256,256]{2,1,0:T(8,128)(2,1)S(1)}, bf16[2,256,256]{2,1,0:T(8,128)(2,1)S(1)}, u32[]{:S(2)}, u32[]{:S(2)}) collective-permute-start(bf16[2,256,256]{2,1,0:T(8,128)(2,1)S(1)} %collective-permute-done.3.a2), channel_id=1, source_target_pairs={{1,0},{2,1},{3,2},{4,3},{5,4},{6,5},{7,6},{8,7},{9,8},{10,9},{11,1... | collective-permute-start | bytes 786440 | tf_op jit(solution)/shard_map/ppermute | solution.py:266
  54.8 26.1 %copy-start.4 = (bf16[2,256,256]{2,1,0:T(8,128)(2,1)}, bf16[2,256,256]{2,1,0:T(8,128)(2,1)S(1)}, u32[]{:S(2)}) copy-start(bf16[2,256,256]{2,1,0:T(8,128)(2,1)S(1)} %collective-permute-done.4.b3) | copy-start | bytes 786436
  59.0 36.8 %copy-start.9 = (bf16[2,256,256]{2,1,0:T(8,128)(2,1)}, bf16[2,256,256]{2,1,0:T(8,128)(2,1)S(1)}, u32[]{:S(2)}) copy-start(bf16[2,256,256]{2,1,0:T(8,128)(2,1)S(1)} %collective-permute-done.5.a3) | copy-start | bytes 786436
  59.0 21.8 %collective-permute-start.6 = (bf16[2,256,256]{2,1,0:T(8,128)(2,1)S(1)}, bf16[2,256,256]{2,1,0:T(8,128)(2,1)S(1)}, u32[]{:S(2)}, u32[]{:S(2)}) collective-permute-start(bf16[2,256,256]{2,1,0:T(8,128)(2,1)S(1)} %collective-permute-done.4.b3), channel_id=1, source_target_pairs={{0,1},{1,2},{2,3},{3,4},{4,5},{5,6},{6,7},{7,8},{8,9},{9,10},{10,1... | collective-permute-start | bytes 786440 | tf_op jit(solution)/shard_map/ppermute | solution.py:266
  62.9 17.9 %collective-permute-start.7 = (bf16[2,256,256]{2,1,0:T(8,128)(2,1)S(1)}, bf16[2,256,256]{2,1,0:T(8,128)(2,1)S(1)}, u32[]{:S(2)}, u32[]{:S(2)}) collective-permute-start(bf16[2,256,256]{2,1,0:T(8,128)(2,1)S(1)} %collective-permute-done.5.a3), channel_id=1, source_target_pairs={{1,0},{2,1},{3,2},{4,3},{5,4},{6,5},{7,6},{8,7},{9,8},{10,9},{11,1... | collective-permute-start | bytes 786440 | tf_op jit(solution)/shard_map/ppermute | solution.py:266
  64.9 25.6 %all-to-all-start.1 = ((bf16[8,26,256]{2,1,0:T(8,128)(2,1)}), bf16[8,26,256]{2,1,0:T(8,128)(2,1)S(1)}, u32[]{:S(2)}, u32[]{:S(2)}) async-start(bf16[8,26,256]{2,1,0:T(8,128)(2,1)} %broadcast_in_dim.80), calls=%async_computation.2 | async-start | bytes 262144 | tf_op jit(solution)/shard_map/all_to_all | solution.py:278
  80.9 0.7 copy-start.5
  81.6 14.2 %copy-start.10 = (bf16[2,256,256]{2,1,0:T(8,128)(2,1)}, bf16[2,256,256]{2,1,0:T(8,128)(2,1)S(1)}, u32[]{:S(2)}) copy-start(bf16[2,256,256]{2,1,0:T(8,128)(2,1)S(1)} %collective-permute-done.7.a4) | copy-start | bytes 786436
  85.4 10.4 %collective-permute-start.10 = (f32[8,256]{1,0:T(8,128)}, f32[8,256]{1,0:T(8,128)S(1)}, u32[]{:S(2)}, u32[]{:S(2)}) collective-permute-start(f32[8,256]{1,0:T(8,128)} %shard_map.225.stats), channel_id=1, source_target_pairs={{3,0},{4,1},{5,2},{6,3},{7,4},{8,5},{9,6},{10,7},{11,8},{12,9},{13... | collective-permute-start | bytes 24584 | tf_op jit(solution)/shard_map/ppermute | solution.py:266
  86.6 9.1 %collective-permute-start.11 = (f32[8,256]{1,0:T(8,128)}, f32[8,256]{1,0:T(8,128)S(1)}, u32[]{:S(2)}, u32[]{:S(2)}) collective-permute-start(f32[8,256]{1,0:T(8,128)} %shard_map.225.stats), channel_id=1, source_target_pairs={{4,0},{5,1},{6,2},{7,3},{8,4},{9,5},{10,6},{11,7},{12,8},{13,9},{1... | collective-permute-start | bytes 24584 | tf_op jit(solution)/shard_map/ppermute | solution.py:266
  87.9 7.9 %collective-permute-start.8 = (f32[8,256]{1,0:T(8,128)}, f32[8,256]{1,0:T(8,128)S(1)}, u32[]{:S(2)}, u32[]{:S(2)}) collective-permute-start(f32[8,256]{1,0:T(8,128)} %shard_map.225.stats), channel_id=1, source_target_pairs={{1,0},{2,1},{3,2},{4,3},{5,4},{6,5},{7,6},{8,7},{9,8},{10,9},{11,1... | collective-permute-start | bytes 24584 | tf_op jit(solution)/shard_map/ppermute | solution.py:266
  89.2 6.6 %collective-permute-start.9 = (f32[8,256]{1,0:T(8,128)}, f32[8,256]{1,0:T(8,128)S(1)}, u32[]{:S(2)}, u32[]{:S(2)}) collective-permute-start(f32[8,256]{1,0:T(8,128)} %shard_map.225.stats), channel_id=1, source_target_pairs={{2,0},{3,1},{4,2},{5,3},{6,4},{7,5},{8,6},{9,7},{10,8},{11,9},{12,... | collective-permute-start | bytes 24584 | tf_op jit(solution)/shard_map/ppermute | solution.py:266
  101.5 6.2 %collective-permute-start.12 = (bf16[3,64,256]{2,1,0:T(8,128)(2,1)}, bf16[3,64,256]{2,1,0:T(8,128)(2,1)S(1)}, u32[]{:S(2)}, u32[]{:S(2)}) collective-permute-start(bf16[3,64,256]{2,1,0:T(8,128)(2,1)} %get-tuple-element.41.own), channel_id=1, source_target_pairs={{0,1},{1,0},{2,3},{3,2},{4,5},{5,4},{6,7},{7,6},{8,9},{9,8},{10,11... | collective-permute-start | bytes 294920 | tf_op jit(solution)/shard_map/ppermute | solution.py:270
  107.7 19.4 %copy-start.14 = (bf16[3,64,256]{2,1,0:T(8,128)(2,1)}, bf16[3,64,256]{2,1,0:T(8,128)(2,1)S(1)}, u32[]{:S(2)}) copy-start(bf16[3,64,256]{2,1,0:T(8,128)(2,1)S(1)} %collective-permute-done.12.other) | copy-start | bytes 294916
  107.7 13.1 %collective-permute-start.13 = (bf16[3,256,256]{2,1,0:T(8,128)(2,1)}, bf16[3,256,256]{2,1,0:T(8,128)(2,1)S(1)}, u32[]{:S(2)}, u32[]{:S(2)}) collective-permute-start(bf16[3,256,256]{2,1,0:T(8,128)(2,1)} %get-tuple-element.42.own), channel_id=1, source_target_pairs={{0,1},{1,0},{2,3},{3,2},{4,5},{5,4},{6,7},{7,6},{8,9},{9,8},{10,11... | collective-permute-start | bytes 1179656 | tf_op jit(solution)/shard_map/ppermute | solution.py:270
  111.9 21.2 %all-to-all-start.2 = ((bf16[8,82,256]{2,1,0:T(8,128)(2,1)}), bf16[8,82,256]{2,1,0:T(8,128)(2,1)S(1)}, u32[]{:S(2)}, u32[]{:S(2)}) async-start(bf16[8,82,256]{2,1,0:T(8,128)(2,1)} %broadcast_in_dim.81), calls=%async_computation.3 | async-start | bytes 720896 | tf_op jit(solution)/shard_map/all_to_all | solution.py:278
  120.8 123.8 %reduce-scatter.2.cloned.1.call-start = ((), (), s32[]{:S(2)}) async-start(), calls=%async_computation.9 | async-start | bytes 2359296 | tf_op jit(solution)/shard_map/reduce_scatter | solution.py:447
  120.9 0.8 copy-start.6
  127.1 2.5 copy-start.11
  170.0 14.8 %all-to-all-start.4 = ((bf16[16,64,256]{2,1,0:T(8,128)(2,1)}), bf16[16,64,256]{2,1,0:T(8,128)(2,1)S(1)}, u32[]{:S(2)}, u32[]{:S(2)}) async-start(bf16[16,64,256]{2,1,0:T(8,128)(2,1)} %bitcast.45), calls=%async_computation.5 | async-start | bytes 1048576 | tf_op jit(solution)/shard_map/all_to_all | solution.py:278
  184.9 0.8 copy-start
  185.7 58.3 %copy-start.15 = (f32[18,256]{1,0:T(8,128)S(1)}, f32[18,256]{1,0:T(8,128)}, u32[]{:S(2)}) copy-start(f32[18,256]{1,0:T(8,128)} %param.33) | copy-start | bytes 55300
  185.7 58.3 %copy-start.16 = (f32[18,256]{1,0:T(8,128)S(1)}, f32[18,256]{1,0:T(8,128)}, u32[]{:S(2)}) copy-start(f32[18,256]{1,0:T(8,128)} %param.35) | copy-start | bytes 55300
  189.3 58.6 %copy-start.17 = (f32[18,128]{1,0:T(8,128)S(1)}, f32[18,128]{1,0:T(8,128)}, u32[]{:S(2)}) copy-start(f32[18,128]{1,0:T(8,128)} %param.30) | copy-start | bytes 27652
  189.3 58.6 %copy-start.18 = (f32[18,128]{1,0:T(8,128)S(1)}, f32[18,128]{1,0:T(8,128)}, u32[]{:S(2)}) copy-start(f32[18,128]{1,0:T(8,128)} %param.32) | copy-start | bytes 27652
  189.3 58.6 %copy-start.19 = (f32[18,128]{1,0:T(8,128)S(1)}, f32[18,128]{1,0:T(8,128)}, u32[]{:S(2)}) copy-start(f32[18,128]{1,0:T(8,128)} %param.34) | copy-start | bytes 27652
  231.3 10.7 %all-to-all-start.7 = ((f32[8,8,128]{2,1,0:T(8,128)}), f32[8,8,128]{2,1,0:T(8,128)S(1)}, u32[]{:S(2)}, u32[]{:S(2)}) async-start(f32[8,8,128]{2,1,0:T(8,128)} %broadcast_in_dim.83), calls=%async_computation.8 | async-start | bytes 65536 | tf_op jit(solution)/shard_map/all_to_all | solution.py:278
  245.6 6.2 %collective-permute-start.14 = (bf16[256,256]{1,0:T(8,128)(2,1)S(1)}, bf16[256,256]{1,0:T(8,128)(2,1)S(1)}, u32[]{:S(2)}, u32[]{:S(2)}) collective-permute-start(bf16[256,256]{1,0:T(8,128)(2,1)S(1)} %broadcast_select_fusion.2), channel_id=1, source_target_pairs={{0,1},{1,0},{2,3},{3,2},{4,5},{5,4},{6,7},{7,6},{8,9},{9,8},{10,11... | collective-permute-start | bytes 393224 | tf_op jit(solution)/shard_map/ppermute | solution.py:270
  (4 other events, 2.4 us)
Sparse Core Ops, SparseCore 0:
  36.2 63.8 all-gather.2
  127.2 57.4 reduce-scatter.1
